TPU v7x, 32 devices: a whole 2x2x4 slice. The times are simulated.
32 devices in a mesh: dp: 4 (over y, x), seq: 8 (over z, core).
Axes of the slice: x: 2, y: 2, z: 4, core: 2. Of those that a mesh axis runs over, the one named last changes fastest.
Arguments:
- layer_in: float32 [4096, 2048], P(('dp', 'seq')), may hold values from -6 to 6
- norm1_gain: float32 [2048], replicated, may hold values from 0.25 to 1.75
- qkv_weight: bfloat16 [2048, 6144], P('dp'), may hold values from -0.79549513 to 0.79549513
- out_weight: bfloat16 [2048, 2048], P('dp'), may hold values from -2 to 2
- norm2_gain: float32 [2048], replicated, may hold values from 0.25 to 1.75
- gate_up_weight: bfloat16 [2048, 16384], P('dp'), may hold values from -0.125 to 0.125
- down_weight: bfloat16 [2048, 8192], P('dp'), may hold values from -0.0625 to 0.0625
- cotangent: float32 [4096, 2048], P(('dp', 'seq')), may hold values from -6 to 6
Outputs:
- layer_out: float32 [4096, 2048], P(('dp', 'seq'))
- input_grad: float32 [4096, 2048], P(('dp', 'seq'))
- norm1_grad: float32 [2048], P(('dp', 'seq'))
- qkv_grad: float32 [2048, 6144], P(('dp', 'seq'))
- out_grad: float32 [2048, 2048], P(('dp', 'seq'))
- norm2_grad: float32 [2048], P(('dp', 'seq'))
- gate_up_grad: float32 [2048, 16384], P(('dp', 'seq'))
- down_grad: float32 [2048, 8192], P(('dp', 'seq'))
All inputs are finite; a program needn't handle non-finite values.
Results may differ from a plain program's by a relative error of at most 0.018.
Values may be sent and summed in bfloat16 or wider, within the bound.
No kernel may reach another device: no remote copies, remote signals or barrier semaphores. Data moves between devices by JAX's collectives and lax.ppermute only.
A program may use at most 384 MiB of HBM per device.

v0:
```python
import functools

import jax
import jax.numpy as jnp
from jax import lax
from jax.experimental import pallas as pl
from jax.experimental.pallas import tpu as pltpu
from jax.sharding import PartitionSpec as P


HD = 64
EPS = 1e-05
THETA = 130000.0
BF = jnp.bfloat16
F32 = jnp.float32

GRAY = (0, 1, 3, 2)


def after(values, *earlier):
    return lax.optimization_barrier((values, *earlier))[0]


def rotary_tables(length):
    half = HD // 2
    inverse = THETA ** (-(jnp.arange(half).astype(F32) * 2.0) / HD)
    angles = jnp.arange(length).astype(F32)[:, None] * inverse[None, :]
    cosine = jnp.cos(angles)
    sine = jnp.sin(angles)
    return (
        jnp.concatenate([cosine] * 4, 1),
        jnp.concatenate([-sine, sine, -sine, sine], 1),
    )


def contract_last(left, right):
    return lax.dot_general(left, right, (((1,), (1,)), ((), ())), preferred_element_type=F32)


def contract_first(left, right):
    return lax.dot_general(left, right, (((0,), (0,)), ((), ())), preferred_element_type=F32)


def half_turn(values):
    lane = lax.broadcasted_iota(jnp.int32, values.shape, 1)
    upper = (lane & (HD // 2)) != 0
    return jnp.where(
        upper, pltpu.roll(values, HD // 2, 1), pltpu.roll(values, 128 - HD // 2, 1)
    )


def head_only(values, head):
    lane = lax.broadcasted_iota(jnp.int32, values.shape, 1)
    return jnp.where(lane // HD == head, values, jnp.zeros_like(values))


def causal(block):
    key_pos = lax.broadcasted_iota(jnp.int32, (block, block), 0)
    query_pos = lax.broadcasted_iota(jnp.int32, (block, block), 1)
    return key_pos <= query_pos


def assembled(pieces, per_row, target_ref, sems):
    copies, row = [], 0
    for first in range(0, len(pieces), per_row):
        column = 0
        for piece in pieces[first : first + per_row]:
            rows, columns = piece.shape
            place = target_ref.at[pl.ds(row, rows), pl.ds(column, columns)]
            copies.append(pltpu.make_async_copy(piece, place, sems.at[len(copies)]))
            column += columns
        row += rows
    return copies


def attention_forward_kernel(block, count, per_row, xn_ref, *refs):
    pieces, refs = refs[:count], refs[count:]
    cos_ref, sin_ref, attn_ref, q_ref, k_ref, v_ref, lse_ref, weight_ref, vt_ref, sems = refs
    head = pl.program_id(0)
    length, width = q_ref.shape
    tokens = attn_ref.shape[3]
    scale = HD ** (-0.5)

    @pl.when(head == 0)
    def _():
        copies = assembled(pieces, per_row, weight_ref, sems)
        for copy in copies:
            copy.start()
        for copy in copies:
            copy.wait()

        @pl.loop(0, length // block)
        def _(i):
            at = pl.ds(pl.multiple_of(i * block, block), block)
            qkv = jnp.dot(xn_ref[at, :], weight_ref[...], preferred_element_type=F32).astype(BF)
            v_ref[at, :] = qkv[:, 2 * width :]
            for c in range(width // 128):
                for source, target, factor in ((0, q_ref, scale), (width, k_ref, 1.0)):
                    u = qkv[:, source + c * 128 : source + (c + 1) * 128].astype(F32)
                    turned = u * cos_ref[at, :] + half_turn(u) * sin_ref[at, :]
                    target[at, c * 128 : (c + 1) * 128] = turned.astype(BF) * factor

        for c in range(width // 128):
            cols = slice(c * 128, (c + 1) * 128)
            vt_ref[cols, :] = v_ref[:, cols].astype(F32).T.astype(BF)

    rows = pl.ds(pl.multiple_of(head * HD, HD), HD)
    for i in range(length // block):
        low, high = i * block, (i + 1) * block
        query = head_only(q_ref[low:high, :], head)
        near = contract_last(k_ref[low:high, :], query)
        near = jnp.where(causal(block), near, -1e30)
        top = jnp.max(near, axis=0, keepdims=True)
        if i:
            far = contract_last(k_ref[0:low, :], query)
            top = jnp.maximum(top, jnp.max(far, axis=0, keepdims=True))
        near = jnp.exp(near - top)
        total = jnp.sum(near, axis=0, keepdims=True)
        mixed = jnp.dot(vt_ref[rows, low:high], near.astype(BF), preferred_element_type=F32)
        if i:
            far = jnp.exp(far - top)
            total = total + jnp.sum(far, axis=0, keepdims=True)
            mixed = mixed + jnp.dot(
                vt_ref[rows, 0:low], far.astype(BF), preferred_element_type=F32
            )
        mixed = (mixed / total).astype(BF)
        for part in range(block // tokens):
            attn_ref[head, low // tokens + part] = mixed[:, part * tokens : (part + 1) * tokens]
        lse_ref[pl.ds(head, 1), low:high] = top + jnp.log(total)


def attention_backward_kernel(
    block, count, per_row, q_ref, k_ref, v_ref, attn_ref, grad_ref, lse_ref, cos_ref, sin_ref, *refs
):
    pieces, refs = refs[:count], refs[count:]
    out_ref, dxn_ref, weight_ref, dq_ref, dk_ref, dv_ref, delta_ref, flat_ref, sems = refs
    head = pl.program_id(0)
    length, width = q_ref.shape
    tokens = attn_ref.shape[3]
    scale = HD ** (-0.5)

    @pl.when(head == 0)
    def _():
        for copy in assembled(pieces, per_row, weight_ref, sems):
            copy.start()
        dq_ref[...] = jnp.zeros_like(dq_ref)
        dk_ref[...] = jnp.zeros_like(dk_ref)
        dv_ref[...] = jnp.zeros_like(dv_ref)
        for c in range(width // 128):
            for j in range(length // tokens):
                pair = jnp.concatenate([grad_ref[2 * c, j], grad_ref[2 * c + 1, j]], 0)
                flat_ref[j * tokens : (j + 1) * tokens, c * 128 : (c + 1) * 128] = (
                    pair.astype(F32).T.astype(BF)
                )

    for j in range(length // tokens):
        product = grad_ref[head, j].astype(F32) * attn_ref[head, j].astype(F32)
        delta_ref[:, j * tokens : (j + 1) * tokens] = jnp.sum(product, axis=0, keepdims=True)

    def piece(keys, low, high, query, grad, diagonal):
        prob = jnp.exp(contract_last(k_ref[keys, :], query) - lse_ref[pl.ds(head, 1), low:high])
        if diagonal:
            prob = jnp.where(causal(block), prob, 0.0)
        dprob = contract_last(v_ref[keys, :], grad)
        dscore = (prob * (dprob - delta_ref[:, low:high])).astype(BF)
        dv_ref[keys, :] += jnp.dot(prob.astype(BF), grad, preferred_element_type=F32)
        dk_ref[keys, :] += jnp.dot(dscore, query, preferred_element_type=F32)
        dq_ref[low:high, :] += contract_first(dscore, head_only(k_ref[keys, :], head))

    for i in range(length // block):
        low, high = i * block, (i + 1) * block
        query = head_only(q_ref[low:high, :], head)
        grad = head_only(flat_ref[low:high, :], head)
        piece(slice(low, high), low, high, query, grad, True)
        if i:
            piece(slice(0, low), low, high, query, grad, False)

    @pl.when(head == pl.num_programs(0) - 1)
    def _():
        for copy in assembled(pieces, per_row, weight_ref, sems):
            copy.wait()

        @pl.loop(0, length // block)
        def _(i):
            at = pl.ds(pl.multiple_of(i * block, block), block)
            for c in range(width // 128):
                cols = slice(c * 128, (c + 1) * 128)
                for source, target, factor in ((dq_ref, 0, scale), (dk_ref, width, 1.0)):
                    u = source[at, cols] * factor
                    turned = u * cos_ref[at, :] - half_turn(u) * sin_ref[at, :]
                    out_ref[at, target + c * 128 : target + (c + 1) * 128] = turned.astype(BF)
            out_ref[at, 2 * width : 3 * width] = dv_ref[at, :].astype(BF)
            dxn_ref[at, :] = contract_last(out_ref[at, :], weight_ref[...]).astype(BF)


def resident(shape):
    return pl.BlockSpec(shape, lambda h: tuple(0 for _ in shape))


def attention_forward(xn, pieces, per_row, cosine, sine, tokens):
    length, model_width = xn.shape
    width = sum(piece.shape[1] for piece in pieces[:per_row]) // 3
    heads = width // HD
    block = min(256, length)
    pairs = heads * length * length
    out = (heads, length // tokens, HD, tokens)
    return pl.pallas_call(
        functools.partial(attention_forward_kernel, block, len(pieces), per_row),
        grid=(heads,),
        in_specs=[resident(xn.shape)]
        + [pl.BlockSpec(memory_space=pl.ANY)] * len(pieces)
        + [resident(cosine.shape)] * 2,
        out_specs=[resident(out)] + [resident((length, width))] * 3 + [resident((8, length))],
        out_shape=[jax.ShapeDtypeStruct(out, BF)]
        + [jax.ShapeDtypeStruct((length, width), BF)] * 3
        + [jax.ShapeDtypeStruct((8, length), F32)],
        scratch_shapes=[
            pltpu.VMEM((model_width, 3 * width), BF),
            pltpu.VMEM((width, length), BF),
            pltpu.SemaphoreType.DMA((len(pieces),)),
        ],
        cost_estimate=pl.CostEstimate(
            flops=2 * pairs * HD + 6 * length * model_width * width,
            bytes_accessed=8 * length * width + 2 * model_width * (length + 3 * width),
            transcendentals=pairs // 2,
        ),
        name="attention_forward",
    )(xn, *pieces, cosine, sine)


def attention_backward(query, key, value, attn, grad, lse, cosine, sine, pieces, per_row):
    length, width = query.shape
    model_width = sum(piece.shape[0] for piece in pieces[::per_row])
    heads = width // HD
    block = min(256, length)
    pairs = heads * length * length
    flat = resident((length, width))
    return pl.pallas_call(
        functools.partial(attention_backward_kernel, block, len(pieces), per_row),
        grid=(heads,),
        in_specs=[flat, flat, flat, resident(attn.shape), resident(attn.shape)]
        + [resident((8, length))]
        + [resident(cosine.shape)] * 2
        + [pl.BlockSpec(memory_space=pl.ANY)] * len(pieces),
        out_specs=[resident((length, 3 * width)), resident((length, model_width))],
        out_shape=[
            jax.ShapeDtypeStruct((length, 3 * width), BF),
            jax.ShapeDtypeStruct((length, model_width), BF),
        ],
        scratch_shapes=[pltpu.VMEM((model_width, 3 * width), BF)]
        + [pltpu.VMEM((length, width), F32)] * 3
        + [
            pltpu.VMEM((1, length), F32),
            pltpu.VMEM((length, width), BF),
            pltpu.SemaphoreType.DMA((len(pieces),)),
        ],
        cost_estimate=pl.CostEstimate(
            flops=5 * pairs * HD + 6 * length * model_width * width,
            bytes_accessed=20 * length * width + 2 * model_width * (length + 3 * width),
            transcendentals=pairs // 2,
        ),
        name="attention_backward",
    )(query, key, value, attn, grad, lse, cosine, sine, *pieces)


def strided_heads_kernel(which_ref, *refs):
    runs, outs = refs[:-2], refs[-2:]
    parity = which_ref[0] % 2
    half = len(runs) // 2

    for odd in range(2):

        @pl.when(parity == odd)
        def _():
            cols = slice(odd * HD, (odd + 1) * HD)
            for out, first in zip(outs, (0, half)):
                for r in range(0, half, 2):
                    out[:, r * HD : (r + 2) * HD] = jnp.concatenate(
                        [runs[first + r][:, cols], runs[first + r + 1][:, cols]], 1
                    )


def strided_heads(weight, group, group_count):
    rows, columns = weight.shape
    run = group_count * HD // 128
    runs = columns // (group_count * HD)

    def spec(r):
        return pl.BlockSpec((rows, 128), lambda g, w: (0, r * run + w[0] // 2))

    half = (rows, runs // 2 * HD)
    return pl.pallas_call(
        strided_heads_kernel,
        grid_spec=pltpu.PrefetchScalarGridSpec(
            num_scalar_prefetch=1,
            grid=(1,),
            in_specs=[spec(r) for r in range(runs)],
            out_specs=[pl.BlockSpec(half, lambda g, w: (0, 0))] * 2,
        ),
        out_shape=[jax.ShapeDtypeStruct(half, weight.dtype)] * 2,
        name="strided_heads",
    )(group.reshape(1), *[weight] * runs)


def strided_rows_kernel(which_ref, in_ref, weight_ref, out_ref, sum_ref):
    groups, rows, width = in_ref.shape
    total = jnp.zeros((rows, 128), F32)
    for b in range(width // HD):
        cols = slice(b * HD, (b + 1) * HD)
        for pair in range(groups // 2):
            both = jnp.concatenate(
                [in_ref[2 * pair, :, cols], in_ref[2 * pair + 1, :, cols]], 1
            ).astype(F32)
            at = (b * groups + 2 * pair) * HD
            out_ref[:, at : at + 128] = both
            total = total + both * weight_ref[:, at : at + 128].astype(F32)
    sum_ref[...] = jnp.broadcast_to(jnp.sum(total, axis=1, keepdims=True), sum_ref.shape)


def strided_rows(parts, weight, group):
    _, rows, _ = parts.shape
    return pl.pallas_call(
        strided_rows_kernel,
        grid_spec=pltpu.PrefetchScalarGridSpec(
            num_scalar_prefetch=1,
            grid=(1,),
            in_specs=[
                pl.BlockSpec(parts.shape, lambda g, w: (0, 0, 0)),
                pl.BlockSpec((rows, weight.shape[1]), lambda g, w: (w[0], 0)),
            ],
            out_specs=[
                pl.BlockSpec((rows, weight.shape[1]), lambda g, w: (0, 0)),
                pl.BlockSpec((rows, 128), lambda g, w: (0, 0)),
            ],
        ),
        out_shape=[
            jax.ShapeDtypeStruct((rows, weight.shape[1]), F32),
            jax.ShapeDtypeStruct((rows, 128), F32),
        ],
        name="strided_rows",
    )(group.reshape(1), parts, weight)


def side_rows_kernel(runs, which_ref, *refs):
    parts, (weight_ref, out_ref, sum_ref) = refs[:runs], refs[runs:]
    groups, rows, piece = parts[0].shape

    @pl.when(pl.program_id(0) == 0)
    def _():
        sum_ref[...] = jnp.zeros_like(sum_ref)

    for run in range(runs):

        @pl.when(pl.program_id(0) == run)
        def _():
            total = jnp.zeros((rows, 128), F32)
            for s in range(groups):
                values = parts[run][s].astype(F32)
                cols = slice(s * piece, (s + 1) * piece)
                out_ref[:, cols] = values
                product = values * weight_ref[:, cols].astype(F32)
                for c in range(piece // 128):
                    total = total + product[:, c * 128 : (c + 1) * 128]
            sum_ref[...] += jnp.broadcast_to(jnp.sum(total, axis=1, keepdims=True), sum_ref.shape)


def side_rows(parts, weight, group):
    groups, rows, piece = parts[0].shape
    runs = len(parts)
    return pl.pallas_call(
        functools.partial(side_rows_kernel, runs),
        grid_spec=pltpu.PrefetchScalarGridSpec(
            num_scalar_prefetch=1,
            grid=(runs,),
            in_specs=[pl.BlockSpec((groups, rows, piece), lambda c, w: (0, 0, 0))] * runs
            + [pl.BlockSpec((rows, groups * piece), lambda c, w: (w[0], c))],
            out_specs=[
                pl.BlockSpec((rows, groups * piece), lambda c, w: (0, c)),
                pl.BlockSpec((rows, 128), lambda c, w: (0, 0)),
            ],
        ),
        out_shape=[
            jax.ShapeDtypeStruct((rows, runs * groups * piece), F32),
            jax.ShapeDtypeStruct((rows, 128), F32),
        ],
        name="side_rows",
    )(group.reshape(1), *parts, weight)


def at_block(ref, index):
    width = ref.shape[1] // BLOCKS
    return ref.at[:, pl.ds(pl.multiple_of(index * width, width), width)]


BLOCKS = 4


def norm_in_kernel(orders_ref, x_ref, gain_ref, grad_ref, xn_ref, dy_ref):
    x = x_ref[...]
    inv = lax.rsqrt(jnp.mean(x * x, axis=1, keepdims=True) + EPS)
    for p in range(BLOCKS):
        block = orders_ref[p]
        normed = at_block(x_ref, block)[...] * inv * at_block(gain_ref, block)[...]
        at_block(xn_ref, p)[...] = normed.astype(BF)
        at_block(dy_ref, p)[...] = at_block(grad_ref, block)[...].astype(BF)


def norm_mid_kernel(orders_ref, x_ref, own_ref, *refs):
    others, (gain_ref, mid_ref, xn_ref) = refs[:-3], refs[-3:]
    mid = x_ref[...] + own_ref[...]
    for other in others:
        mid = mid + other[...].astype(F32)
    mid_ref[...] = mid
    inv = lax.rsqrt(jnp.mean(mid * mid, axis=1, keepdims=True) + EPS)
    for p in range(BLOCKS):
        block = orders_ref[p]
        normed = at_block(mid_ref, block)[...] * inv * at_block(gain_ref, block)[...]
        at_block(xn_ref, p)[...] = normed.astype(BF)


def norm_grad_kernel(places_ref, x_ref, base_ref, grad_ref, gain_ref, out_ref, *low_ref):
    x = x_ref[...]
    inv = lax.rsqrt(jnp.mean(x * x, axis=1, keepdims=True) + EPS)
    grad = jnp.concatenate(
        [at_block(grad_ref, places_ref[j])[...] for j in range(BLOCKS)], 1
    ).astype(F32)
    normed = x * inv
    grad_hat = grad * gain_ref[...]
    mean = jnp.mean(grad_hat * normed, axis=1, keepdims=True)
    out = base_ref[...] + inv * (grad_hat - normed * mean)
    out_ref[...] = out
    for ref in low_ref:
        ref[...] = out.astype(BF)


def add_placed_kernel(places_ref, base_ref, part_ref, out_ref):
    for j in range(BLOCKS):
        part = at_block(part_ref, places_ref[j])[...].astype(F32)
        at_block(out_ref, j)[...] = at_block(base_ref, j)[...] + part


def on_rows(kernel, table, inputs, out_types):
    rows, width = inputs[0].shape
    block = rows

    def spec(shape):
        if shape[0] == 1:
            return pl.BlockSpec(shape, lambda i, t: (0, 0))
        return pl.BlockSpec((block, width), lambda i, t: (i, 0))

    return pl.pallas_call(
        kernel,
        grid_spec=pltpu.PrefetchScalarGridSpec(
            num_scalar_prefetch=1,
            grid=(rows // block,),
            in_specs=[spec(v.shape) for v in inputs],
            out_specs=[spec((rows, width)) for _ in out_types],
        ),
        out_shape=[jax.ShapeDtypeStruct((rows, width), t) for t in out_types],
    )(table, *inputs)


def placed(pieces, column, columns, target_ref, at_column, sems, copies):
    row = 0
    for piece in pieces:
        rows = piece.shape[0]
        source = piece.at[:, pl.ds(column, columns)]
        place = target_ref.at[pl.ds(row, rows), pl.ds(at_column, columns)]
        copies.append(pltpu.make_async_copy(source, place, sems.at[len(copies)]))
        row += rows


def feed_kernel(count_a, count_b, xn_ref, dy_ref, *refs):
    part_a, part_b, refs = refs[:count_a], refs[count_a : count_a + count_b], refs[count_a + count_b :]
    act_ref, grad_ref, dxn_ref, gate_up_ref, down_ref, sems = refs
    cut = part_a[0].shape[1]
    hidden = act_ref.shape[1]
    split = 2 * hidden - cut

    @pl.when(pl.program_id(0) == 0)
    def _():
        copies = []
        placed(part_a, 0, cut, gate_up_ref, 0, sems, copies)
        placed(part_b, 0, split, gate_up_ref, cut, sems, copies)
        placed(part_b, split, hidden, down_ref, 0, sems, copies)
        for copy in copies:
            copy.start()
        for copy in copies:
            copy.wait()

    gate_up = jnp.dot(xn_ref[...], gate_up_ref[...], preferred_element_type=F32)
    gate, up_part = gate_up[:, :hidden], gate_up[:, hidden:]
    sigmoid_gate = jax.nn.sigmoid(gate)
    gated = gate * sigmoid_gate
    act_ref[...] = (gated * up_part).astype(BF)
    grad_act = jnp.dot(dy_ref[...], down_ref[...], preferred_element_type=F32)
    grad_gate = grad_act * up_part * sigmoid_gate * (1.0 + gate * (1.0 - sigmoid_gate))
    grad_ref[:, :hidden] = grad_gate.astype(BF)
    grad_ref[:, hidden:] = (grad_act * gated).astype(BF)
    dxn_ref[...] = contract_last(grad_ref[...], gate_up_ref[...]).astype(BF)


OVER_X_FIRST = ((1, 2), (3,), (0,))
OVER_Y_FIRST = ((2, 3), (1,), (0,))
ONE_EACH = ((0,), (1,), (2,), (3,))


def outer_kernel(layouts, left_ref, right_ref, *out_refs):
    step = pl.program_id(0)
    turned = left_ref[...].T
    column = 0
    refs = iter(out_refs)
    for layout in layouts:
        targets = [next(refs) for _ in layout]
        width = targets[0].shape[1]
        right = right_ref[:, column : column + width]
        block = jnp.dot(turned, right, preferred_element_type=F32).astype(BF)
        column += width
        for target, held in zip(targets, layout):

            @pl.when((step >= held[0]) & (step <= held[-1]))
            def _():
                target[...] = block


def outer_blocks(left, right, layouts):
    tokens, rows = left.shape
    width = right.shape[1] // len(layouts)
    block = rows // 4
    held = [blocks for layout in layouts for blocks in layout]

    def spec(blocks):
        return pl.BlockSpec(
            (block, width), lambda p: (jnp.clip(p - blocks[0], 0, len(blocks) - 1), 0)
        )

    outs = pl.pallas_call(
        functools.partial(outer_kernel, layouts),
        grid=(4,),
        in_specs=[
            pl.BlockSpec((tokens, block), lambda p: (0, p)),
            pl.BlockSpec(right.shape, lambda p: (0, 0)),
        ],
        out_specs=[spec(blocks) for blocks in held],
        out_shape=[jax.ShapeDtypeStruct((len(blocks) * block, width), BF) for blocks in held],
        cost_estimate=pl.CostEstimate(
            flops=2 * tokens * rows * right.shape[1],
            bytes_accessed=2 * (tokens * (rows + right.shape[1]) + rows * right.shape[1]),
            transcendentals=0,
        ),
        name="outer_blocks",
    )(left, right)
    outs = iter(outs)
    return [[next(outs) for _ in layout] for layout in layouts]


def in_order(parts):
    return [piece for k in GRAY for piece in parts[k]]


def feed_forward(xn, dy, part_a, part_b, hidden):
    tokens, model_width = xn.shape
    block = min(256, tokens)
    part_a, part_b = in_order(part_a), in_order(part_b)

    def blocks(columns):
        return pl.BlockSpec((block, columns), lambda i: (i, 0))

    return pl.pallas_call(
        functools.partial(feed_kernel, len(part_a), len(part_b)),
        grid=(tokens // block,),
        in_specs=[blocks(model_width)] * 2
        + [pl.BlockSpec(memory_space=pl.ANY)] * (len(part_a) + len(part_b)),
        out_specs=[blocks(hidden), blocks(2 * hidden), blocks(model_width)],
        out_shape=[
            jax.ShapeDtypeStruct((tokens, columns), BF)
            for columns in (hidden, 2 * hidden, model_width)
        ],
        scratch_shapes=[
            pltpu.VMEM((model_width, 2 * hidden), BF),
            pltpu.VMEM((model_width, hidden), BF),
            pltpu.SemaphoreType.DMA((len(part_a) + 2 * len(part_b),)),
        ],
        cost_estimate=pl.CostEstimate(
            flops=10 * tokens * model_width * hidden,
            bytes_accessed=2 * (4 * tokens * model_width + 3 * model_width * hidden),
            transcendentals=tokens * hidden,
        ),
        name="feed_forward",
    )(xn, dy, *part_a, *part_b)


def feed_out_kernel(count, act_ref, *refs):
    pieces, (out_ref, down_ref, sems) = refs[:count], refs[count:]
    hidden = act_ref.shape[1]

    @pl.when(pl.program_id(0) == 0)
    def _():
        copies = []
        placed(pieces, pieces[0].shape[1] - hidden, hidden, down_ref, 0, sems, copies)
        for copy in copies:
            copy.start()
        for copy in copies:
            copy.wait()

    out_ref[...] = contract_last(act_ref[...], down_ref[...]).astype(BF)


def feed_out(act, part_b, model_width):
    tokens, hidden = act.shape
    block = min(256, tokens)
    pieces = in_order(part_b)
    return pl.pallas_call(
        functools.partial(feed_out_kernel, len(pieces)),
        grid=(tokens // block,),
        in_specs=[pl.BlockSpec((block, hidden), lambda i: (i, 0))]
        + [pl.BlockSpec(memory_space=pl.ANY)] * len(pieces),
        out_specs=pl.BlockSpec((block, model_width), lambda i: (i, 0)),
        out_shape=jax.ShapeDtypeStruct((tokens, model_width), BF),
        scratch_shapes=[
            pltpu.VMEM((model_width, hidden), BF), pltpu.SemaphoreType.DMA((len(pieces),))
        ],
        cost_estimate=pl.CostEstimate(
            flops=2 * tokens * model_width * hidden,
            bytes_accessed=2 * (tokens + model_width) * hidden + 2 * tokens * model_width,
            transcendentals=0,
        ),
        name="feed_out",
    )(act, *pieces)


def partner(array, bits):
    return lax.ppermute(array, "dp", [(i, i ^ bits) for i in range(4)])


class Quad:
    def __init__(self, index):
        self.index = index

    def gather_direct(self, block):
        return [block] + [partner(block, k) for k in (1, 2, 3)]

    def gather(self, first, second):
        a = {0: [first], 1: [partner(first, 1)]}
        b = {0: [second], 2: [partner(second, 2)]}
        a[2], b[1] = [partner(first, 2)], [partner(second, 1)]
        a[3], b[3] = [partner(a[1][0], 2)], [partner(b[2][0], 1)]
        return a, b

    def gather_late(self, first, second, first_high, second_high):
        rows = first_high.shape[0]
        a = {0: [first], 1: [partner(first, 1)]}
        b = {0: [second], 2: [partner(second, 2)]}
        a[2], b[1] = [partner(first_high, 2)], [partner(second_high, 1)]

        def late(*earlier):
            first_low, second_low, near_a, near_b = (
                after(v, *earlier) for v in (first[rows:], second[rows:], a[1][0], b[2][0])
            )
            a[2].append(partner(first_low, 2))
            b[1].append(partner(second_low, 1))
            a[3], b[3] = [partner(near_a, 2)], [partner(near_b, 1)]
            return a, b

        return late


def add(*terms):
    total = terms[0].astype(F32)
    for term in terms[1:]:
        total = total + term.astype(F32)
    return total.astype(BF)


class PairSum:
    def __init__(self, first, second):
        (send_a, *self.keep_a), (send_b, *self.keep_b) = first, second
        self.sent_a = partner(send_a, 1)
        self.sent_b = partner(send_b, 2)

    def second(self):
        rows = self.keep_a[0].shape[0]
        send_a = add(self.keep_a[0], self.sent_a[rows:])
        send_b = add(self.keep_b[0], self.sent_b[:rows])
        self.far_a = partner(send_a, 2)
        self.far_b = partner(send_b, 1)

    def total(self):
        rows = self.keep_a[0].shape[0]
        return jnp.concatenate(
            [
                add(self.keep_a[1], self.sent_a[:rows], self.far_a),
                add(self.keep_b[1], self.sent_b[rows:], self.far_b),
            ],
            1,
        )


def sum_direct(blocks):
    others = [partner(blocks[p], GRAY[p]) for p in (1, 2, 3)]
    return add(blocks[0], *others)


def reduce_plain(left, right):
    return lax.psum_scatter(
        contract_first(left, right).astype(BF), "dp", scatter_dimension=0, tiled=True
    )


def over_seq(values):
    return lax.all_gather(values, "seq", axis=0, tiled=True)


def sum_over_seq(values):
    return lax.psum_scatter(values.astype(BF), "seq", scatter_dimension=0, tiled=True)


def exchange(values, axes):
    return lax.all_to_all(values, axes, split_axis=0, concat_axis=0, tiled=True)


def exchange_rows(values, group_count):
    return exchange(
        values.reshape(group_count, values.shape[0] // group_count, values.shape[1]), "seq"
    )


def feed_forward_plain(xn, dy, gate_up_full, down_full, hidden):
    gate_up = jnp.dot(xn, gate_up_full, preferred_element_type=F32)
    gate, up_part = gate_up[:, :hidden], gate_up[:, hidden:]
    sigmoid_gate = jax.nn.sigmoid(gate)
    act = (gate * sigmoid_gate * up_part).astype(BF)
    grad_act = jnp.dot(dy, down_full, preferred_element_type=F32)
    grad_gate = grad_act * up_part * sigmoid_gate * (1.0 + gate * (1.0 - sigmoid_gate))
    grad_up = grad_act * gate * sigmoid_gate
    grad_gate_up = jnp.concatenate([grad_gate, grad_up], 1).astype(BF)
    return act, grad_gate_up, contract_last(grad_gate_up, gate_up_full).astype(BF)


def shards(
    layer_in, norm1_gain, qkv_weight, out_weight, norm2_gain, gate_up_weight, down_weight, cotangent
):
    token_rows, model_width = layer_in.shape
    group_count = lax.axis_size("seq")
    dp_count = lax.axis_size("dp")
    group = lax.axis_index("seq")
    member = lax.axis_index("dp")
    length = token_rows * group_count
    dp_rows = model_width // dp_count
    shard_rows = dp_rows // group_count
    hidden_units = down_weight.shape[1]
    hidden = hidden_units // group_count
    width = model_width // group_count
    quad = Quad(member) if dp_count == 4 else None
    strided = quad is not None and shard_rows == HD

    blocks_at = jnp.arange(4, dtype=jnp.int32)
    if quad:
        orders = (blocks_at ^ (blocks_at >> 1)) ^ member
        places = blocks_at ^ member
        places = places ^ (places >> 1)
    else:
        orders, places = blocks_at, blocks_at
    gain1, gain2 = norm1_gain[None, :], norm2_gain[None, :]

    xn1_own, dy_own = on_rows(norm_in_kernel, orders, (layer_in, gain1, cotangent), (BF, BF))
    xn1 = over_seq(xn1_own)

    if strided:
        left, right = strided_heads(qkv_weight, group, group_count)
    else:
        qkv_piece = jnp.concatenate(
            [
                lax.dynamic_slice_in_dim(qkv_weight, part * model_width + group * width, width, 1)
                for part in range(3)
            ],
            1,
        )
    gate_piece = lax.dynamic_slice_in_dim(gate_up_weight, group * hidden, hidden, 1)
    up_piece = lax.dynamic_slice_in_dim(gate_up_weight, hidden_units + group * hidden, hidden, 1)
    down_piece = lax.dynamic_slice_in_dim(down_weight, group * hidden, hidden, 1)
    if quad:
        if not strided:
            cut = qkv_piece.shape[1] // 2
            left, right = qkv_piece[:, :cut], qkv_piece[:, cut:]
        left, right = quad.gather(left, right)
        blocks = (left[3][0], right[3][0])
        qkv_pieces = [part[k][0] for k in GRAY for part in (left, right)]
        per_row = 2
        half = hidden // 2
        part_a = after(jnp.concatenate([gate_piece, up_piece[:, :half]], 1), *blocks)
        part_b = after(jnp.concatenate([up_piece[:, half:], down_piece], 1), *blocks)
        high_a, high_b = part_a[: dp_rows // 2], part_b[: dp_rows // 2]
        xn1, high_a, high_b = lax.optimization_barrier((xn1, high_a, high_b))
        rest_of_weights = quad.gather_late(part_a, part_b, high_a, high_b)
    else:
        qkv_pieces, per_row = [lax.all_gather(qkv_piece, "dp", axis=0, tiled=True)], 1
        gate_up_full = lax.all_gather(
            jnp.concatenate([gate_piece, up_piece], 1), "dp", axis=0, tiled=True
        )
        down_full = lax.all_gather(down_piece, "dp", axis=0, tiled=True)

    cosine, sine = rotary_tables(length)
    attn, query, key, value, lse = attention_forward(
        xn1, qkv_pieces, per_row, cosine, sine, token_rows
    )

    dy = over_seq(after(dy_own, attn))

    def to_features(by_head):
        if strided:
            moved = exchange(by_head.reshape(-1, HD, token_rows), ("dp", "seq"))
        else:
            by_tokens = by_head.transpose(1, 0, 2, 3).reshape(group_count, width, token_rows)
            moved = exchange(exchange(by_tokens, "seq").reshape(dp_count, dp_rows, token_rows), "dp")
        return moved.reshape(dp_count, dp_rows, token_rows)

    def to_heads(features):
        if strided:
            moved = exchange(features.reshape(-1, HD, token_rows), ("dp", "seq"))
            return moved.reshape(-1, group_count, HD, token_rows)
        moved = exchange(features, "dp").reshape(group_count, width, token_rows)
        moved = exchange(moved, "seq").reshape(group_count, width // HD, HD, token_rows)
        return moved.transpose(1, 0, 2, 3)

    features = to_features(attn)
    if quad:
        features = jnp.stack(
            [lax.dynamic_index_in_dim(features, member ^ k, 0, False) for k in range(4)]
        )
        parts = [contract_first(features[k], out_weight) for k in range(4)]
        others = [partner(parts[k].astype(BF), k) for k in (1, 2, 3)]
        partials = (parts[0], *others)
    else:
        partials = (
            lax.psum_scatter(
                jnp.einsum("dft,fn->dtn", features, out_weight, preferred_element_type=F32)
                .astype(BF)
                .reshape(dp_count * token_rows, model_width),
                "dp", scatter_dimension=0, tiled=True,
            ).astype(F32),
        )

    hidden_res, xn2_own = on_rows(norm_mid_kernel, orders, (layer_in, *partials, gain2), (F32, BF))
    xn2 = over_seq(xn2_own)
    if quad:
        part_a, part_b = rest_of_weights(*partials)
        act, grad_gate_up, partial_xn2 = feed_forward(xn2, dy, part_a, part_b, hidden)
        feed_sum = feed_out(after(act, partial_xn2), part_b, model_width)
    else:
        act, grad_gate_up, partial_xn2 = feed_forward_plain(
            xn2, dy, gate_up_full, down_full, hidden
        )
        feed_sum = contract_last(act, down_full).astype(BF)
    raw_xn2 = sum_over_seq(partial_xn2)
    feed_sum = after(feed_sum, raw_xn2)
    grad_hidden, hidden_low = on_rows(
        norm_grad_kernel, places, (hidden_res, cotangent, raw_xn2, gain2), (F32, BF)
    )
    feed_sum = sum_over_seq(feed_sum)
    if quad:
        halves = outer_blocks(dy, act, (OVER_X_FIRST, OVER_Y_FIRST))
        down_sum = PairSum(*halves)
        halves = outer_blocks(xn2, grad_gate_up, (OVER_X_FIRST, OVER_Y_FIRST) * 2)
        gate_sum, up_sum = PairSum(*halves[:2]), PairSum(*halves[2:])
        rows_low = quad.gather_direct(hidden_low)
        rows_low = jnp.stack(rows_low)
    else:
        down_rows = reduce_plain(dy, act)
        gate_rows = reduce_plain(xn2, grad_gate_up[:, :hidden])
        up_rows = reduce_plain(xn2, grad_gate_up[:, hidden:])
        rows_low = lax.all_gather(hidden_low, "dp", axis=0)

    grad_features = jnp.einsum(
        "fn,ktn->kft", out_weight, rows_low, preferred_element_type=F32
    ).astype(BF)
    if quad:
        grad_features = jnp.stack(
            [lax.dynamic_index_in_dim(grad_features, member ^ j, 0, False) for j in range(4)]
        )
    grad_attn = to_heads(grad_features)
    if quad:
        down_sum.second()
        gate_sum.second()
        up_sum.second()
    out_rows = jnp.einsum("kft,ktn->fn", features, rows_low, preferred_element_type=F32)
    out_rows = out_rows.astype(BF)
    out_grad = sum_over_seq(out_rows).astype(F32)
    grad_qkv, partial_xn1 = attention_backward(
        query, key, value, attn, grad_attn, lse, cosine, sine, qkv_pieces, per_row
    )
    raw_xn1 = sum_over_seq(partial_xn1)
    (input_grad,) = on_rows(
        norm_grad_kernel, places, (layer_in, grad_hidden, raw_xn1, gain1), (F32,)
    )
    (layer_out,) = on_rows(
        add_placed_kernel, places, (hidden_res, after(feed_sum, partial_xn1)), (F32,)
    )

    if quad:
        (blocks,) = outer_blocks(xn1, grad_qkv, (ONE_EACH,))
        qkv_rows = sum_direct(blocks)
        down_rows, gate_rows, up_rows = down_sum.total(), gate_sum.total(), up_sum.total()
    else:
        qkv_rows = reduce_plain(xn1, grad_qkv)
    down_parts = exchange_rows(down_rows, group_count)
    gate_parts = exchange_rows(gate_rows, group_count)
    up_parts = exchange_rows(up_rows, group_count)
    qkv_parts = exchange_rows(qkv_rows, group_count)
    down_grad, _ = side_rows([down_parts], down_weight, group)
    gate_up_grad, gain2_sum = side_rows([gate_parts, up_parts], gate_up_weight, group)
    if strided:
        qkv_grad, gain1_sum = strided_rows(qkv_parts, qkv_weight, group)
    else:
        thirds = [qkv_parts[:, :, i * width : (i + 1) * width] for i in range(3)]
        qkv_grad, gain1_sum = side_rows(thirds, qkv_weight, group)

    def gain_grad(sums, gain):
        own = lax.dynamic_slice_in_dim(gain, member * dp_rows + group * shard_rows, shard_rows, 0)
        return sums[:, 0] / own

    return (
        layer_out,
        input_grad,
        gain_grad(gain1_sum, norm1_gain),
        qkv_grad,
        out_grad,
        gain_grad(gain2_sum, norm2_gain),
        gate_up_grad,
        down_grad,
    )


def solution(mesh):
    rows = P(("dp", "seq"), None)
    in_specs = (
        rows, P(), P("dp", None), P("dp", None), P(), P("dp", None), P("dp", None), rows,
    )
    vector = P(("dp", "seq"))
    out_specs = (rows, rows, vector, rows, rows, vector, rows, rows)
    return jax.shard_map(shards, mesh=mesh, in_specs=in_specs, out_specs=out_specs, check_vma=False)
```

profile of v0, /device:TPU:0, one launch (start us, length us, event | category | flops | bytes accessed | tf_op | source)
XLA Modules:
  0.0 641.8 jit_solution(6037736676504243415)
XLA Ops:
  7.8 3.5 shard_map.143
  11.4 2.7 strided_heads.1
  14.1 3.0 collective-permute-start.2
  17.1 1.5 collective-permute-start.4
  23.2 1.9 fusion.12
  25.1 11.2 %collective-permute-done.refs_2_ = bf16[512,384]{1,0:T(8,128)(2,1)S(1)} collective-permute-done((bf16[512,384]{1,0:T(8,128)(2,1)}, bf16[512,384]{1,0:T(8,128)(2,1)S(1)}, u32[]{:S(2)}, u32[]{:S(2)}) %collective-permute-start) | collective-permute-done | bytes 393248 | tf_op jit(solution)/shard_map/ppermute | solution.py:633
  36.6 1.7 collective-permute-start.3
  38.3 1.9 pad_maximum_fusion.6
  40.5 5.6 collective-permute-done.1.refs_4_
  48.7 12.4 %all-gather.4.cloned.1.call-done.xn_ref.left_ref = bf16[1024,2048]{1,0:T(8,128)(2,1)} async-done(((bf16[128,2048]{1,0:T(8,128)(2,1)}), bf16[1024,2048]{1,0:T(8,128)(2,1)}) %all-gather.4.cloned.1.call-update) | async-done | bytes 4194320 | tf_op jit(solution)/shard_map/all_gather | solution.py:711
  61.1 16.0 %attention_forward.1 = (bf16[4,8,64,128]{3,2,1,0:T(8,128)(2,1)}, bf16[1024,256]{1,0:T(8,128)(2,1)}, bf16[1024,256]{1,0:T(8,128)(2,1)}, bf16[1024,256]{1,0:T(8,128)(2,1)}, f32[8,1024]{1,0:T(8,128)}) custom-call(bf16[1024,2048]{1,0:T(8,128)(2,1)} %all-gather.4.cloned.1.call-done.xn_ref.left_ref, bf16[512,384]{1,0:T(8,128)(2,1)} %get-tuple-element.67.refs_0_, ...), custom_call_target="tpu_custom_call" | custom-call | flops 3758096384 | bytes 9437184 | tf_op jit(solution)/shard_map/attention_forward/pallas_call | solution.py:207
  77.1 3.4 all-to-all-start
  80.6 25.0 %all-to-all-done = bf16[32,64,128]{2,1,0:T(8,128)(2,1)S(1)} async-done(((bf16[32,64,128]{2,1,0:T(8,128)(2,1)}), bf16[32,64,128]{2,1,0:T(8,128)(2,1)S(1)}, u32[]{:S(2)}, u32[]{:S(2)}) %all-to-all-start) | async-done | bytes 524320 | tf_op jit(solution)/shard_map/all_to_all | solution.py:719
  108.3 2.4 collective-permute-start.8
  112.2 7.7 %collective-permute-done.6.refs_0_ = bf16[128,2048]{1,0:T(8,128)(2,1)S(1)} collective-permute-done((bf16[128,2048]{1,0:T(8,128)(2,1)S(1)}, bf16[128,2048]{1,0:T(8,128)(2,1)S(1)}, u32[]{:S(2)}, u32[]{:S(2)}) %collective-permute-start.6) | collective-permute-done | bytes 524320 | tf_op jit(solution)/shard_map/ppermute | solution.py:633
  120.0 10.4 %collective-permute-done.8.refs_2_ = bf16[128,2048]{1,0:T(8,128)(2,1)} collective-permute-done((bf16[128,2048]{1,0:T(8,128)(2,1)S(1)}, bf16[128,2048]{1,0:T(8,128)(2,1)}, u32[]{:S(2)}, u32[]{:S(2)}) %collective-permute-start.8) | collective-permute-done | bytes 524320 | tf_op jit(solution)/shard_map/ppermute | solution.py:633
  130.4 4.2 shard_map.144
  134.8 2.6 collective-permute-start.15
  138.7 1.9 collective-permute-start.11
  140.7 31.8 %collective-permute-done.15.refs_9_.refs_4_ = bf16[512,1536]{1,0:T(8,128)(2,1)S(1)} collective-permute-done((bf16[512,1536]{1,0:T(8,128)(2,1)}, bf16[512,1536]{1,0:T(8,128)(2,1)S(1)}, u32[]{:S(2)}, u32[]{:S(2)}) %collective-permute-start.15) | collective-permute-done | bytes 1572896 | tf_op jit(solution)/shard_map/ppermute | solution.py:633
  172.5 3.7 collective-permute-start.16
  178.2 11.1 %collective-permute-done.11.refs_3_ = bf16[256,1536]{1,0:T(8,128)(2,1)S(1)} collective-permute-done((bf16[256,1536]{1,0:T(8,128)(2,1)}, bf16[256,1536]{1,0:T(8,128)(2,1)S(1)}, u32[]{:S(2)}, u32[]{:S(2)}) %collective-permute-start.11) | collective-permute-done | bytes 786464 | tf_op jit(solution)/shard_map/ppermute | solution.py:633
  189.3 2.4 collective-permute-start.12
  191.7 36.5 %collective-permute-done.13.refs_6_.refs_1_ = bf16[256,1536]{1,0:T(8,128)(2,1)S(1)} collective-permute-done((bf16[256,1536]{1,0:T(8,128)(2,1)}, bf16[256,1536]{1,0:T(8,128)(2,1)S(1)}, u32[]{:S(2)}, u32[]{:S(2)}) %collective-permute-start.13) | collective-permute-done | bytes 786464 | tf_op jit(solution)/shard_map/ppermute | solution.py:633
  228.2 15.7 %collective-permute-done.14.refs_7_.refs_2_ = bf16[256,1536]{1,0:T(8,128)(2,1)S(1)} collective-permute-done((bf16[256,1536]{1,0:T(8,128)(2,1)}, bf16[256,1536]{1,0:T(8,128)(2,1)S(1)}, u32[]{:S(2)}, u32[]{:S(2)}) %collective-permute-start.14) | collective-permute-done | bytes 786464 | tf_op jit(solution)/shard_map/ppermute | solution.py:633
  246.3 31.1 %feed_forward.1 = (bf16[1024,1024]{1,0:T(8,128)(2,1)}, bf16[1024,2048]{1,0:T(8,128)(2,1)}, bf16[1024,2048]{1,0:T(8,128)(2,1)}) custom-call(bf16[1024,2048]{1,0:T(8,128)(2,1)} %all-gather.6.cloned.1.call-done.xn_ref.left_ref, bf16[1024,2048]{1,0:T(8,128)(2,1)} %all-gather.8.cloned.1.call-done.dy_ref.left_ref, bf16[512,1536]{1,0:T(8,128)(2,1)} %copy-done.2, ...), custom_call_target="tpu_custom_call" | custom-call | flops 21474836480 | bytes 29360128 | tf_op jit(solution)/shard_map/feed_forward/pallas_call | solution.py:569
  278.0 48.8 %reduce-scatter.5.cloned.1.call-done.grad_ref = bf16[128,2048]{1,0:T(8,128)(2,1)} async-done(((bf16[1024,2048]{1,0:T(8,128)(2,1)}), bf16[128,2048]{1,0:T(8,128)(2,1)}) %reduce-scatter.5.cloned.1.call-update) | async-done | bytes 524304 | tf_op jit(solution)/shard_map/reduce_scatter | solution.py:715
  326.8 3.9 shard_map.145
  334.2 11.5 %collective-permute-done.17 = bf16[128,2048]{1,0:T(8,128)(2,1)S(1)} collective-permute-done((bf16[128,2048]{1,0:T(8,128)(2,1)}, bf16[128,2048]{1,0:T(8,128)(2,1)S(1)}, u32[]{:S(2)}, u32[]{:S(2)}) %collective-permute-start.17) | collective-permute-done | bytes 524320 | tf_op jit(solution)/shard_map/ppermute | solution.py:633
  345.8 9.4 %collective-permute-done.18 = bf16[128,2048]{1,0:T(8,128)(2,1)S(1)} collective-permute-done((bf16[128,2048]{1,0:T(8,128)(2,1)}, bf16[128,2048]{1,0:T(8,128)(2,1)S(1)}, u32[]{:S(2)}, u32[]{:S(2)}) %collective-permute-start.18) | collective-permute-done | bytes 524320 | tf_op jit(solution)/shard_map/ppermute | solution.py:633
  356.2 3.6 bitcast_convert_fusion
  359.9 9.7 %feed_out.1 = bf16[1024,2048]{1,0:T(8,128)(2,1)} custom-call(bf16[1024,1024]{1,0:T(8,128)(2,1)} %get-tuple-element.85.act_ref.right_ref, bf16[512,1536]{1,0:T(8,128)(2,1)} %copy-done.1, bf16[256,1536]{1,0:T(8,128)(2,1)} %copy-done.21, bf16[256,1536]{1,0:T(8,128)(2,1)} %copy-done.22, bf16[512,1536]{1,0:T(8,128)(2,1)} %copy-done.19, bf16[512,1536]{1,0:T(8,128)(2,1)} %copy-done.18), custom_call_target="tpu_custom_call" | custom-call | flops 4294967296 | bytes 10485760 | tf_op jit(solution)/shard_map/feed_out/pallas_call | solution.py:613
  369.6 10.1 %outer_blocks.5 = (bf16[1024,512]{1,0:T(8,128)(2,1)}, bf16[512,512]{1,0:T(8,128)(2,1)}, bf16[512,512]{1,0:T(8,128)(2,1)}, bf16[1024,512]{1,0:T(8,128)(2,1)}, bf1...) custom-call(bf16[1024,2048]{1,0:T(8,128)(2,1)} %all-gather.8.cloned.1.call-done.dy_ref.left_ref, ...), custom_call_target="tpu_custom_call" | custom-call | flops 4294967296 | bytes 10485760 | tf_op jit(solution)/shard_map/outer_blocks/pallas_call | solution.py:537
  381.6 2.5 fusion.2
  385.3 4.2 all-to-all-start.1
  389.7 16.8 %collective-permute-done.31 = bf16[1024,512]{1,0:T(8,128)(2,1)} collective-permute-done((bf16[1024,512]{1,0:T(8,128)(2,1)}, bf16[1024,512]{1,0:T(8,128)(2,1)}, u32[]{:S(2)}, u32[]{:S(2)}) %collective-permute-start.31) | collective-permute-done | bytes 1048608 | tf_op jit(solution)/shard_map/ppermute | solution.py:633
  408.0 3.2 collective-permute-done.33
  412.6 21.0 %attention_backward.1 = (bf16[1024,768]{1,0:T(8,128)(2,1)}, bf16[1024,2048]{1,0:T(8,128)(2,1)}) custom-call(bf16[1024,256]{1,0:T(8,128)(2,1)} %get-tuple-element.87.q_ref, bf16[1024,256]{1,0:T(8,128)(2,1)} %get-tuple-element.88.k_ref, bf16[1024,256]{1,0:T(8,128)(2,1)} %get-tuple-element.89.v_ref, bf16[4,8,64,128]{3,2,1,0:T(8,128)(2,1)} %get-tuple-element.72.attn_ref, ...), custom_call_target="tpu_custom_call" | custom-call | flops 4563402752 | bytes 12582912 | tf_op jit(solution)/shard_map/attention_backward/pallas_call | solution.py:238
  433.6 17.7 %outer_blocks.4 = (bf16[1024,512]{1,0:T(8,128)(2,1)}, bf16[512,512]{1,0:T(8,128)(2,1)}, bf16[512,512]{1,0:T(8,128)(2,1)}, bf16[1024,512]{1,0:T(8,128)(2,1)}, bf1...) custom-call(bf16[1024,2048]{1,0:T(8,128)(2,1)} %all-gather.6.cloned., ...), custom_call_target="tpu_custom_call" | custom-call | flops 8589934592 | bytes 16777216 | tf_op jit(solution)/shard_map/outer_blocks/pallas_call | solution.py:537
  451.4 2.0 collective-permute-start.27
  454.6 1.6 add_convert_fusion.3
  458.7 4.4 all-to-all-start.5
  463.0 12.8 %collective-permute-done.27 = bf16[1024,512]{1,0:T(8,128)(2,1)} collective-permute-done((bf16[1024,512]{1,0:T(8,128)(2,1)}, bf16[1024,512]{1,0:T(8,128)(2,1)}, u32[]{:S(2)}, u32[]{:S(2)}) %collective-permute-start.27) | collective-permute-done | bytes 1048608 | tf_op jit(solution)/shard_map/ppermute | solution.py:633
  480.1 1.7 collective-permute-start.23
  482.7 9.3 %collective-permute-done.28 = bf16[512,512]{1,0:T(8,128)(2,1)S(1)} collective-permute-done((bf16[512,512]{1,0:T(8,128)(2,1)S(1)}, bf16[512,512]{1,0:T(8,128)(2,1)S(1)}, u32[]{:S(2)}, u32[]{:S(2)}) %collective-permute-start.28) | collective-permute-done | bytes 524320 | tf_op jit(solution)/shard_map/ppermute | solution.py:633
  496.9 10.0 %all-to-all-done.5.refs_0_ = bf16[8,64,1024]{2,1,0:T(8,128)(2,1)S(1)} async-done(((bf16[8,64,1024]{2,1,0:T(8,128)(2,1)}), bf16[8,64,1024]{2,1,0:T(8,128)(2,1)S(1)}, u32[]{:S(2)}, u32[]{:S(2)}) %all-to-all-start.5) | async-done | bytes 1048608 | tf_op jit(solution)/shard_map/all_to_all | solution.py:719
  506.9 4.2 all-to-all-start.4
  511.2 2.9 collective-permute-done.23
  518.1 8.8 %collective-permute-done.24 = bf16[512,512]{1,0:T(8,128)(2,1)S(1)} collective-permute-done((bf16[512,512]{1,0:T(8,128)(2,1)S(1)}, bf16[512,512]{1,0:T(8,128)(2,1)S(1)}, u32[]{:S(2)}, u32[]{:S(2)}) %collective-permute-start.24) | collective-permute-done | bytes 524320 | tf_op jit(solution)/shard_map/ppermute | solution.py:633
  528.1 1.5 collective-permute-done.26
  532.0 9.9 %all-to-all-done.4.refs_1_ = bf16[8,64,1024]{2,1,0:T(8,128)(2,1)} async-done(((bf16[8,64,1024]{2,1,0:T(8,128)(2,1)}), bf16[8,64,1024]{2,1,0:T(8,128)(2,1)}, u32[]{:S(2)}, u32[]{:S(2)}) %all-to-all-start.4) | async-done | bytes 1048608 | tf_op jit(solution)/shard_map/all_to_all | solution.py:719
  541.9 3.6 all-to-all-start.3
  545.4 8.1 %outer_blocks.3 = (bf16[512,768]{1,0:T(8,128)(2,1)}, bf16[512,768]{1,0:T(8,128)(2,1)}, bf16[512,768]{1,0:T(8,128)(2,1)}, bf16[512,768]{1,0:T(8,128)(2,1)}) custom-call(bf16[1024,2048]{1,0:T(8,128)(2,1)} %all-gather.4.cloned.1.call-done.xn_ref.left_ref, bf16[1024,768]{1,0:T(8,128)(2,1)} %get-tuple-element.95.right_ref), custom_call_target="tpu_custom_call" | custom-call | flops 3221225472 | bytes 8912896 | tf_op jit(solution)/shard_map/outer_blocks/pallas_call | solution.py:537
  557.0 17.1 %collective-permute-done.20 = bf16[512,768]{1,0:T(8,128)(2,1)S(1)} collective-permute-done((bf16[512,768]{1,0:T(8,128)(2,1)}, bf16[512,768]{1,0:T(8,128)(2,1)S(1)}, u32[]{:S(2)}, u32[]{:S(2)}) %collective-permute-start.20) | collective-permute-done | bytes 786464 | tf_op jit(solution)/shard_map/ppermute | solution.py:633
  574.1 17.3 %collective-permute-done.21 = bf16[512,768]{1,0:T(8,128)(2,1)S(1)} collective-permute-done((bf16[512,768]{1,0:T(8,128)(2,1)}, bf16[512,768]{1,0:T(8,128)(2,1)S(1)}, u32[]{:S(2)}, u32[]{:S(2)}) %collective-permute-start.21) | collective-permute-done | bytes 786464 | tf_op jit(solution)/shard_map/ppermute | solution.py:633
  592.8 2.4 add_convert_fusion
  595.2 4.7 all-to-all-start.2
  600.0 3.1 side_rows.3
  603.1 4.3 side_rows.2
  609.6 11.5 %all-to-all-done.2.in_ref = bf16[8,64,768]{2,1,0:T(8,128)(2,1)} async-done(((bf16[8,64,768]{2,1,0:T(8,128)(2,1)}), bf16[8,64,768]{2,1,0:T(8,128)(2,1)}, u32[]{:S(2)}, u32[]{:S(2)}) %all-to-all-start.2) | async-done | bytes 786464 | tf_op jit(solution)/shard_map/all_to_all | solution.py:719
  621.0 2.8 strided_rows.1
  626.0 1.8 convert_element_type.214
  627.8 3.1 shard_map.146
  630.8 3.8 shard_map.147
  (162 shorter events, 60.4 us)
Async XLA Ops:
  7.2 98.5 %copy-start = (bf16[512,2048]{1,0:T(8,128)(2,1)S(1)}, bf16[512,2048]{1,0:T(8,128)(2,1)}, u32[]{:S(2)}) copy-start(bf16[512,2048]{1,0:T(8,128)(2,1)} %param.11) | copy-start | bytes 6291460
  7.2 53.9 %all-gather.4.cloned.1.call-start = ((), (), s32[]{:S(2)}) async-start(), calls=%async_computation.10 | async-start | bytes 4718592 | tf_op jit(solution)/shard_map/all_gather | solution.py:711
  11.3 234.9 %all-gather.8.cloned.1.call-start = ((), (), s32[]{:S(2)}) async-start(), calls=%async_computation.12 | async-start | bytes 4718592 | tf_op jit(solution)/shard_map/all_gather | solution.py:711
  14.1 22.5 %collective-permute-start.2 = (bf16[512,384]{1,0:T(8,128)(2,1)}, bf16[512,384]{1,0:T(8,128)(2,1)S(1)}, u32[]{:S(2)}, u32[]{:S(2)}) collective-permute-start(bf16[512,384]{1,0:T(8,128)(2,1)} %get-tuple-element.68.refs_1_), channel_id=1, source_target_pairs={{0,16},{8,24},{16,0},{24,8},{1,17},{9,25},{17,1},{25,9},{2,18},{10... | collective-permute-start | bytes 1179656 | tf_op jit(solution)/shard_map/ppermute | solution.py:633
  17.1 44.0 %collective-permute-start.4 = (bf16[512,384]{1,0:T(8,128)(2,1)}, bf16[512,384]{1,0:T(8,128)(2,1)}, u32[]{:S(2)}, u32[]{:S(2)}) collective-permute-start(bf16[512,384]{1,0:T(8,128)(2,1)} %get-tuple-element.68.refs_1_), channel_id=1, source_target_pairs={{0,8},{8,0},{16,24},{24,16},{1,9},{9,1},{17,25},{25,17},{2,10},{10... | collective-permute-start | bytes 1179656 | tf_op jit(solution)/shard_map/ppermute | solution.py:633
  18.6 17.7 %collective-permute-start = (bf16[512,384]{1,0:T(8,128)(2,1)}, bf16[512,384]{1,0:T(8,128)(2,1)S(1)}, u32[]{:S(2)}, u32[]{:S(2)}) collective-permute-start(bf16[512,384]{1,0:T(8,128)(2,1)} %get-tuple-element.67.refs_0_), channel_id=1, source_target_pairs={{0,8},{8,0},{16,24},{24,16},{1,9},{9,1},{17,25},{25,17},{2,10},{10... | collective-permute-start | bytes 1179656 | tf_op jit(solution)/shard_map/ppermute | solution.py:633
  19.1 42.0 %collective-permute-start.5 = (bf16[512,384]{1,0:T(8,128)(2,1)}, bf16[512,384]{1,0:T(8,128)(2,1)}, u32[]{:S(2)}, u32[]{:S(2)}) collective-permute-start(bf16[512,384]{1,0:T(8,128)(2,1)} %get-tuple-element.67.refs_0_), channel_id=1, source_target_pairs={{0,16},{8,24},{16,0},{24,8},{1,17},{9,25},{17,1},{25,9},{2,18},{10... | collective-permute-start | bytes 1179656 | tf_op jit(solution)/shard_map/ppermute | solution.py:633
  36.3 9.8 %collective-permute-start.1 = (bf16[512,384]{1,0:T(8,128)(2,1)S(1)}, bf16[512,384]{1,0:T(8,128)(2,1)S(1)}, u32[]{:S(2)}, u32[]{:S(2)}) collective-permute-start(bf16[512,384]{1,0:T(8,128)(2,1)S(1)} %collective-permute-done.refs_2_), channel_id=1, source_target_pairs={{0,16},{8,24},{16,0},{24,8},{1,17},{9,25},{17,1},{25,9},{2,18},{10... | collective-permute-start | bytes 1179656 | tf_op jit(solution)/shard_map/ppermute | solution.py:633
  36.6 9.8 %collective-permute-start.3 = (bf16[512,384]{1,0:T(8,128)(2,1)S(1)}, bf16[512,384]{1,0:T(8,128)(2,1)S(1)}, u32[]{:S(2)}, u32[]{:S(2)}) collective-permute-start(bf16[512,384]{1,0:T(8,128)(2,1)S(1)} %collective-permute-done.2.refs_7_), channel_id=1, source_target_pairs={{0,8},{8,0},{16,24},{24,16},{1,9},{9,1},{17,25},{25,17},{2,10},{10... | collective-permute-start | bytes 1179656 | tf_op jit(solution)/shard_map/ppermute | solution.py:633
  77.1 28.5 %all-to-all-start = ((bf16[32,64,128]{2,1,0:T(8,128)(2,1)}), bf16[32,64,128]{2,1,0:T(8,128)(2,1)S(1)}, u32[]{:S(2)}, u32[]{:S(2)}) async-start(bf16[32,64,128]{2,1,0:T(8,128)(2,1)} %bitcast.50), calls=%async_computation | async-start | bytes 1048576 | tf_op jit(solution)/shard_map/all_to_all | solution.py:719
  80.5 165.8 %all-gather.6.cloned.1.call-start = ((), (), s32[]{:S(2)}) async-start(), calls=%async_computation.11 | async-start | bytes 4718592 | tf_op jit(solution)/shard_map/all_gather | solution.py:711
  106.1 13.8 %collective-permute-start.6 = (bf16[128,2048]{1,0:T(8,128)(2,1)S(1)}, bf16[128,2048]{1,0:T(8,128)(2,1)S(1)}, u32[]{:S(2)}, u32[]{:S(2)}) collective-permute-start(bf16[128,2048]{1,0:T(8,128)(2,1)S(1)} %convolution_convert_fusion.2), channel_id=1, source_target_pairs={{0,8},{8,0},{16,24},{24,16},{1,9},{9,1},{17,25},{25,17},{2,10},{10... | collective-permute-start | bytes 1572872 | tf_op jit(solution)/shard_map/ppermute | solution.py:633
  106.7 13.3 %collective-permute-start.7 = (bf16[128,2048]{1,0:T(8,128)(2,1)S(1)}, bf16[128,2048]{1,0:T(8,128)(2,1)}, u32[]{:S(2)}, u32[]{:S(2)}) collective-permute-start(bf16[128,2048]{1,0:T(8,128)(2,1)S(1)} %convolution_convert_fusion.1), channel_id=1, source_target_pairs={{0,16},{8,24},{16,0},{24,8},{1,17},{9,25},{17,1},{25,9},{2,18},{10... | collective-permute-start | bytes 1572872 | tf_op jit(solution)/shard_map/ppermute | solution.py:633
  108.3 22.0 %collective-permute-start.8 = (bf16[128,2048]{1,0:T(8,128)(2,1)S(1)}, bf16[128,2048]{1,0:T(8,128)(2,1)}, u32[]{:S(2)}, u32[]{:S(2)}) collective-permute-start(bf16[128,2048]{1,0:T(8,128)(2,1)S(1)} %convolution_convert_fusion), channel_id=1, source_target_pairs={{0,24},{8,16},{16,8},{24,0},{1,25},{9,17},{17,9},{25,1},{2,26},{10... | collective-permute-start | bytes 1572872 | tf_op jit(solution)/shard_map/ppermute | solution.py:633
  120.0 10.4 %copy-start.11 = (bf16[128,2048]{1,0:T(8,128)(2,1)}, bf16[128,2048]{1,0:T(8,128)(2,1)S(1)}, u32[]{:S(2)}) copy-start(bf16[128,2048]{1,0:T(8,128)(2,1)S(1)} %collective-permute-done.6.refs_0_) | copy-start | bytes 1572868
  134.6 192.2 %reduce-scatter.5.cloned.1.call-start = ((), (), s32[]{:S(2)}) async-start(), calls=%async_computation.13 | async-start | bytes 4718592 | tf_op jit(solution)/shard_map/reduce_scatter | solution.py:715
  134.8 37.7 %collective-permute-start.15 = (bf16[512,1536]{1,0:T(8,128)(2,1)}, bf16[512,1536]{1,0:T(8,128)(2,1)S(1)}, u32[]{:S(2)}, u32[]{:S(2)}) collective-permute-start(bf16[512,1536]{1,0:T(8,128)(2,1)} %copy-done.1), channel_id=1, source_target_pairs={{0,16},{8,24},{16,0},{24,8},{1,17},{9,25},{17,1},{25,9},{2,18},{10... | collective-permute-start | bytes 4718600 | tf_op jit(solution)/shard_map/ppermute | solution.py:633
  137.4 38.8 %collective-permute-start.9 = (bf16[512,1536]{1,0:T(8,128)(2,1)}, bf16[512,1536]{1,0:T(8,128)(2,1)S(1)}, u32[]{:S(2)}, u32[]{:S(2)}) collective-permute-start(bf16[512,1536]{1,0:T(8,128)(2,1)} %copy-done.2), channel_id=1, source_target_pairs={{0,8},{8,0},{16,24},{24,16},{1,9},{9,1},{17,25},{25,17},{2,10},{10... | collective-permute-start | bytes 4718600 | tf_op jit(solution)/shard_map/ppermute | solution.py:633
  138.7 50.6 %collective-permute-start.11 = (bf16[256,1536]{1,0:T(8,128)(2,1)}, bf16[256,1536]{1,0:T(8,128)(2,1)S(1)}, u32[]{:S(2)}, u32[]{:S(2)}) collective-permute-start(bf16[256,1536]{1,0:T(8,128)(2,1)} %get-tuple-element.78), channel_id=1, source_target_pairs={{0,16},{8,24},{16,0},{24,8},{1,17},{9,25},{17,1},{25,9},{2,18},{10... | collective-permute-start | bytes 2359304 | tf_op jit(solution)/shard_map/ppermute | solution.py:633
  172.5 71.5 %copy-start.18 = (bf16[512,1536]{1,0:T(8,128)(2,1)}, bf16[512,1536]{1,0:T(8,128)(2,1)S(1)}, u32[]{:S(2)}) copy-start(bf16[512,1536]{1,0:T(8,128)(2,1)S(1)} %collective-permute-done.15.refs_9_.refs_4_) | copy-start | bytes 4718596
  172.5 71.5 %collective-permute-start.16 = (bf16[512,1536]{1,0:T(8,128)(2,1)S(1)}, bf16[512,1536]{1,0:T(8,128)(2,1)S(1)}, u32[]{:S(2)}, u32[]{:S(2)}) collective-permute-start(bf16[512,1536]{1,0:T(8,128)(2,1)S(1)} %collective-permute-done.15.refs_9_.refs_4_), channel_id=1, source_target_pairs={{0,8},{8,0},{16,24},{24,16},{1,9},{9,1},{17,25},{25,17},{2,10},{10... | collective-permute-start | bytes 4718600 | tf_op jit(solution)/shard_map/ppermute | solution.py:633
  176.1 67.9 %copy-start.20 = (bf16[512,1536]{1,0:T(8,128)(2,1)}, bf16[512,1536]{1,0:T(8,128)(2,1)S(1)}, u32[]{:S(2)}) copy-start(bf16[512,1536]{1,0:T(8,128)(2,1)S(1)} %collective-permute-done.9.refs_1_) | copy-start | bytes 4718596
  176.1 70.1 %collective-permute-start.10 = (bf16[512,1536]{1,0:T(8,128)(2,1)S(1)}, bf16[512,1536]{1,0:T(8,128)(2,1)}, u32[]{:S(2)}, u32[]{:S(2)}) collective-permute-start(bf16[512,1536]{1,0:T(8,128)(2,1)S(1)} %collective-permute-done.9.refs_1_), channel_id=1, source_target_pairs={{0,16},{8,24},{16,0},{24,8},{1,17},{9,25},{17,1},{25,9},{2,18},{10... | collective-permute-start | bytes 4718600 | tf_op jit(solution)/shard_map/ppermute | solution.py:633
  176.1 52.1 %collective-permute-start.13 = (bf16[256,1536]{1,0:T(8,128)(2,1)}, bf16[256,1536]{1,0:T(8,128)(2,1)S(1)}, u32[]{:S(2)}, u32[]{:S(2)}) collective-permute-start(bf16[256,1536]{1,0:T(8,128)(2,1)} %get-tuple-element.80), channel_id=1, source_target_pairs={{0,8},{8,0},{16,24},{24,16},{1,9},{9,1},{17,25},{25,17},{2,10},{10... | collective-permute-start | bytes 2359304 | tf_op jit(solution)/shard_map/ppermute | solution.py:633
  177.5 66.5 %collective-permute-start.14 = (bf16[256,1536]{1,0:T(8,128)(2,1)}, bf16[256,1536]{1,0:T(8,128)(2,1)S(1)}, u32[]{:S(2)}, u32[]{:S(2)}) collective-permute-start(bf16[256,1536]{1,0:T(8,128)(2,1)} %get-tuple-element.81), channel_id=1, source_target_pairs={{0,8},{8,0},{16,24},{24,16},{1,9},{9,1},{17,25},{25,17},{2,10},{10... | collective-permute-start | bytes 2359304 | tf_op jit(solution)/shard_map/ppermute | solution.py:633
  189.3 54.7 %copy-start.23 = (bf16[256,1536]{1,0:T(8,128)(2,1)}, bf16[256,1536]{1,0:T(8,128)(2,1)S(1)}, u32[]{:S(2)}) copy-start(bf16[256,1536]{1,0:T(8,128)(2,1)S(1)} %collective-permute-done.11.refs_3_) | copy-start | bytes 2359300
  189.3 54.7 %collective-permute-start.12 = (bf16[256,1536]{1,0:T(8,128)(2,1)S(1)}, bf16[256,1536]{1,0:T(8,128)(2,1)S(1)}, u32[]{:S(2)}, u32[]{:S(2)}) collective-permute-start(bf16[256,1536]{1,0:T(8,128)(2,1)S(1)} %get-tuple-element.79), channel_id=1, source_target_pairs={{0,16},{8,24},{16,0},{24,8},{1,17},{9,25},{17,1},{25,9},{2,18},{10... | collective-permute-start | bytes 2359304 | tf_op jit(solution)/shard_map/ppermute | solution.py:633
  228.2 15.8 %copy-start.21 = (bf16[256,1536]{1,0:T(8,128)(2,1)}, bf16[256,1536]{1,0:T(8,128)(2,1)S(1)}, u32[]{:S(2)}) copy-start(bf16[256,1536]{1,0:T(8,128)(2,1)S(1)} %collective-permute-done.13.refs_6_.refs_1_) | copy-start | bytes 2359300
  277.4 78.7 %copy-start.13 = (bf16[1,512,128]{2,1,0:T(8,128)(2,1)S(1)}, bf16[1,512,128]{2,1,0:T(8,128)(2,1)}, u32[]{:S(2)}) copy-start(bf16[1,512,128]{2,1,0:T(8,128)(2,1)} %copy-done.12) | copy-start | bytes 393220
  277.4 78.7 %copy-start.15 = (bf16[1,512,128]{2,1,0:T(8,128)(2,1)S(1)}, bf16[1,512,128]{2,1,0:T(8,128)(2,1)}, u32[]{:S(2)}) copy-start(bf16[1,512,128]{2,1,0:T(8,128)(2,1)} %copy-done.14) | copy-start | bytes 393220
  277.4 78.7 %copy-start.17 = (bf16[1,512,128]{2,1,0:T(8,128)(2,1)S(1)}, bf16[1,512,128]{2,1,0:T(8,128)(2,1)}, u32[]{:S(2)}) copy-start(bf16[1,512,128]{2,1,0:T(8,128)(2,1)} %copy-done.16) | copy-start | bytes 393220
  277.5 348.5 %reduce-scatter.11.cloned.1.call-start = ((), (), s32[]{:S(2)}) async-start(), calls=%async_computation.16 | async-start | bytes 2359296 | tf_op jit(solution)/shard_map/reduce_scatter | solution.py:715
  330.8 15.0 %collective-permute-start.17 = (bf16[128,2048]{1,0:T(8,128)(2,1)}, bf16[128,2048]{1,0:T(8,128)(2,1)S(1)}, u32[]{:S(2)}, u32[]{:S(2)}) collective-permute-start(bf16[128,2048]{1,0:T(8,128)(2,1)} %get-tuple-element.90), channel_id=1, source_target_pairs={{0,8},{8,0},{16,24},{24,16},{1,9},{9,1},{17,25},{25,17},{2,10},{10... | collective-permute-start | bytes 1572872 | tf_op jit(solution)/shard_map/ppermute | solution.py:633
  332.2 23.0 %collective-permute-start.18 = (bf16[128,2048]{1,0:T(8,128)(2,1)}, bf16[128,2048]{1,0:T(8,128)(2,1)S(1)}, u32[]{:S(2)}, u32[]{:S(2)}) collective-permute-start(bf16[128,2048]{1,0:T(8,128)(2,1)} %get-tuple-element.90), channel_id=1, source_target_pairs={{0,16},{8,24},{16,0},{24,8},{1,17},{9,25},{17,1},{25,9},{2,18},{10... | collective-permute-start | bytes 1572872 | tf_op jit(solution)/shard_map/ppermute | solution.py:633
  333.7 21.5 %collective-permute-start.19 = (bf16[128,2048]{1,0:T(8,128)(2,1)}, bf16[128,2048]{1,0:T(8,128)(2,1)S(1)}, u32[]{:S(2)}, u32[]{:S(2)}) collective-permute-start(bf16[128,2048]{1,0:T(8,128)(2,1)} %get-tuple-element.90), channel_id=1, source_target_pairs={{0,24},{8,16},{16,8},{24,0},{1,25},{9,17},{17,9},{25,1},{2,26},{10... | collective-permute-start | bytes 1572872 | tf_op jit(solution)/shard_map/ppermute | solution.py:633
  359.8 267.9 %reduce-scatter.7.cloned.1.call-start = ((), (), s32[]{:S(2)}) async-start(), calls=%async_computation.14 | async-start | bytes 4718592 | tf_op jit(solution)/shard_map/reduce_scatter | solution.py:715
  369.6 12.1 %copy-start.25 = (bf16[128,2048]{1,0:T(8,128)(2,1)S(1)}, bf16[128,2048]{1,0:T(8,128)(2,1)}, u32[]{:S(2)}) copy-start(bf16[128,2048]{1,0:T(8,128)(2,1)} %get-tuple-element.90) | copy-start | bytes 1572868
  379.6 26.9 %collective-permute-start.31 = (bf16[1024,512]{1,0:T(8,128)(2,1)}, bf16[1024,512]{1,0:T(8,128)(2,1)}, u32[]{:S(2)}, u32[]{:S(2)}) collective-permute-start(bf16[1024,512]{1,0:T(8,128)(2,1)} %get-tuple-element.118), channel_id=1, source_target_pairs={{0,8},{8,0},{16,24},{24,16},{1,9},{9,1},{17,25},{25,17},{2,10},{10... | collective-permute-start | bytes 3145736 | tf_op jit(solution)/shard_map/ppermute | solution.py:633
  380.6 30.6 %collective-permute-start.33 = (bf16[1024,512]{1,0:T(8,128)(2,1)}, bf16[1024,512]{1,0:T(8,128)(2,1)}, u32[]{:S(2)}, u32[]{:S(2)}) collective-permute-start(bf16[1024,512]{1,0:T(8,128)(2,1)} %get-tuple-element.121), channel_id=1, source_target_pairs={{0,16},{8,24},{16,0},{24,8},{1,17},{9,25},{17,1},{25,9},{2,18},{10... | collective-permute-start | bytes 3145736 | tf_op jit(solution)/shard_map/ppermute | solution.py:633
  384.1 22.4 %copy-start.5 = (bf16[512,512]{1,0:T(8,128)(2,1)S(1)}, bf16[512,512]{1,0:T(8,128)(2,1)}, u32[]{:S(2)}) copy-start(bf16[512,512]{1,0:T(8,128)(2,1)} %get-tuple-element.119) | copy-start | bytes 1572868
  385.3 27.4 %all-to-all-start.1 = ((bf16[32,64,128]{2,1,0:T(8,128)(2,1)}), bf16[32,64,128]{2,1,0:T(8,128)(2,1)}, u32[]{:S(2)}, u32[]{:S(2)}) async-start(bf16[32,64,128]{2,1,0:T(8,128)(2,1)} %bitcast.18), calls=%async_computation.3 | async-start | bytes 1048576 | tf_op jit(solution)/shard_map/all_to_all | solution.py:719
  389.5 241.4 %reduce-scatter.9.cloned.1.call-start = ((), (), s32[]{:S(2)}) async-start(), calls=%async_computation.15 | async-start | bytes 4718592 | tf_op jit(solution)/shard_map/reduce_scatter | solution.py:715
  407.7 46.8 %collective-permute-start.32 = (bf16[512,512]{1,0:T(8,128)(2,1)S(1)}, bf16[512,512]{1,0:T(8,128)(2,1)}, u32[]{:S(2)}, u32[]{:S(2)}) collective-permute-start(bf16[512,512]{1,0:T(8,128)(2,1)S(1)} %add_convert_fusion.4), channel_id=1, source_target_pairs={{0,16},{8,24},{16,0},{24,8},{1,17},{9,25},{17,1},{25,9},{2,18},{10... | collective-permute-start | bytes 1572872 | tf_op jit(solution)/shard_map/ppermute | solution.py:633
  412.5 43.6 %collective-permute-start.34 = (bf16[512,512]{1,0:T(8,128)(2,1)S(1)}, bf16[512,512]{1,0:T(8,128)(2,1)}, u32[]{:S(2)}, u32[]{:S(2)}) collective-permute-start(bf16[512,512]{1,0:T(8,128)(2,1)S(1)} %add_convert_fusion.2), channel_id=1, source_target_pairs={{0,8},{8,0},{16,24},{24,16},{1,9},{9,1},{17,25},{25,17},{2,10},{10... | collective-permute-start | bytes 1572872 | tf_op jit(solution)/shard_map/ppermute | solution.py:633
  451.4 24.4 %collective-permute-start.27 = (bf16[1024,512]{1,0:T(8,128)(2,1)}, bf16[1024,512]{1,0:T(8,128)(2,1)}, u32[]{:S(2)}, u32[]{:S(2)}) collective-permute-start(bf16[1024,512]{1,0:T(8,128)(2,1)} %get-tuple-element.110), channel_id=1, source_target_pairs={{0,8},{8,0},{16,24},{24,16},{1,9},{9,1},{17,25},{25,17},{2,10},{10... | collective-permute-start | bytes 3145736 | tf_op jit(solution)/shard_map/ppermute | solution.py:633
  453.4 25.0 %collective-permute-start.29 = (bf16[1024,512]{1,0:T(8,128)(2,1)}, bf16[1024,512]{1,0:T(8,128)(2,1)}, u32[]{:S(2)}, u32[]{:S(2)}) collective-permute-start(bf16[1024,512]{1,0:T(8,128)(2,1)} %get-tuple-element.113), channel_id=1, source_target_pairs={{0,16},{8,24},{16,0},{24,8},{1,17},{9,25},{17,1},{25,9},{2,18},{10... | collective-permute-start | bytes 3145736 | tf_op jit(solution)/shard_map/ppermute | solution.py:633
  458.7 48.3 %all-to-all-start.5 = ((bf16[8,64,1024]{2,1,0:T(8,128)(2,1)}), bf16[8,64,1024]{2,1,0:T(8,128)(2,1)S(1)}, u32[]{:S(2)}, u32[]{:S(2)}) async-start(bf16[8,64,1024]{2,1,0:T(8,128)(2,1)} %bitcast.46), calls=%async_computation.9 | async-start | bytes 2097152 | tf_op jit(solution)/shard_map/all_to_all | solution.py:719
  463.0 29.0 %copy-start.10 = (bf16[512,512]{1,0:T(8,128)(2,1)S(1)}, bf16[512,512]{1,0:T(8,128)(2,1)}, u32[]{:S(2)}) copy-start(bf16[512,512]{1,0:T(8,128)(2,1)} %get-tuple-element.109) | copy-start | bytes 1572868
  477.2 17.4 %copy-start.9 = (bf16[512,512]{1,0:T(8,128)(2,1)S(1)}, bf16[512,512]{1,0:T(8,128)(2,1)}, u32[]{:S(2)}) copy-start(bf16[512,512]{1,0:T(8,128)(2,1)} %get-tuple-element.112) | copy-start | bytes 1572868
  477.2 14.9 %collective-permute-start.28 = (bf16[512,512]{1,0:T(8,128)(2,1)S(1)}, bf16[512,512]{1,0:T(8,128)(2,1)S(1)}, u32[]{:S(2)}, u32[]{:S(2)}) collective-permute-start(bf16[512,512]{1,0:T(8,128)(2,1)S(1)} %add_convert_fusion.8), channel_id=1, source_target_pairs={{0,16},{8,24},{16,0},{24,8},{1,17},{9,25},{17,1},{25,9},{2,18},{10... | collective-permute-start | bytes 1572872 | tf_op jit(solution)/shard_map/ppermute | solution.py:633
  479.7 14.9 %collective-permute-start.30 = (bf16[512,512]{1,0:T(8,128)(2,1)S(1)}, bf16[512,512]{1,0:T(8,128)(2,1)S(1)}, u32[]{:S(2)}, u32[]{:S(2)}) collective-permute-start(bf16[512,512]{1,0:T(8,128)(2,1)S(1)} %add_convert_fusion.6), channel_id=1, source_target_pairs={{0,8},{8,0},{16,24},{24,16},{1,9},{9,1},{17,25},{25,17},{2,10},{10... | collective-permute-start | bytes 1572872 | tf_op jit(solution)/shard_map/ppermute | solution.py:633
  480.1 34.0 %collective-permute-start.23 = (bf16[1024,512]{1,0:T(8,128)(2,1)}, bf16[1024,512]{1,0:T(8,128)(2,1)}, u32[]{:S(2)}, u32[]{:S(2)}) collective-permute-start(bf16[1024,512]{1,0:T(8,128)(2,1)} %get-tuple-element.104), channel_id=1, source_target_pairs={{0,8},{8,0},{16,24},{24,16},{1,9},{9,1},{17,25},{25,17},{2,10},{10... | collective-permute-start | bytes 3145736 | tf_op jit(solution)/shard_map/ppermute | solution.py:633
  481.8 34.6 %collective-permute-start.25 = (bf16[1024,512]{1,0:T(8,128)(2,1)}, bf16[1024,512]{1,0:T(8,128)(2,1)}, u32[]{:S(2)}, u32[]{:S(2)}) collective-permute-start(bf16[1024,512]{1,0:T(8,128)(2,1)} %get-tuple-element.107), channel_id=1, source_target_pairs={{0,16},{8,24},{16,0},{24,8},{1,17},{9,25},{17,1},{25,9},{2,18},{10... | collective-permute-start | bytes 3145736 | tf_op jit(solution)/shard_map/ppermute | solution.py:633
  506.9 10.8 %copy-start.3 = (bf16[8,64,1024]{2,1,0:T(8,128)(2,1)}, bf16[8,64,1024]{2,1,0:T(8,128)(2,1)S(1)}, u32[]{:S(2)}) copy-start(bf16[8,64,1024]{2,1,0:T(8,128)(2,1)S(1)} %all-to-all-done.5.refs_0_) | copy-start | bytes 3145732
  506.9 34.9 %all-to-all-start.4 = ((bf16[8,64,1024]{2,1,0:T(8,128)(2,1)}), bf16[8,64,1024]{2,1,0:T(8,128)(2,1)}, u32[]{:S(2)}, u32[]{:S(2)}) async-start(bf16[8,64,1024]{2,1,0:T(8,128)(2,1)} %bitcast.47), calls=%async_computation.8 | async-start | bytes 2097152 | tf_op jit(solution)/shard_map/all_to_all | solution.py:719
  511.2 15.7 %copy-start.8 = (bf16[512,512]{1,0:T(8,128)(2,1)S(1)}, bf16[512,512]{1,0:T(8,128)(2,1)}, u32[]{:S(2)}) copy-start(bf16[512,512]{1,0:T(8,128)(2,1)} %get-tuple-element.103) | copy-start | bytes 1572868
  515.4 14.3 %copy-start.7 = (bf16[512,512]{1,0:T(8,128)(2,1)S(1)}, bf16[512,512]{1,0:T(8,128)(2,1)}, u32[]{:S(2)}) copy-start(bf16[512,512]{1,0:T(8,128)(2,1)} %get-tuple-element.106) | copy-start | bytes 1572868
  515.4 11.5 %collective-permute-start.24 = (bf16[512,512]{1,0:T(8,128)(2,1)S(1)}, bf16[512,512]{1,0:T(8,128)(2,1)S(1)}, u32[]{:S(2)}, u32[]{:S(2)}) collective-permute-start(bf16[512,512]{1,0:T(8,128)(2,1)S(1)} %add_convert_fusion.12), channel_id=1, source_target_pairs={{0,16},{8,24},{16,0},{24,8},{1,17},{9,25},{17,1},{25,9},{2,18},{10... | collective-permute-start | bytes 1572872 | tf_op jit(solution)/shard_map/ppermute | solution.py:633
  517.7 11.9 %collective-permute-start.26 = (bf16[512,512]{1,0:T(8,128)(2,1)S(1)}, bf16[512,512]{1,0:T(8,128)(2,1)S(1)}, u32[]{:S(2)}, u32[]{:S(2)}) collective-permute-start(bf16[512,512]{1,0:T(8,128)(2,1)S(1)} %add_convert_fusion.10), channel_id=1, source_target_pairs={{0,8},{8,0},{16,24},{24,16},{1,9},{9,1},{17,25},{25,17},{2,10},{10... | collective-permute-start | bytes 1572872 | tf_op jit(solution)/shard_map/ppermute | solution.py:633
  541.9 53.4 %all-to-all-start.3 = ((bf16[8,64,1024]{2,1,0:T(8,128)(2,1)}), bf16[8,64,1024]{2,1,0:T(8,128)(2,1)S(1)}, u32[]{:S(2)}, u32[]{:S(2)}) async-start(bf16[8,64,1024]{2,1,0:T(8,128)(2,1)} %bitcast.22), calls=%async_computation.7 | async-start | bytes 2097152 | tf_op jit(solution)/shard_map/all_to_all | solution.py:719
  553.5 20.6 %collective-permute-start.20 = (bf16[512,768]{1,0:T(8,128)(2,1)}, bf16[512,768]{1,0:T(8,128)(2,1)S(1)}, u32[]{:S(2)}, u32[]{:S(2)}) collective-permute-start(bf16[512,768]{1,0:T(8,128)(2,1)} %get-tuple-element.97), channel_id=1, source_target_pairs={{0,8},{8,0},{16,24},{24,16},{1,9},{9,1},{17,25},{25,17},{2,10},{10... | collective-permute-start | bytes 2359304 | tf_op jit(solution)/shard_map/ppermute | solution.py:633
  555.0 36.5 %collective-permute-start.21 = (bf16[512,768]{1,0:T(8,128)(2,1)}, bf16[512,768]{1,0:T(8,128)(2,1)S(1)}, u32[]{:S(2)}, u32[]{:S(2)}) collective-permute-start(bf16[512,768]{1,0:T(8,128)(2,1)} %get-tuple-element.98), channel_id=1, source_target_pairs={{0,24},{8,16},{16,8},{24,0},{1,25},{9,17},{17,9},{25,1},{2,26},{10... | collective-permute-start | bytes 2359304 | tf_op jit(solution)/shard_map/ppermute | solution.py:633
  556.4 36.3 %collective-permute-start.22 = (bf16[512,768]{1,0:T(8,128)(2,1)}, bf16[512,768]{1,0:T(8,128)(2,1)S(1)}, u32[]{:S(2)}, u32[]{:S(2)}) collective-permute-start(bf16[512,768]{1,0:T(8,128)(2,1)} %get-tuple-element.99), channel_id=1, source_target_pairs={{0,16},{8,24},{16,0},{24,8},{1,17},{9,25},{17,1},{25,9},{2,18},{10... | collective-permute-start | bytes 2359304 | tf_op jit(solution)/shard_map/ppermute | solution.py:633
  595.2 25.8 %all-to-all-start.2 = ((bf16[8,64,768]{2,1,0:T(8,128)(2,1)}), bf16[8,64,768]{2,1,0:T(8,128)(2,1)}, u32[]{:S(2)}, u32[]{:S(2)}) async-start(bf16[8,64,768]{2,1,0:T(8,128)(2,1)} %bitcast.48), calls=%async_computation.5 | async-start | bytes 1572864 | tf_op jit(solution)/shard_map/all_to_all | solution.py:719
  (16 other events, 46.1 us)
Sparse Core Ops, SparseCore 0:
  11.4 49.5 all-gather.3
  77.2 53.7 all-gather.7
  134.7 48.6 all-gather.5
  277.5 49.2 reduce-scatter.4
  359.9 36.0 reduce-scatter.10
  398.2 49.1 reduce-scatter.6
  449.7 65.8 reduce-scatter.8
where the time goes:
time: 651 us; the launch traced here: 642 us
  waiting for transfers between devices  361 us (55%)
  Pallas kernels  145 us (22%)
  starting transfers between devices  68 us (10%)
  other arithmetic  31.1 us (5%)
  between operations  15 us (2%)
  local copies, waits for them, and re-layouts  12.4 us (2%)
  matrix products  8.98 us (1%)
    ppermute x35, waiting for transfers between devices, partner(): return lax.ppermute(array, 'dp', [(i, i ^ bits) for i in range(4)])  244 us
    all_to_all x6, waiting for transfers between devices, exchange(): return lax.all_to_all(values, axes, split_axis=0, concat_axis=0, tiled=True)  56.3 us
    reduce_scatter x4, waiting for transfers between devices, sum_over_seq(): lax.psum_scatter(values.astype(BF), 'seq', scatter_dimension=0, tiled=True)  48.8 us
    ppermute x35, starting transfers between devices, partner(): return lax.ppermute(array, 'dp', [(i, i ^ bits) for i in range(4)])  42.8 us
    pallas_call x3, Pallas kernels, outer_blocks(): pl.pallas_call(functools.partial(outer_kernel, layouts), grid=(4,), in_sp...  35.8 us
    pallas_call x1, Pallas kernels, feed_forward(): pl.pallas_call(functools.partial(feed_kernel, len(part_a), len(part_b)),...  31.1 us
    all_to_all x6, starting transfers between devices, exchange(): return lax.all_to_all(values, axes, split_axis=0, concat_axis=0, tiled=True)  24.5 us
    pallas_call x1, Pallas kernels, attention_backward(): pl.pallas_call(functools.partial(attention_backward_kernel, block, len(pi...  21 us
  transfers between devices with their start and end apart: 48, of which 28 were waited for; matrix products, arithmetic and copies ran while one was open for 7% of the time, Pallas kernels for 13%

commit v1 on v0

--- a/solution.py
+++ b/solution.py
@@ -21,15 +21,26 @@
     return lax.optimization_barrier((values, *earlier))[0]
 
 
+def rotary_kernel(inverse_ref, cos_ref, sin_ref):
+    step = min(32, cos_ref.shape[0])
+
+    @pl.loop(0, cos_ref.shape[0] // step)
+    def _(i):
+        at = pl.ds(pl.multiple_of(i * step, step), step)
+        position = i * step + lax.broadcasted_iota(jnp.int32, (step, 128), 0)
+        angles = position.astype(F32) * inverse_ref[...]
+        lane = lax.broadcasted_iota(jnp.int32, (step, 128), 1)
+        sine = jnp.sin(angles)
+        cos_ref[at, :] = jnp.cos(angles)
+        sin_ref[at, :] = jnp.where((lane & (HD // 2)) != 0, sine, -sine)
+
+
 def rotary_tables(length):
     half = HD // 2
     inverse = THETA ** (-(jnp.arange(half).astype(F32) * 2.0) / HD)
-    angles = jnp.arange(length).astype(F32)[:, None] * inverse[None, :]
-    cosine = jnp.cos(angles)
-    sine = jnp.sin(angles)
-    return (
-        jnp.concatenate([cosine] * 4, 1),
-        jnp.concatenate([-sine, sine, -sine, sine], 1),
+    table = jax.ShapeDtypeStruct((length, 128), F32)
+    return pl.pallas_call(rotary_kernel, out_shape=[table, table], name="rotary")(
+        jnp.tile(inverse, 4)[None, :]
     )
 
 
@@ -302,11 +313,15 @@
     )(group.reshape(1), *[weight] * runs)
 
 
-def strided_rows_kernel(which_ref, in_ref, weight_ref, out_ref, sum_ref):
+def lane_sums(values):
+    return jnp.sum(values.T, axis=0, keepdims=True)
+
+
+def strided_rows_kernel(first, which_ref, in_ref, weight_ref, gain_ref, out_ref, sum_ref):
     groups, rows, width = in_ref.shape
     total = jnp.zeros((rows, 128), F32)
-    for b in range(width // HD):
-        cols = slice(b * HD, (b + 1) * HD)
+    for b in range((width - first) // HD):
+        cols = slice(first + b * HD, first + (b + 1) * HD)
         for pair in range(groups // 2):
             both = jnp.concatenate(
                 [in_ref[2 * pair, :, cols], in_ref[2 * pair + 1, :, cols]], 1
@@ -314,35 +329,36 @@
             at = (b * groups + 2 * pair) * HD
             out_ref[:, at : at + 128] = both
             total = total + both * weight_ref[:, at : at + 128].astype(F32)
-    sum_ref[...] = jnp.broadcast_to(jnp.sum(total, axis=1, keepdims=True), sum_ref.shape)
-
-
-def strided_rows(parts, weight, group):
+    sum_ref[...] = lane_sums(total) / gain_ref[...]
+
+
+def strided_rows(parts, first, weight, gain, group):
     _, rows, _ = parts.shape
     return pl.pallas_call(
-        strided_rows_kernel,
+        functools.partial(strided_rows_kernel, first),
         grid_spec=pltpu.PrefetchScalarGridSpec(
             num_scalar_prefetch=1,
             grid=(1,),
             in_specs=[
                 pl.BlockSpec(parts.shape, lambda g, w: (0, 0, 0)),
                 pl.BlockSpec((rows, weight.shape[1]), lambda g, w: (w[0], 0)),
+                pl.BlockSpec((1, rows), lambda g, w: (0, 0)),
             ],
             out_specs=[
                 pl.BlockSpec((rows, weight.shape[1]), lambda g, w: (0, 0)),
-                pl.BlockSpec((rows, 128), lambda g, w: (0, 0)),
+                pl.BlockSpec((1, rows), lambda g, w: (0, 0)),
             ],
         ),
         out_shape=[
             jax.ShapeDtypeStruct((rows, weight.shape[1]), F32),
-            jax.ShapeDtypeStruct((rows, 128), F32),
+            jax.ShapeDtypeStruct((1, rows), F32),
         ],
         name="strided_rows",
-    )(group.reshape(1), parts, weight)
+    )(group.reshape(1), parts, weight, gain)
 
 
 def side_rows_kernel(runs, which_ref, *refs):
-    parts, (weight_ref, out_ref, sum_ref) = refs[:runs], refs[runs:]
+    parts, (weight_ref, gain_ref, out_ref, sum_ref) = refs[:runs], refs[runs:]
     groups, rows, piece = parts[0].shape
 
     @pl.when(pl.program_id(0) == 0)
@@ -353,90 +369,113 @@
 
         @pl.when(pl.program_id(0) == run)
         def _():
-            total = jnp.zeros((rows, 128), F32)
-            for s in range(groups):
+            def step(s, total):
                 values = parts[run][s].astype(F32)
-                cols = slice(s * piece, (s + 1) * piece)
+                cols = pl.ds(pl.multiple_of(s * piece, piece), piece)
                 out_ref[:, cols] = values
                 product = values * weight_ref[:, cols].astype(F32)
                 for c in range(piece // 128):
                     total = total + product[:, c * 128 : (c + 1) * 128]
-            sum_ref[...] += jnp.broadcast_to(jnp.sum(total, axis=1, keepdims=True), sum_ref.shape)
-
-
-def side_rows(parts, weight, group):
-    groups, rows, piece = parts[0].shape
+                return total
+
+            total = lax.fori_loop(0, groups, step, jnp.zeros((rows, 128), F32))
+            sum_ref[...] += lane_sums(total) / gain_ref[...]
+
+
+def side_rows(parts, piece, weight, gain, group):
+    groups, rows, _ = parts[0][0].shape
     runs = len(parts)
+
+    def spec(place):
+        return pl.BlockSpec((groups, rows, piece), lambda c, w: (0, 0, place))
+
     return pl.pallas_call(
         functools.partial(side_rows_kernel, runs),
         grid_spec=pltpu.PrefetchScalarGridSpec(
             num_scalar_prefetch=1,
             grid=(runs,),
-            in_specs=[pl.BlockSpec((groups, rows, piece), lambda c, w: (0, 0, 0))] * runs
-            + [pl.BlockSpec((rows, groups * piece), lambda c, w: (w[0], c))],
+            in_specs=[spec(place) for _, place in parts]
+            + [
+                pl.BlockSpec((rows, groups * piece), lambda c, w: (w[0], c)),
+                pl.BlockSpec((1, rows), lambda c, w: (0, 0)),
+            ],
             out_specs=[
                 pl.BlockSpec((rows, groups * piece), lambda c, w: (0, c)),
-                pl.BlockSpec((rows, 128), lambda c, w: (0, 0)),
+                pl.BlockSpec((1, rows), lambda c, w: (0, 0)),
             ],
         ),
         out_shape=[
             jax.ShapeDtypeStruct((rows, runs * groups * piece), F32),
-            jax.ShapeDtypeStruct((rows, 128), F32),
+            jax.ShapeDtypeStruct((1, rows), F32),
         ],
         name="side_rows",
-    )(group.reshape(1), *parts, weight)
-
-
-def at_block(ref, index):
+    )(group.reshape(1), *[array for array, _ in parts], weight, gain)
+
+
+BLOCKS = 4
+
+
+def at_block(ref, rows, index):
     width = ref.shape[1] // BLOCKS
-    return ref.at[:, pl.ds(pl.multiple_of(index * width, width), width)]
-
-
-BLOCKS = 4
-
-
-def norm_in_kernel(orders_ref, x_ref, gain_ref, grad_ref, xn_ref, dy_ref):
-    x = x_ref[...]
+    return ref.at[rows, pl.ds(pl.multiple_of(index * width, width), width)]
+
+
+def by_rows(kernel):
+    def run(table_ref, x_ref, *refs):
+        step = min(32, x_ref.shape[0])
+
+        @pl.loop(0, x_ref.shape[0] // step)
+        def _(i):
+            kernel(pl.ds(pl.multiple_of(i * step, step), step), table_ref, x_ref, *refs)
+
+    return run
+
+
+ALL = slice(None)
+
+
+def norm_in_kernel(rows, orders_ref, x_ref, gain_ref, grad_ref, xn_ref, dy_ref):
+    x = x_ref[rows, :]
     inv = lax.rsqrt(jnp.mean(x * x, axis=1, keepdims=True) + EPS)
     for p in range(BLOCKS):
         block = orders_ref[p]
-        normed = at_block(x_ref, block)[...] * inv * at_block(gain_ref, block)[...]
-        at_block(xn_ref, p)[...] = normed.astype(BF)
-        at_block(dy_ref, p)[...] = at_block(grad_ref, block)[...].astype(BF)
-
-
-def norm_mid_kernel(orders_ref, x_ref, own_ref, *refs):
+        normed = at_block(x_ref, rows, block)[...] * inv * at_block(gain_ref, ALL, block)[...]
+        at_block(xn_ref, rows, p)[...] = normed.astype(BF)
+        at_block(dy_ref, rows, p)[...] = at_block(grad_ref, rows, block)[...].astype(BF)
+
+
+def norm_mid_kernel(rows, orders_ref, x_ref, own_ref, *refs):
     others, (gain_ref, mid_ref, xn_ref) = refs[:-3], refs[-3:]
-    mid = x_ref[...] + own_ref[...]
+    mid = x_ref[rows, :] + own_ref[rows, :]
     for other in others:
-        mid = mid + other[...].astype(F32)
-    mid_ref[...] = mid
+        mid = mid + other[rows, :].astype(F32)
+    mid_ref[rows, :] = mid
     inv = lax.rsqrt(jnp.mean(mid * mid, axis=1, keepdims=True) + EPS)
     for p in range(BLOCKS):
         block = orders_ref[p]
-        normed = at_block(mid_ref, block)[...] * inv * at_block(gain_ref, block)[...]
-        at_block(xn_ref, p)[...] = normed.astype(BF)
-
-
-def norm_grad_kernel(places_ref, x_ref, base_ref, grad_ref, gain_ref, out_ref, *low_ref):
-    x = x_ref[...]
+        normed = at_block(mid_ref, rows, block)[...] * inv * at_block(gain_ref, ALL, block)[...]
+        at_block(xn_ref, rows, p)[...] = normed.astype(BF)
+
+
+def norm_grad_kernel(rows, places_ref, x_ref, base_ref, grad_ref, gain_ref, out_ref, *low_ref):
+    x = x_ref[rows, :]
     inv = lax.rsqrt(jnp.mean(x * x, axis=1, keepdims=True) + EPS)
     grad = jnp.concatenate(
-        [at_block(grad_ref, places_ref[j])[...] for j in range(BLOCKS)], 1
+        [at_block(grad_ref, rows, places_ref[j])[...] for j in range(BLOCKS)], 1
     ).astype(F32)
     normed = x * inv
     grad_hat = grad * gain_ref[...]
     mean = jnp.mean(grad_hat * normed, axis=1, keepdims=True)
-    out = base_ref[...] + inv * (grad_hat - normed * mean)
-    out_ref[...] = out
+    out = base_ref[rows, :] + inv * (grad_hat - normed * mean)
+    out_ref[rows, :] = out
     for ref in low_ref:
-        ref[...] = out.astype(BF)
-
-
-def add_placed_kernel(places_ref, base_ref, part_ref, out_ref):
+        ref[rows, :] = out.astype(BF)
+
+
+def add_placed_kernel(rows, places_ref, base_ref, part_ref, out_ref):
     for j in range(BLOCKS):
-        part = at_block(part_ref, places_ref[j])[...].astype(F32)
-        at_block(out_ref, j)[...] = at_block(base_ref, j)[...] + part
+        part = at_block(part_ref, rows, places_ref[j])[...].astype(F32)
+        at_block(out_ref, rows, j)[...] = at_block(base_ref, rows, j)[...] + part
 
 
 def on_rows(kernel, table, inputs, out_types):
@@ -449,7 +488,7 @@
         return pl.BlockSpec((block, width), lambda i, t: (i, 0))
 
     return pl.pallas_call(
-        kernel,
+        by_rows(kernel),
         grid_spec=pltpu.PrefetchScalarGridSpec(
             num_scalar_prefetch=1,
             grid=(rows // block,),
@@ -477,15 +516,16 @@
     hidden = act_ref.shape[1]
     split = 2 * hidden - cut
 
+    copies = []
+    placed(part_a, 0, cut, gate_up_ref, 0, sems, copies)
+    placed(part_b, 0, split, gate_up_ref, cut, sems, copies)
+    placed(part_b, split, hidden, down_ref, 0, sems, copies)
+
     @pl.when(pl.program_id(0) == 0)
     def _():
-        copies = []
-        placed(part_a, 0, cut, gate_up_ref, 0, sems, copies)
-        placed(part_b, 0, split, gate_up_ref, cut, sems, copies)
-        placed(part_b, split, hidden, down_ref, 0, sems, copies)
         for copy in copies:
             copy.start()
-        for copy in copies:
+        for copy in copies[: count_a + count_b]:
             copy.wait()
 
     gate_up = jnp.dot(xn_ref[...], gate_up_ref[...], preferred_element_type=F32)
@@ -493,20 +533,36 @@
     sigmoid_gate = jax.nn.sigmoid(gate)
     gated = gate * sigmoid_gate
     act_ref[...] = (gated * up_part).astype(BF)
+
+    @pl.when(pl.program_id(0) == 0)
+    def _():
+        for copy in copies[count_a + count_b :]:
+            copy.wait()
+
     grad_act = jnp.dot(dy_ref[...], down_ref[...], preferred_element_type=F32)
     grad_gate = grad_act * up_part * sigmoid_gate * (1.0 + gate * (1.0 - sigmoid_gate))
     grad_ref[:, :hidden] = grad_gate.astype(BF)
     grad_ref[:, hidden:] = (grad_act * gated).astype(BF)
-    dxn_ref[...] = contract_last(grad_ref[...], gate_up_ref[...]).astype(BF)
-
-
-OVER_X_FIRST = ((1, 2), (3,), (0,))
-OVER_Y_FIRST = ((2, 3), (1,), (0,))
-ONE_EACH = ((0,), (1,), (2,), (3,))
+    columns_last(grad_ref, gate_up_ref, dxn_ref)
+
+
+def columns_last(left_ref, right_ref, out_ref):
+    chunk = min(1024, out_ref.shape[1])
+
+    @pl.loop(0, out_ref.shape[1] // chunk)
+    def _(c):
+        at = pl.ds(pl.multiple_of(c * chunk, chunk), chunk)
+        out_ref[:, at] = contract_last(left_ref[...], right_ref[at, :]).astype(BF)
+
+
+OVER_X_FIRST = ((1, 3), (3, 4), (0, 1))
+OVER_Y_FIRST = ((2, 4), (1, 2), (0, 1))
+ONE_EACH = ((0, 1), (1, 2), (2, 3), (3, 4))
 
 
 def outer_kernel(layouts, left_ref, right_ref, *out_refs):
     step = pl.program_id(0)
+    steps = pl.num_programs(0) // 4
     turned = left_ref[...].T
     column = 0
     refs = iter(out_refs)
@@ -516,36 +572,40 @@
         right = right_ref[:, column : column + width]
         block = jnp.dot(turned, right, preferred_element_type=F32).astype(BF)
         column += width
-        for target, held in zip(targets, layout):
-
-            @pl.when((step >= held[0]) & (step <= held[-1]))
+        for target, (first, end) in zip(targets, layout):
+
+            @pl.when((step >= first * steps) & (step < end * steps))
             def _():
                 target[...] = block
 
 
-def outer_blocks(left, right, layouts):
+def outer_blocks(left, right, layouts, steps=2, side=None):
     tokens, rows = left.shape
-    width = right.shape[1] // len(layouts)
-    block = rows // 4
+    columns = right.shape[1] if side is None else right.shape[1] // 2
+    width = columns // len(layouts)
+    block = rows // (4 * steps)
     held = [blocks for layout in layouts for blocks in layout]
 
-    def spec(blocks):
+    def spec(first, end):
         return pl.BlockSpec(
-            (block, width), lambda p: (jnp.clip(p - blocks[0], 0, len(blocks) - 1), 0)
+            (block, width),
+            lambda p: (jnp.clip(p - first * steps, 0, (end - first) * steps - 1), 0),
         )
 
     outs = pl.pallas_call(
         functools.partial(outer_kernel, layouts),
-        grid=(4,),
+        grid=(4 * steps,),
         in_specs=[
             pl.BlockSpec((tokens, block), lambda p: (0, p)),
-            pl.BlockSpec(right.shape, lambda p: (0, 0)),
+            pl.BlockSpec((tokens, columns), lambda p: (0, side or 0)),
         ],
-        out_specs=[spec(blocks) for blocks in held],
-        out_shape=[jax.ShapeDtypeStruct((len(blocks) * block, width), BF) for blocks in held],
+        out_specs=[spec(*blocks) for blocks in held],
+        out_shape=[
+            jax.ShapeDtypeStruct(((end - first) * rows // 4, width), BF) for first, end in held
+        ],
         cost_estimate=pl.CostEstimate(
-            flops=2 * tokens * rows * right.shape[1],
-            bytes_accessed=2 * (tokens * (rows + right.shape[1]) + rows * right.shape[1]),
+            flops=2 * tokens * rows * columns,
+            bytes_accessed=2 * (tokens * (rows + columns) + rows * columns),
             transcendentals=0,
         ),
         name="outer_blocks",
@@ -603,7 +663,7 @@
         for copy in copies:
             copy.wait()
 
-    out_ref[...] = contract_last(act_ref[...], down_ref[...]).astype(BF)
+    columns_last(act_ref, down_ref, out_ref)
 
 
 def feed_out(act, part_b, model_width):
@@ -627,6 +687,52 @@
         ),
         name="feed_out",
     )(act, *pieces)
+
+
+def rows_by_member(pieces, places_ref, target_ref, sems):
+    height = pieces[0].shape[0]
+    copies = [
+        pltpu.make_async_copy(
+            piece,
+            target_ref.at[pl.ds(pl.multiple_of(places_ref[k] * height, height), height)],
+            sems.at[k],
+        )
+        for k, piece in enumerate(pieces)
+    ]
+    for copy in copies:
+        copy.start()
+    for copy in copies:
+        copy.wait()
+
+
+def out_rows_kernel(members_ref, features_ref, *refs):
+    pieces, (out_ref, rows_ref, sems) = refs[:4], refs[4:]
+    rows_by_member(pieces, members_ref, rows_ref, sems)
+    left = jnp.concatenate([features_ref[d] for d in range(4)], 1)
+    chunk = 512
+
+    @pl.loop(0, out_ref.shape[1] // chunk)
+    def _(c):
+        at = pl.ds(pl.multiple_of(c * chunk, chunk), chunk)
+        out_ref[:, at] = jnp.dot(left, rows_ref[:, at], preferred_element_type=F32).astype(BF)
+
+
+def out_rows_grad(features, pieces, members):
+    tokens, width = pieces[0].shape
+    count = features.shape[1]
+    return pl.pallas_call(
+        out_rows_kernel,
+        grid_spec=pltpu.PrefetchScalarGridSpec(
+            num_scalar_prefetch=1,
+            grid=(1,),
+            in_specs=[pl.BlockSpec(features.shape, lambda i, m: (0, 0, 0))]
+            + [pl.BlockSpec(memory_space=pl.ANY)] * 4,
+            out_specs=pl.BlockSpec((count, width), lambda i, m: (0, 0)),
+            scratch_shapes=[pltpu.VMEM((4 * tokens, width), BF), pltpu.SemaphoreType.DMA((4,))],
+        ),
+        out_shape=jax.ShapeDtypeStruct((count, width), BF),
+        name="out_rows",
+    )(members, features, *pieces)
 
 
 def partner(array, bits):
@@ -790,7 +896,8 @@
         half = hidden // 2
         part_a = after(jnp.concatenate([gate_piece, up_piece[:, :half]], 1), *blocks)
         part_b = after(jnp.concatenate([up_piece[:, half:], down_piece], 1), *blocks)
-        high_a, high_b = part_a[: dp_rows // 2], part_b[: dp_rows // 2]
+        high = dp_rows // 2
+        high_a, high_b = part_a[:high], part_b[:high]
         xn1, high_a, high_b = lax.optimization_barrier((xn1, high_a, high_b))
         rest_of_weights = quad.gather_late(part_a, part_b, high_a, high_b)
     else:
@@ -825,10 +932,12 @@
 
     features = to_features(attn)
     if quad:
-        features = jnp.stack(
-            [lax.dynamic_index_in_dim(features, member ^ k, 0, False) for k in range(4)]
-        )
-        parts = [contract_first(features[k], out_weight) for k in range(4)]
+        parts = [
+            contract_first(
+                lax.dynamic_index_in_dim(features, member ^ k, 0, False), out_weight
+            )
+            for k in range(4)
+        ]
         others = [partner(parts[k].astype(BF), k) for k in (1, 2, 3)]
         partials = (parts[0], *others)
     else:
@@ -859,20 +968,19 @@
     )
     feed_sum = sum_over_seq(feed_sum)
     if quad:
-        halves = outer_blocks(dy, act, (OVER_X_FIRST, OVER_Y_FIRST))
-        down_sum = PairSum(*halves)
-        halves = outer_blocks(xn2, grad_gate_up, (OVER_X_FIRST, OVER_Y_FIRST) * 2)
-        gate_sum, up_sum = PairSum(*halves[:2]), PairSum(*halves[2:])
+        sides = (OVER_X_FIRST, OVER_Y_FIRST)
+        down_sum = PairSum(*outer_blocks(dy, act, sides, 1))
+        gate_sum = PairSum(*outer_blocks(xn2, grad_gate_up, sides, 1, 0))
+        up_sum = PairSum(*outer_blocks(xn2, grad_gate_up, sides, 1, 1))
         rows_low = quad.gather_direct(hidden_low)
-        rows_low = jnp.stack(rows_low)
     else:
         down_rows = reduce_plain(dy, act)
         gate_rows = reduce_plain(xn2, grad_gate_up[:, :hidden])
         up_rows = reduce_plain(xn2, grad_gate_up[:, hidden:])
-        rows_low = lax.all_gather(hidden_low, "dp", axis=0)
+        rows_low = list(lax.all_gather(hidden_low, "dp", axis=0))
 
     grad_features = jnp.einsum(
-        "fn,ktn->kft", out_weight, rows_low, preferred_element_type=F32
+        "fn,ktn->kft", out_weight, jnp.stack(rows_low), preferred_element_type=F32
     ).astype(BF)
     if quad:
         grad_features = jnp.stack(
@@ -883,8 +991,12 @@
         down_sum.second()
         gate_sum.second()
         up_sum.second()
-    out_rows = jnp.einsum("kft,ktn->fn", features, rows_low, preferred_element_type=F32)
-    out_rows = out_rows.astype(BF)
+    if quad:
+        out_rows = out_rows_grad(features, rows_low, blocks_at ^ member)
+    else:
+        out_rows = jnp.einsum(
+            "kft,ktn->fn", features, jnp.stack(rows_low), preferred_element_type=F32
+        ).astype(BF)
     out_grad = sum_over_seq(out_rows).astype(F32)
     grad_qkv, partial_xn1 = attention_backward(
         query, key, value, attn, grad_attn, lse, cosine, sine, qkv_pieces, per_row
@@ -903,29 +1015,30 @@
         down_rows, gate_rows, up_rows = down_sum.total(), gate_sum.total(), up_sum.total()
     else:
         qkv_rows = reduce_plain(xn1, grad_qkv)
-    down_parts = exchange_rows(down_rows, group_count)
-    gate_parts = exchange_rows(gate_rows, group_count)
-    up_parts = exchange_rows(up_rows, group_count)
-    qkv_parts = exchange_rows(qkv_rows, group_count)
-    down_grad, _ = side_rows([down_parts], down_weight, group)
-    gate_up_grad, gain2_sum = side_rows([gate_parts, up_parts], gate_up_weight, group)
+    near_parts = exchange_rows(jnp.concatenate([down_rows, gate_rows], 1), group_count)
+    far_parts = exchange_rows(jnp.concatenate([up_rows, qkv_rows], 1), group_count)
+    own_at = member * dp_rows + group * shard_rows
+    own1 = lax.dynamic_slice_in_dim(gain1, own_at, shard_rows, 1)
+    own2 = lax.dynamic_slice_in_dim(gain2, own_at, shard_rows, 1)
+    down_grad, _ = side_rows([(near_parts, 0)], hidden, down_weight, own2, group)
+    gate_up_grad, norm2_grad = side_rows(
+        [(near_parts, 1), (far_parts, 0)], hidden, gate_up_weight, own2, group
+    )
     if strided:
-        qkv_grad, gain1_sum = strided_rows(qkv_parts, qkv_weight, group)
+        qkv_grad, norm1_grad = strided_rows(far_parts, hidden, qkv_weight, own1, group)
     else:
-        thirds = [qkv_parts[:, :, i * width : (i + 1) * width] for i in range(3)]
-        qkv_grad, gain1_sum = side_rows(thirds, qkv_weight, group)
-
-    def gain_grad(sums, gain):
-        own = lax.dynamic_slice_in_dim(gain, member * dp_rows + group * shard_rows, shard_rows, 0)
-        return sums[:, 0] / own
+        qkv_parts = far_parts[:, :, hidden:]
+        qkv_grad, norm1_grad = side_rows(
+            [(qkv_parts, i) for i in range(3)], width, qkv_weight, own1, group
+        )
 
     return (
         layer_out,
         input_grad,
-        gain_grad(gain1_sum, norm1_gain),
+        norm1_grad.reshape(shard_rows),
         qkv_grad,
         out_grad,
-        gain_grad(gain2_sum, norm2_gain),
+        norm2_grad.reshape(shard_rows),
         gate_up_grad,
         down_grad,
     )

time: 651 us -> 646 us (level); the launches traced: 642 us -> 644 us
  Pallas kernels: 145 us -> 164 us
  waiting for transfers between devices: 361 us -> 352 us
    pallas_call x9 -> x12, Pallas kernels: 57.2 us -> 74.2 us  [the longest x4 40 us: outer_blocks(): pl.pallas_call(functools.partial(outer_kernel, layouts), grid=(4 * steps,...]
    ppermute x35, waiting for transfers between devices: 244 us -> 230 us  [partner(): return lax.ppermute(array, 'dp', [(i, i ^ bits) for i in range(4)])]
    all_to_all x6 -> x4, starting transfers between devices: 24.5 us -> 16 us  [exchange(): return lax.all_to_all(values, axes, split_axis=0, concat_axis=0, tiled=True)]
    all_to_all x6 -> x4, waiting for transfers between devices: 56.3 us -> 61 us  [exchange(): return lax.all_to_all(values, axes, split_axis=0, concat_axis=0, tiled=True)]
  transfers between devices with their start and end apart: 48 -> 46, of which waited for: 28 -> 23; matrix products, arithmetic and copies ran while one was open for 7% -> 7% of each run, Pallas kernels for 13% -> 15%
where the time goes in v1:
time: 646 us; the launch traced here: 644 us
  waiting for transfers between devices  352 us (54%)
  Pallas kernels  164 us (25%)
  starting transfers between devices  62.3 us (10%)
  other arithmetic  28.2 us (4%)
  local copies, waits for them, and re-layouts  15.4 us (2%)
  between operations  14.5 us (2%)
  matrix products  7.81 us (1%)
    ppermute x35, waiting for transfers between devices, partner(): return lax.ppermute(array, 'dp', [(i, i ^ bits) for i in range(4)])  230 us
    all_to_all x4, waiting for transfers between devices, exchange(): return lax.all_to_all(values, axes, split_axis=0, concat_axis=0, tiled=True)  61 us
    reduce_scatter x4, waiting for transfers between devices, sum_over_seq(): lax.psum_scatter(values.astype(BF), 'seq', scatter_dimension=0, tiled=True)  48.6 us
    ppermute x35, starting transfers between devices, partner(): return lax.ppermute(array, 'dp', [(i, i ^ bits) for i in range(4)])  45.8 us
    pallas_call x4, Pallas kernels, outer_blocks(): pl.pallas_call(functools.partial(outer_kernel, layouts), grid=(4 * steps,...  40 us
    pallas_call x1, Pallas kernels, feed_forward(): pl.pallas_call(functools.partial(feed_kernel, len(part_a), len(part_b)),...  32.4 us
    pallas_call x1, Pallas kernels, attention_backward(): pl.pallas_call(functools.partial(attention_backward_kernel, block, len(pi...  20.9 us
    pallas_call x5, Pallas kernels, on_rows(): pl.pallas_call(by_rows(kernel), grid_spec=pltpu.PrefetchScalarGridSpec(nu...  20.3 us
  transfers between devices with their start and end apart: 46, of which 23 were waited for; matrix products, arithmetic and copies ran while one was open for 7% of the time, Pallas kernels for 15%

profile of v1, /device:TPU:0, one launch (start us, length us, event | category | flops | bytes accessed | tf_op | source)
XLA Modules:
  0.0 644.4 jit_solution(87909224024816118)
XLA Ops:
  7.8 3.7 shard_map.143
  11.6 2.7 strided_heads.1
  14.2 3.0 collective-permute-start.2
  19.3 2.2 constant_dynamic-slice_fusion.2
  22.9 2.3 constant_dynamic-slice_fusion.1
  25.1 11.4 %collective-permute-done.refs_2_ = bf16[512,384]{1,0:T(8,128)(2,1)} collective-permute-done((bf16[512,384]{1,0:T(8,128)(2,1)}, bf16[512,384]{1,0:T(8,128)(2,1)}, u32[]{:S(2)}, u32[]{:S(2)}) %collective-permute-start) | collective-permute-done | bytes 393248 | tf_op jit(solution)/shard_map/ppermute | solution.py:739
  36.9 1.7 collective-permute-start.3
  39.1 4.4 rotary.1
  43.5 1.8 pad_maximum_fusion.2
  49.0 12.3 %all-gather.4.cloned.1.call-done.xn_ref.left_ref = bf16[1024,2048]{1,0:T(8,128)(2,1)} async-done(((bf16[128,2048]{1,0:T(8,128)(2,1)}), bf16[1024,2048]{1,0:T(8,128)(2,1)}) %all-gather.4.cloned.1.call-update) | async-done | bytes 4194320 | tf_op jit(solution)/shard_map/all_gather | solution.py:817
  61.3 16.0 %attention_forward.1 = (bf16[4,8,64,128]{3,2,1,0:T(8,128)(2,1)}, bf16[1024,256]{1,0:T(8,128)(2,1)}, bf16[1024,256]{1,0:T(8,128)(2,1)}, bf16[1024,256]{1,0:T(8,128)(2,1)}, f32[8,1024]{1,0:T(8,128)}) custom-call(bf16[1024,2048]{1,0:T(8,128)(2,1)} %all-gather.4.cloned.1.call-done.xn_ref.left_ref, bf16[512,384]{1,0:T(8,128)(2,1)} %get-tuple-element.69.refs_0_, ...), custom_call_target="tpu_custom_call" | custom-call | flops 3758096384 | bytes 9437184 | tf_op jit(solution)/shard_map/attention_forward/pallas_call | solution.py:218
  77.3 3.4 all-to-all-start
  80.8 25.0 %all-to-all-done = bf16[32,64,128]{2,1,0:T(8,128)(2,1)S(1)} async-done(((bf16[32,64,128]{2,1,0:T(8,128)(2,1)}), bf16[32,64,128]{2,1,0:T(8,128)(2,1)S(1)}, u32[]{:S(2)}, u32[]{:S(2)}) %all-to-all-start) | async-done | bytes 524320 | tf_op jit(solution)/shard_map/all_to_all | solution.py:825
  110.7 2.4 collective-permute-start.8
  114.5 6.6 %collective-permute-done.6.refs_1_ = bf16[128,2048]{1,0:T(8,128)(2,1)} collective-permute-done((bf16[128,2048]{1,0:T(8,128)(2,1)}, bf16[128,2048]{1,0:T(8,128)(2,1)}, u32[]{:S(2)}, u32[]{:S(2)}) %collective-permute-start.6) | collective-permute-done | bytes 524320 | tf_op jit(solution)/shard_map/ppermute | solution.py:739
  122.3 9.1 %collective-permute-done.8.refs_3_ = bf16[128,2048]{1,0:T(8,128)(2,1)} collective-permute-done((bf16[128,2048]{1,0:T(8,128)(2,1)}, bf16[128,2048]{1,0:T(8,128)(2,1)}, u32[]{:S(2)}, u32[]{:S(2)}) %collective-permute-start.8) | collective-permute-done | bytes 524320 | tf_op jit(solution)/shard_map/ppermute | solution.py:739
  131.4 4.6 shard_map.144
  136.1 2.6 collective-permute-start.15
  138.6 2.1 collective-permute-start.9
  140.7 1.9 collective-permute-start.11
  142.7 30.3 %collective-permute-done.15.refs_9_.refs_4_ = bf16[512,1536]{1,0:T(8,128)(2,1)S(1)} collective-permute-done((bf16[512,1536]{1,0:T(8,128)(2,1)}, bf16[512,1536]{1,0:T(8,128)(2,1)S(1)}, u32[]{:S(2)}, u32[]{:S(2)}) %collective-permute-start.15) | collective-permute-done | bytes 1572896 | tf_op jit(solution)/shard_map/ppermute | solution.py:739
  173.0 5.1 collective-permute-start.16
  180.2 9.6 %collective-permute-done.11.refs_3_ = bf16[256,1536]{1,0:T(8,128)(2,1)S(1)} collective-permute-done((bf16[256,1536]{1,0:T(8,128)(2,1)}, bf16[256,1536]{1,0:T(8,128)(2,1)S(1)}, u32[]{:S(2)}, u32[]{:S(2)}) %collective-permute-start.11) | collective-permute-done | bytes 786464 | tf_op jit(solution)/shard_map/ppermute | solution.py:739
  189.8 2.4 collective-permute-start.12
  192.2 38.0 %collective-permute-done.13.refs_6_.refs_1_ = bf16[256,1536]{1,0:T(8,128)(2,1)S(1)} collective-permute-done((bf16[256,1536]{1,0:T(8,128)(2,1)}, bf16[256,1536]{1,0:T(8,128)(2,1)S(1)}, u32[]{:S(2)}, u32[]{:S(2)}) %collective-permute-start.13) | collective-permute-done | bytes 786464 | tf_op jit(solution)/shard_map/ppermute | solution.py:739
  230.2 15.7 %collective-permute-done.14.refs_7_.refs_2_ = bf16[256,1536]{1,0:T(8,128)(2,1)S(1)} collective-permute-done((bf16[256,1536]{1,0:T(8,128)(2,1)}, bf16[256,1536]{1,0:T(8,128)(2,1)S(1)}, u32[]{:S(2)}, u32[]{:S(2)}) %collective-permute-start.14) | collective-permute-done | bytes 786464 | tf_op jit(solution)/shard_map/ppermute | solution.py:739
  248.2 32.4 %feed_forward.1 = (bf16[1024,1024]{1,0:T(8,128)(2,1)}, bf16[1024,2048]{1,0:T(8,128)(2,1)}, bf16[1024,2048]{1,0:T(8,128)(2,1)}) custom-call(bf16[1024,2048]{1,0:T(8,128)(2,1)} %all-gather.6.cloned.1.call-done.xn_ref.left_ref, bf16[1024,2048]{1,0:T(8,128)(2,1)} %all-gather.8.cloned.1.call-done.dy_ref.left_ref, bf16[512,1536]{1,0:T(8,128)(2,1)} %copy-done.2, ...), custom_call_target="tpu_custom_call" | custom-call | flops 21474836480 | bytes 29360128 | tf_op jit(solution)/shard_map/feed_forward/pallas_call | solution.py:629
  281.4 48.6 %reduce-scatter.5.cloned.1.call-done.refs_1_ = bf16[128,2048]{1,0:T(8,128)(2,1)} async-done(((bf16[1024,2048]{1,0:T(8,128)(2,1)}), bf16[128,2048]{1,0:T(8,128)(2,1)}) %reduce-scatter.5.cloned.1.call-update) | async-done | bytes 524304 | tf_op jit(solution)/shard_map/reduce_scatter | solution.py:821
  330.0 4.6 shard_map.145
  338.7 11.0 %collective-permute-done.17.refs_1_ = bf16[128,2048]{1,0:T(8,128)(2,1)S(1)} collective-permute-done((bf16[128,2048]{1,0:T(8,128)(2,1)}, bf16[128,2048]{1,0:T(8,128)(2,1)S(1)}, u32[]{:S(2)}, u32[]{:S(2)}) %collective-permute-start.17) | collective-permute-done | bytes 524320 | tf_op jit(solution)/shard_map/ppermute | solution.py:739
  349.7 9.4 %collective-permute-done.18.refs_2_ = bf16[128,2048]{1,0:T(8,128)(2,1)S(1)} collective-permute-done((bf16[128,2048]{1,0:T(8,128)(2,1)}, bf16[128,2048]{1,0:T(8,128)(2,1)S(1)}, u32[]{:S(2)}, u32[]{:S(2)}) %collective-permute-start.18) | collective-permute-done | bytes 524320 | tf_op jit(solution)/shard_map/ppermute | solution.py:739
  359.9 6.4 out_rows.1
  366.3 10.4 %feed_out.1 = bf16[1024,2048]{1,0:T(8,128)(2,1)} custom-call(bf16[1024,1024]{1,0:T(8,128)(2,1)} %get-tuple-element.89.act_ref.right_ref, bf16[512,1536]{1,0:T(8,128)(2,1)} %copy-done.1, bf16[256,1536]{1,0:T(8,128)(2,1)} %copy-done.17, bf16[256,1536]{1,0:T(8,128)(2,1)} %copy-done.18, bf16[512,1536]{1,0:T(8,128)(2,1)} %copy-done.15, bf16[512,1536]{1,0:T(8,128)(2,1)} %copy-done.14), custom_call_target="tpu_custom_call" | custom-call | flops 4294967296 | bytes 10485760 | tf_op jit(solution)/shard_map/feed_out/pallas_call | solution.py:673
  376.7 10.0 %outer_blocks.6 = (bf16[1024,512]{1,0:T(8,128)(2,1)}, bf16[512,512]{1,0:T(8,128)(2,1)}, bf16[512,512]{1,0:T(8,128)(2,1)}, bf16[1024,512]{1,0:T(8,128)(2,1)}, bf1...) custom-call(bf16[1024,2048]{1,0:T(8,128)(2,1)} %all-gather.8.cloned.1.call-done.dy_ref.left_ref, ...), custom_call_target="tpu_custom_call" | custom-call | flops 4294967296 | bytes 10485760 | tf_op jit(solution)/shard_map/outer_blocks/pallas_call | solution.py:595
  388.8 10.1 %outer_blocks.7 = (bf16[1024,512]{1,0:T(8,128)(2,1)}, bf16[512,512]{1,0:T(8,128)(2,1)}, bf16[512,512]{1,0:T(8,128)(2,1)}, bf16[1024,512]{1,0:T(8,128)(2,1)}, bf1...) custom-call(bf16[1024,2048]{1,0:T(8,128)(2,1)} %all-gather.6.cloned.1.call-done.xn_ref.left_ref, ...), custom_call_target="tpu_custom_call" | custom-call | flops 4294967296 | bytes 10485760 | tf_op jit(solution)/shard_map/outer_blocks/pallas_call | solution.py:595
  400.4 2.5 fusion.9
  404.0 3.3 all-to-all-start.1
  407.4 1.7 collective-permute-start.33
  409.1 5.2 collective-permute-done.27
  414.3 2.1 add_convert_fusion.8
  417.9 2.1 add_convert_fusion.6
  420.6 19.2 %collective-permute-done.31 = bf16[1024,512]{1,0:T(8,128)(2,1)} collective-permute-done((bf16[1024,512]{1,0:T(8,128)(2,1)}, bf16[1024,512]{1,0:T(8,128)(2,1)}, u32[]{:S(2)}, u32[]{:S(2)}) %collective-permute-start.31) | collective-permute-done | bytes 1048608 | tf_op jit(solution)/shard_map/ppermute | solution.py:739
  439.8 2.1 add_convert_fusion.4
  443.4 20.9 %attention_backward.1 = (bf16[1024,768]{1,0:T(8,128)(2,1)}, bf16[1024,2048]{1,0:T(8,128)(2,1)}) custom-call(bf16[1024,256]{1,0:T(8,128)(2,1)} %get-tuple-element.91.q_ref, bf16[1024,256]{1,0:T(8,128)(2,1)} %get-tuple-element.92.k_ref, bf16[1024,256]{1,0:T(8,128)(2,1)} %get-tuple-element.93.v_ref, bf16[4,8,64,128]{3,2,1,0:T(8,128)(2,1)} %get-tuple-element.76.attn_ref, ...), custom_call_target="tpu_custom_call" | custom-call | flops 4563402752 | bytes 12582912 | tf_op jit(solution)/shard_map/attention_backward/pallas_call | solution.py:249
  466.2 1.6 add_convert_fusion.7
  470.9 6.7 %collective-permute-done.34 = bf16[512,512]{1,0:T(8,128)(2,1)S(1)} collective-permute-done((bf16[512,512]{1,0:T(8,128)(2,1)S(1)}, bf16[512,512]{1,0:T(8,128)(2,1)S(1)}, u32[]{:S(2)}, u32[]{:S(2)}) %collective-permute-start.34) | collective-permute-done | bytes 524320 | tf_op jit(solution)/shard_map/ppermute | solution.py:739
  477.8 1.6 pad_maximum_fusion
  479.4 4.6 all-to-all-start.3
  484.0 10.1 %outer_blocks.4 = (bf16[1024,512]{1,0:T(8,128)(2,1)}, bf16[512,512]{1,0:T(8,128)(2,1)}, bf16[512,512]{1,0:T(8,128)(2,1)}, bf16[1024,512]{1,0:T(8,128)(2,1)}, bf1...) custom-call(bf16[1024,2048]{1,0:T(8,128)(2,1)} %all-gather.6.cloned.1.call-done.xn_ref.left_ref, ...), custom_call_target="tpu_custom_call" | custom-call | flops 4294967296 | bytes 10485760 | tf_op jit(solution)/shard_map/outer_blocks/pallas_call | solution.py:595
  495.5 24.0 %collective-permute-done.20 = bf16[1024,512]{1,0:T(8,128)(2,1)S(1)} collective-permute-done((bf16[1024,512]{1,0:T(8,128)(2,1)}, bf16[1024,512]{1,0:T(8,128)(2,1)S(1)}, u32[]{:S(2)}, u32[]{:S(2)}) %collective-permute-start.20) | collective-permute-done | bytes 1048608 | tf_op jit(solution)/shard_map/ppermute | solution.py:739
  519.5 2.3 add_convert_fusion.12
  522.8 2.0 add_convert_fusion.10
  525.2 9.7 %outer_blocks.5 = (bf16[512,768]{1,0:T(8,128)(2,1)}, bf16[512,768]{1,0:T(8,128)(2,1)}, bf16[512,768]{1,0:T(8,128)(2,1)}, bf16[512,768]{1,0:T(8,128)(2,1)}) custom-call(bf16[1024,2048]{1,0:T(8,128)(2,1)} %all-gather.4.cloned.1.call-done.xn_ref.left_ref, bf16[1024,768]{1,0:T(8,128)(2,1)} %get-tuple-element.106.right_ref), custom_call_target="tpu_custom_call" | custom-call | flops 3221225472 | bytes 8912896 | tf_op jit(solution)/shard_map/outer_blocks/pallas_call | solution.py:595
  538.5 1.6 add_convert_fusion.11
  541.4 14.7 %collective-permute-done.24 = bf16[512,768]{1,0:T(8,128)(2,1)S(1)} collective-permute-done((bf16[512,768]{1,0:T(8,128)(2,1)}, bf16[512,768]{1,0:T(8,128)(2,1)S(1)}, u32[]{:S(2)}, u32[]{:S(2)}) %collective-permute-start.24) | collective-permute-done | bytes 786464 | tf_op jit(solution)/shard_map/ppermute | solution.py:739
  556.1 16.1 %collective-permute-done.25 = bf16[512,768]{1,0:T(8,128)(2,1)S(1)} collective-permute-done((bf16[512,768]{1,0:T(8,128)(2,1)}, bf16[512,768]{1,0:T(8,128)(2,1)S(1)}, u32[]{:S(2)}, u32[]{:S(2)}) %collective-permute-start.25) | collective-permute-done | bytes 786464 | tf_op jit(solution)/shard_map/ppermute | solution.py:739
  574.5 4.7 all-to-all-start.2
  581.7 3.2 side_rows.3
  584.9 1.8 convert_element_type.188
  586.7 36.0 %all-to-all-done.2.in_ref.refs_1_ = bf16[8,64,1792]{2,1,0:T(8,128)(2,1)} async-done(((bf16[8,64,1792]{2,1,0:T(8,128)(2,1)}), bf16[8,64,1792]{2,1,0:T(8,128)(2,1)}, u32[]{:S(2)}, u32[]{:S(2)}) %all-to-all-start.2) | async-done | bytes 1835040 | tf_op jit(solution)/shard_map/all_to_all | solution.py:825
  622.7 4.3 side_rows.2
  627.0 3.2 strided_rows.1
  630.2 3.1 shard_map.146
  633.3 4.3 shard_map.147
  (136 shorter events, 52.0 us)
Async XLA Ops:
  7.2 98.6 %copy-start = (bf16[512,2048]{1,0:T(8,128)(2,1)S(1)}, bf16[512,2048]{1,0:T(8,128)(2,1)}, u32[]{:S(2)}) copy-start(bf16[512,2048]{1,0:T(8,128)(2,1)} %param.11) | copy-start | bytes 6291460
  7.2 54.1 %all-gather.4.cloned.1.call-start = ((), (), s32[]{:S(2)}) async-start(), calls=%async_computation.8 | async-start | bytes 4718592 | tf_op jit(solution)/shard_map/all_gather | solution.py:817
  11.5 236.7 %all-gather.8.cloned.1.call-start = ((), (), s32[]{:S(2)}) async-start(), calls=%async_computation.10 | async-start | bytes 4718592 | tf_op jit(solution)/shard_map/all_gather | solution.py:817
  14.2 22.6 %collective-permute-start.2 = (bf16[512,384]{1,0:T(8,128)(2,1)}, bf16[512,384]{1,0:T(8,128)(2,1)S(1)}, u32[]{:S(2)}, u32[]{:S(2)}) collective-permute-start(bf16[512,384]{1,0:T(8,128)(2,1)} %get-tuple-element.70.refs_1_), channel_id=1, source_target_pairs={{0,16},{8,24},{16,0},{24,8},{1,17},{9,25},{17,1},{25,9},{2,18},{10... | collective-permute-start | bytes 1179656 | tf_op jit(solution)/shard_map/ppermute | solution.py:739
  17.2 44.0 %collective-permute-start.4 = (bf16[512,384]{1,0:T(8,128)(2,1)}, bf16[512,384]{1,0:T(8,128)(2,1)}, u32[]{:S(2)}, u32[]{:S(2)}) collective-permute-start(bf16[512,384]{1,0:T(8,128)(2,1)} %get-tuple-element.70.refs_1_), channel_id=1, source_target_pairs={{0,8},{8,0},{16,24},{24,16},{1,9},{9,1},{17,25},{25,17},{2,10},{10... | collective-permute-start | bytes 1179656 | tf_op jit(solution)/shard_map/ppermute | solution.py:739
  18.7 17.8 %collective-permute-start = (bf16[512,384]{1,0:T(8,128)(2,1)}, bf16[512,384]{1,0:T(8,128)(2,1)}, u32[]{:S(2)}, u32[]{:S(2)}) collective-permute-start(bf16[512,384]{1,0:T(8,128)(2,1)} %get-tuple-element.69.refs_0_), channel_id=1, source_target_pairs={{0,8},{8,0},{16,24},{24,16},{1,9},{9,1},{17,25},{25,17},{2,10},{10... | collective-permute-start | bytes 1179656 | tf_op jit(solution)/shard_map/ppermute | solution.py:739
  19.2 42.0 %collective-permute-start.5 = (bf16[512,384]{1,0:T(8,128)(2,1)}, bf16[512,384]{1,0:T(8,128)(2,1)}, u32[]{:S(2)}, u32[]{:S(2)}) collective-permute-start(bf16[512,384]{1,0:T(8,128)(2,1)} %get-tuple-element.69.refs_0_), channel_id=1, source_target_pairs={{0,16},{8,24},{16,0},{24,8},{1,17},{9,25},{17,1},{25,9},{2,18},{10... | collective-permute-start | bytes 1179656 | tf_op jit(solution)/shard_map/ppermute | solution.py:739
  36.5 10.0 %collective-permute-start.1 = (bf16[512,384]{1,0:T(8,128)(2,1)}, bf16[512,384]{1,0:T(8,128)(2,1)}, u32[]{:S(2)}, u32[]{:S(2)}) collective-permute-start(bf16[512,384]{1,0:T(8,128)(2,1)} %collective-permute-done.refs_2_), channel_id=1, source_target_pairs={{0,16},{8,24},{16,0},{24,8},{1,17},{9,25},{17,1},{25,9},{2,18},{10... | collective-permute-start | bytes 1179656 | tf_op jit(solution)/shard_map/ppermute | solution.py:739
  36.9 8.5 %copy-start.21 = (bf16[512,384]{1,0:T(8,128)(2,1)}, bf16[512,384]{1,0:T(8,128)(2,1)S(1)}, u32[]{:S(2)}) copy-start(bf16[512,384]{1,0:T(8,128)(2,1)S(1)} %collective-permute-done.2.refs_7_) | copy-start | bytes 1179652
  36.9 9.8 %collective-permute-start.3 = (bf16[512,384]{1,0:T(8,128)(2,1)S(1)}, bf16[512,384]{1,0:T(8,128)(2,1)}, u32[]{:S(2)}, u32[]{:S(2)}) collective-permute-start(bf16[512,384]{1,0:T(8,128)(2,1)S(1)} %collective-permute-done.2.refs_7_), channel_id=1, source_target_pairs={{0,8},{8,0},{16,24},{24,16},{1,9},{9,1},{17,25},{25,17},{2,10},{10... | collective-permute-start | bytes 1179656 | tf_op jit(solution)/shard_map/ppermute | solution.py:739
  45.3 1.3 copy-start.1
  45.4 2.6 copy-start.2
  77.3 28.5 %all-to-all-start = ((bf16[32,64,128]{2,1,0:T(8,128)(2,1)}), bf16[32,64,128]{2,1,0:T(8,128)(2,1)S(1)}, u32[]{:S(2)}, u32[]{:S(2)}) async-start(bf16[32,64,128]{2,1,0:T(8,128)(2,1)} %bitcast.58), calls=%async_computation | async-start | bytes 1048576 | tf_op jit(solution)/shard_map/all_to_all | solution.py:825
  80.7 167.5 %all-gather.6.cloned.1.call-start = ((), (), s32[]{:S(2)}) async-start(), calls=%async_computation.9 | async-start | bytes 4718592 | tf_op jit(solution)/shard_map/all_gather | solution.py:817
  105.7 7.4 %copy-start.3 = (bf16[32,64,128]{2,1,0:T(8,128)(2,1)}, bf16[32,64,128]{2,1,0:T(8,128)(2,1)S(1)}, u32[]{:S(2)}) copy-start(bf16[32,64,128]{2,1,0:T(8,128)(2,1)S(1)} %all-to-all-done) | copy-start | bytes 1572868
  107.0 14.1 %collective-permute-start.6 = (bf16[128,2048]{1,0:T(8,128)(2,1)}, bf16[128,2048]{1,0:T(8,128)(2,1)}, u32[]{:S(2)}, u32[]{:S(2)}) collective-permute-start(bf16[128,2048]{1,0:T(8,128)(2,1)} %convolution_convert_fusion.2), channel_id=1, source_target_pairs={{0,8},{8,0},{16,24},{24,16},{1,9},{9,1},{17,25},{25,17},{2,10},{10... | collective-permute-start | bytes 1572872 | tf_op jit(solution)/shard_map/ppermute | solution.py:739
  108.3 14.0 %collective-permute-start.7 = (bf16[128,2048]{1,0:T(8,128)(2,1)}, bf16[128,2048]{1,0:T(8,128)(2,1)}, u32[]{:S(2)}, u32[]{:S(2)}) collective-permute-start(bf16[128,2048]{1,0:T(8,128)(2,1)} %convolution_convert_fusion.1), channel_id=1, source_target_pairs={{0,16},{8,24},{16,0},{24,8},{1,17},{9,25},{17,1},{25,9},{2,18},{10... | collective-permute-start | bytes 1572872 | tf_op jit(solution)/shard_map/ppermute | solution.py:739
  110.7 20.7 %collective-permute-start.8 = (bf16[128,2048]{1,0:T(8,128)(2,1)}, bf16[128,2048]{1,0:T(8,128)(2,1)}, u32[]{:S(2)}, u32[]{:S(2)}) collective-permute-start(bf16[128,2048]{1,0:T(8,128)(2,1)} %convolution_convert_fusion), channel_id=1, source_target_pairs={{0,24},{8,16},{16,8},{24,0},{1,25},{9,17},{17,9},{25,1},{2,26},{10... | collective-permute-start | bytes 1572872 | tf_op jit(solution)/shard_map/ppermute | solution.py:739
  136.0 194.0 %reduce-scatter.5.cloned.1.call-start = ((), (), s32[]{:S(2)}) async-start(), calls=%async_computation.11 | async-start | bytes 4718592 | tf_op jit(solution)/shard_map/reduce_scatter | solution.py:821
  136.1 36.9 %collective-permute-start.15 = (bf16[512,1536]{1,0:T(8,128)(2,1)}, bf16[512,1536]{1,0:T(8,128)(2,1)S(1)}, u32[]{:S(2)}, u32[]{:S(2)}) collective-permute-start(bf16[512,1536]{1,0:T(8,128)(2,1)} %copy-done.1), channel_id=1, source_target_pairs={{0,16},{8,24},{16,0},{24,8},{1,17},{9,25},{17,1},{25,9},{2,18},{10... | collective-permute-start | bytes 4718600 | tf_op jit(solution)/shard_map/ppermute | solution.py:739
  138.6 39.5 %collective-permute-start.9 = (bf16[512,1536]{1,0:T(8,128)(2,1)}, bf16[512,1536]{1,0:T(8,128)(2,1)S(1)}, u32[]{:S(2)}, u32[]{:S(2)}) collective-permute-start(bf16[512,1536]{1,0:T(8,128)(2,1)} %copy-done.2), channel_id=1, source_target_pairs={{0,8},{8,0},{16,24},{24,16},{1,9},{9,1},{17,25},{25,17},{2,10},{10... | collective-permute-start | bytes 4718600 | tf_op jit(solution)/shard_map/ppermute | solution.py:739
  140.7 49.1 %collective-permute-start.11 = (bf16[256,1536]{1,0:T(8,128)(2,1)}, bf16[256,1536]{1,0:T(8,128)(2,1)S(1)}, u32[]{:S(2)}, u32[]{:S(2)}) collective-permute-start(bf16[256,1536]{1,0:T(8,128)(2,1)} %get-tuple-element.82), channel_id=1, source_target_pairs={{0,16},{8,24},{16,0},{24,8},{1,17},{9,25},{17,1},{25,9},{2,18},{10... | collective-permute-start | bytes 2359304 | tf_op jit(solution)/shard_map/ppermute | solution.py:739
  173.0 72.9 %copy-start.14 = (bf16[512,1536]{1,0:T(8,128)(2,1)}, bf16[512,1536]{1,0:T(8,128)(2,1)S(1)}, u32[]{:S(2)}) copy-start(bf16[512,1536]{1,0:T(8,128)(2,1)S(1)} %collective-permute-done.15.refs_9_.refs_4_) | copy-start | bytes 4718596
  173.0 73.0 %collective-permute-start.16 = (bf16[512,1536]{1,0:T(8,128)(2,1)S(1)}, bf16[512,1536]{1,0:T(8,128)(2,1)S(1)}, u32[]{:S(2)}, u32[]{:S(2)}) collective-permute-start(bf16[512,1536]{1,0:T(8,128)(2,1)S(1)} %collective-permute-done.15.refs_9_.refs_4_), channel_id=1, source_target_pairs={{0,8},{8,0},{16,24},{24,16},{1,9},{9,1},{17,25},{25,17},{2,10},{10... | collective-permute-start | bytes 4718600 | tf_op jit(solution)/shard_map/ppermute | solution.py:739
  178.1 67.8 %copy-start.16 = (bf16[512,1536]{1,0:T(8,128)(2,1)}, bf16[512,1536]{1,0:T(8,128)(2,1)S(1)}, u32[]{:S(2)}) copy-start(bf16[512,1536]{1,0:T(8,128)(2,1)S(1)} %collective-permute-done.9.refs_1_) | copy-start | bytes 4718596
  178.1 70.1 %collective-permute-start.10 = (bf16[512,1536]{1,0:T(8,128)(2,1)S(1)}, bf16[512,1536]{1,0:T(8,128)(2,1)}, u32[]{:S(2)}, u32[]{:S(2)}) collective-permute-start(bf16[512,1536]{1,0:T(8,128)(2,1)S(1)} %collective-permute-done.9.refs_1_), channel_id=1, source_target_pairs={{0,16},{8,24},{16,0},{24,8},{1,17},{9,25},{17,1},{25,9},{2,18},{10... | collective-permute-start | bytes 4718600 | tf_op jit(solution)/shard_map/ppermute | solution.py:739
  178.1 52.1 %collective-permute-start.13 = (bf16[256,1536]{1,0:T(8,128)(2,1)}, bf16[256,1536]{1,0:T(8,128)(2,1)S(1)}, u32[]{:S(2)}, u32[]{:S(2)}) collective-permute-start(bf16[256,1536]{1,0:T(8,128)(2,1)} %get-tuple-element.84), channel_id=1, source_target_pairs={{0,8},{8,0},{16,24},{24,16},{1,9},{9,1},{17,25},{25,17},{2,10},{10... | collective-permute-start | bytes 2359304 | tf_op jit(solution)/shard_map/ppermute | solution.py:739
  179.5 66.5 %collective-permute-start.14 = (bf16[256,1536]{1,0:T(8,128)(2,1)}, bf16[256,1536]{1,0:T(8,128)(2,1)S(1)}, u32[]{:S(2)}, u32[]{:S(2)}) collective-permute-start(bf16[256,1536]{1,0:T(8,128)(2,1)} %get-tuple-element.85), channel_id=1, source_target_pairs={{0,8},{8,0},{16,24},{24,16},{1,9},{9,1},{17,25},{25,17},{2,10},{10... | collective-permute-start | bytes 2359304 | tf_op jit(solution)/shard_map/ppermute | solution.py:739
  189.8 56.1 %copy-start.19 = (bf16[256,1536]{1,0:T(8,128)(2,1)}, bf16[256,1536]{1,0:T(8,128)(2,1)S(1)}, u32[]{:S(2)}) copy-start(bf16[256,1536]{1,0:T(8,128)(2,1)S(1)} %collective-permute-done.11.refs_3_) | copy-start | bytes 2359300
  189.8 56.1 %collective-permute-start.12 = (bf16[256,1536]{1,0:T(8,128)(2,1)S(1)}, bf16[256,1536]{1,0:T(8,128)(2,1)S(1)}, u32[]{:S(2)}, u32[]{:S(2)}) collective-permute-start(bf16[256,1536]{1,0:T(8,128)(2,1)S(1)} %get-tuple-element.83), channel_id=1, source_target_pairs={{0,16},{8,24},{16,0},{24,8},{1,17},{9,25},{17,1},{25,9},{2,18},{10... | collective-permute-start | bytes 2359304 | tf_op jit(solution)/shard_map/ppermute | solution.py:739
  230.2 15.8 %copy-start.17 = (bf16[256,1536]{1,0:T(8,128)(2,1)}, bf16[256,1536]{1,0:T(8,128)(2,1)S(1)}, u32[]{:S(2)}) copy-start(bf16[256,1536]{1,0:T(8,128)(2,1)S(1)} %collective-permute-done.13.refs_6_.refs_1_) | copy-start | bytes 2359300
  280.6 304.3 %reduce-scatter.11.cloned.1.call-start = ((), (), s32[]{:S(2)}) async-start(), calls=%async_computation.14 | async-start | bytes 2359296 | tf_op jit(solution)/shard_map/reduce_scatter | solution.py:821
  334.7 15.0 %collective-permute-start.17 = (bf16[128,2048]{1,0:T(8,128)(2,1)}, bf16[128,2048]{1,0:T(8,128)(2,1)S(1)}, u32[]{:S(2)}, u32[]{:S(2)}) collective-permute-start(bf16[128,2048]{1,0:T(8,128)(2,1)} %get-tuple-element.94.refs_0_), channel_id=1, source_target_pairs={{0,8},{8,0},{16,24},{24,16},{1,9},{9,1},{17,25},{25,17},{2,10},{10... | collective-permute-start | bytes 1572872 | tf_op jit(solution)/shard_map/ppermute | solution.py:739
  336.1 22.9 %collective-permute-start.18 = (bf16[128,2048]{1,0:T(8,128)(2,1)}, bf16[128,2048]{1,0:T(8,128)(2,1)S(1)}, u32[]{:S(2)}, u32[]{:S(2)}) collective-permute-start(bf16[128,2048]{1,0:T(8,128)(2,1)} %get-tuple-element.94.refs_0_), channel_id=1, source_target_pairs={{0,16},{8,24},{16,0},{24,8},{1,17},{9,25},{17,1},{25,9},{2,18},{10... | collective-permute-start | bytes 1572872 | tf_op jit(solution)/shard_map/ppermute | solution.py:739
  337.6 21.5 %collective-permute-start.19 = (bf16[128,2048]{1,0:T(8,128)(2,1)}, bf16[128,2048]{1,0:T(8,128)(2,1)}, u32[]{:S(2)}, u32[]{:S(2)}) collective-permute-start(bf16[128,2048]{1,0:T(8,128)(2,1)} %get-tuple-element.94.refs_0_), channel_id=1, source_target_pairs={{0,24},{8,16},{16,8},{24,0},{1,25},{9,17},{17,9},{25,1},{2,26},{10... | collective-permute-start | bytes 1572872 | tf_op jit(solution)/shard_map/ppermute | solution.py:739
  349.7 9.4 %copy-start.7 = (bf16[128,2048]{1,0:T(8,128)(2,1)}, bf16[128,2048]{1,0:T(8,128)(2,1)S(1)}, u32[]{:S(2)}) copy-start(bf16[128,2048]{1,0:T(8,128)(2,1)S(1)} %collective-permute-done.17.refs_1_) | copy-start | bytes 1572868
  366.3 263.9 %reduce-scatter.7.cloned.1.call-start = ((), (), s32[]{:S(2)}) async-start(), calls=%async_computation.12 | async-start | bytes 4718592 | tf_op jit(solution)/shard_map/reduce_scatter | solution.py:821
  386.8 27.5 %collective-permute-start.27 = (bf16[1024,512]{1,0:T(8,128)(2,1)}, bf16[1024,512]{1,0:T(8,128)(2,1)}, u32[]{:S(2)}, u32[]{:S(2)}) collective-permute-start(bf16[1024,512]{1,0:T(8,128)(2,1)} %get-tuple-element.114), channel_id=1, source_target_pairs={{0,8},{8,0},{16,24},{24,16},{1,9},{9,1},{17,25},{25,17},{2,10},{10... | collective-permute-start | bytes 3145736 | tf_op jit(solution)/shard_map/ppermute | solution.py:739
  387.3 30.7 %collective-permute-start.29 = (bf16[1024,512]{1,0:T(8,128)(2,1)}, bf16[1024,512]{1,0:T(8,128)(2,1)}, u32[]{:S(2)}, u32[]{:S(2)}) collective-permute-start(bf16[1024,512]{1,0:T(8,128)(2,1)} %get-tuple-element.117), channel_id=1, source_target_pairs={{0,16},{8,24},{16,0},{24,8},{1,17},{9,25},{17,1},{25,9},{2,18},{10... | collective-permute-start | bytes 3145736 | tf_op jit(solution)/shard_map/ppermute | solution.py:739
  388.8 11.6 %copy-start.6 = (bf16[128,2048]{1,0:T(8,128)(2,1)S(1)}, bf16[128,2048]{1,0:T(8,128)(2,1)}, u32[]{:S(2)}) copy-start(bf16[128,2048]{1,0:T(8,128)(2,1)} %get-tuple-element.94.refs_0_) | copy-start | bytes 1572868
  388.8 11.6 %copy-start.8 = (bf16[128,2048]{1,0:T(8,128)(2,1)S(1)}, bf16[128,2048]{1,0:T(8,128)(2,1)}, u32[]{:S(2)}) copy-start(bf16[128,2048]{1,0:T(8,128)(2,1)} %copy-done.7) | copy-start | bytes 1572868
  398.9 40.9 %collective-permute-start.31 = (bf16[1024,512]{1,0:T(8,128)(2,1)}, bf16[1024,512]{1,0:T(8,128)(2,1)}, u32[]{:S(2)}, u32[]{:S(2)}) collective-permute-start(bf16[1024,512]{1,0:T(8,128)(2,1)} %get-tuple-element.120), channel_id=1, source_target_pairs={{0,8},{8,0},{16,24},{24,16},{1,9},{9,1},{17,25},{25,17},{2,10},{10... | collective-permute-start | bytes 3145736 | tf_op jit(solution)/shard_map/ppermute | solution.py:739
  404.0 39.4 %all-to-all-start.1 = ((bf16[32,64,128]{2,1,0:T(8,128)(2,1)}), bf16[32,64,128]{2,1,0:T(8,128)(2,1)}, u32[]{:S(2)}, u32[]{:S(2)}) async-start(bf16[32,64,128]{2,1,0:T(8,128)(2,1)} %bitcast.18), calls=%async_computation.3 | async-start | bytes 1048576 | tf_op jit(solution)/shard_map/all_to_all | solution.py:825
  407.4 225.9 %reduce-scatter.9.cloned.1.call-start = ((), (), s32[]{:S(2)}) async-start(), calls=%async_computation.13 | async-start | bytes 4718592 | tf_op jit(solution)/shard_map/reduce_scatter | solution.py:821
  407.4 56.9 %collective-permute-start.33 = (bf16[1024,512]{1,0:T(8,128)(2,1)}, bf16[1024,512]{1,0:T(8,128)(2,1)S(1)}, u32[]{:S(2)}, u32[]{:S(2)}) collective-permute-start(bf16[1024,512]{1,0:T(8,128)(2,1)} %get-tuple-element.123), channel_id=1, source_target_pairs={{0,16},{8,24},{16,0},{24,8},{1,17},{9,25},{17,1},{25,9},{2,18},{10... | collective-permute-start | bytes 3145736 | tf_op jit(solution)/shard_map/ppermute | solution.py:739
  416.5 49.7 %collective-permute-start.28 = (bf16[512,512]{1,0:T(8,128)(2,1)}, bf16[512,512]{1,0:T(8,128)(2,1)}, u32[]{:S(2)}, u32[]{:S(2)}) collective-permute-start(bf16[512,512]{1,0:T(8,128)(2,1)} %add_convert_fusion.8), channel_id=1, source_target_pairs={{0,16},{8,24},{16,0},{24,8},{1,17},{9,25},{17,1},{25,9},{2,18},{10... | collective-permute-start | bytes 1572872 | tf_op jit(solution)/shard_map/ppermute | solution.py:739
  420.1 47.8 %collective-permute-start.30 = (bf16[512,512]{1,0:T(8,128)(2,1)}, bf16[512,512]{1,0:T(8,128)(2,1)}, u32[]{:S(2)}, u32[]{:S(2)}) collective-permute-start(bf16[512,512]{1,0:T(8,128)(2,1)} %add_convert_fusion.6), channel_id=1, source_target_pairs={{0,8},{8,0},{16,24},{24,16},{1,9},{9,1},{17,25},{25,17},{2,10},{10... | collective-permute-start | bytes 1572872 | tf_op jit(solution)/shard_map/ppermute | solution.py:739
  441.9 27.5 %collective-permute-start.32 = (bf16[512,512]{1,0:T(8,128)(2,1)}, bf16[512,512]{1,0:T(8,128)(2,1)}, u32[]{:S(2)}, u32[]{:S(2)}) collective-permute-start(bf16[512,512]{1,0:T(8,128)(2,1)} %add_convert_fusion.4), channel_id=1, source_target_pairs={{0,16},{8,24},{16,0},{24,8},{1,17},{9,25},{17,1},{25,9},{2,18},{10... | collective-permute-start | bytes 1572872 | tf_op jit(solution)/shard_map/ppermute | solution.py:739
  464.3 3.5 copy-start.10
  465.6 12.0 %collective-permute-start.34 = (bf16[512,512]{1,0:T(8,128)(2,1)S(1)}, bf16[512,512]{1,0:T(8,128)(2,1)S(1)}, u32[]{:S(2)}, u32[]{:S(2)}) collective-permute-start(bf16[512,512]{1,0:T(8,128)(2,1)S(1)} %add_convert_fusion.2), channel_id=1, source_target_pairs={{0,8},{8,0},{16,24},{24,16},{1,9},{9,1},{17,25},{25,17},{2,10},{10... | collective-permute-start | bytes 1572872 | tf_op jit(solution)/shard_map/ppermute | solution.py:739
  466.2 3.3 copy-start.12
  467.8 9.8 %copy-start.11 = (bf16[512,512]{1,0:T(8,128)(2,1)S(1)}, bf16[512,512]{1,0:T(8,128)(2,1)}, u32[]{:S(2)}) copy-start(bf16[512,512]{1,0:T(8,128)(2,1)} %get-tuple-element.122) | copy-start | bytes 1572868
  479.4 95.1 %all-to-all-start.3 = ((bf16[8,64,2048]{2,1,0:T(8,128)(2,1)}), bf16[8,64,2048]{2,1,0:T(8,128)(2,1)}, u32[]{:S(2)}, u32[]{:S(2)}) async-start(bf16[8,64,2048]{2,1,0:T(8,128)(2,1)} %bitcast.48), calls=%async_computation.7 | async-start | bytes 4194304 | tf_op jit(solution)/shard_map/all_to_all | solution.py:825
  494.1 25.4 %collective-permute-start.20 = (bf16[1024,512]{1,0:T(8,128)(2,1)}, bf16[1024,512]{1,0:T(8,128)(2,1)S(1)}, u32[]{:S(2)}, u32[]{:S(2)}) collective-permute-start(bf16[1024,512]{1,0:T(8,128)(2,1)} %get-tuple-element.101), channel_id=1, source_target_pairs={{0,8},{8,0},{16,24},{24,16},{1,9},{9,1},{17,25},{25,17},{2,10},{10... | collective-permute-start | bytes 3145736 | tf_op jit(solution)/shard_map/ppermute | solution.py:739
  495.0 27.8 %collective-permute-start.22 = (bf16[1024,512]{1,0:T(8,128)(2,1)}, bf16[1024,512]{1,0:T(8,128)(2,1)S(1)}, u32[]{:S(2)}, u32[]{:S(2)}) collective-permute-start(bf16[1024,512]{1,0:T(8,128)(2,1)} %get-tuple-element.104), channel_id=1, source_target_pairs={{0,16},{8,24},{16,0},{24,8},{1,17},{9,25},{17,1},{25,9},{2,18},{10... | collective-permute-start | bytes 3145736 | tf_op jit(solution)/shard_map/ppermute | solution.py:739
  519.5 3.3 copy-start.4
  521.8 16.6 %collective-permute-start.21 = (bf16[512,512]{1,0:T(8,128)(2,1)}, bf16[512,512]{1,0:T(8,128)(2,1)}, u32[]{:S(2)}, u32[]{:S(2)}) collective-permute-start(bf16[512,512]{1,0:T(8,128)(2,1)} %add_convert_fusion.12), channel_id=1, source_target_pairs={{0,16},{8,24},{16,0},{24,8},{1,17},{9,25},{17,1},{25,9},{2,18},{10... | collective-permute-start | bytes 1572872 | tf_op jit(solution)/shard_map/ppermute | solution.py:739
  524.7 15.3 %collective-permute-start.23 = (bf16[512,512]{1,0:T(8,128)(2,1)}, bf16[512,512]{1,0:T(8,128)(2,1)}, u32[]{:S(2)}, u32[]{:S(2)}) collective-permute-start(bf16[512,512]{1,0:T(8,128)(2,1)} %add_convert_fusion.10), channel_id=1, source_target_pairs={{0,8},{8,0},{16,24},{24,16},{1,9},{9,1},{17,25},{25,17},{2,10},{10... | collective-permute-start | bytes 1572872 | tf_op jit(solution)/shard_map/ppermute | solution.py:739
  535.0 5.1 copy-start.13
  535.0 21.1 %collective-permute-start.24 = (bf16[512,768]{1,0:T(8,128)(2,1)}, bf16[512,768]{1,0:T(8,128)(2,1)S(1)}, u32[]{:S(2)}, u32[]{:S(2)}) collective-permute-start(bf16[512,768]{1,0:T(8,128)(2,1)} %get-tuple-element.108), channel_id=1, source_target_pairs={{0,8},{8,0},{16,24},{24,16},{1,9},{9,1},{17,25},{25,17},{2,10},{10... | collective-permute-start | bytes 2359304 | tf_op jit(solution)/shard_map/ppermute | solution.py:739
  536.5 35.6 %collective-permute-start.25 = (bf16[512,768]{1,0:T(8,128)(2,1)}, bf16[512,768]{1,0:T(8,128)(2,1)S(1)}, u32[]{:S(2)}, u32[]{:S(2)}) collective-permute-start(bf16[512,768]{1,0:T(8,128)(2,1)} %get-tuple-element.109), channel_id=1, source_target_pairs={{0,24},{8,16},{16,8},{24,0},{1,25},{9,17},{17,9},{25,1},{2,26},{10... | collective-permute-start | bytes 2359304 | tf_op jit(solution)/shard_map/ppermute | solution.py:739
  538.0 34.8 %collective-permute-start.26 = (bf16[512,768]{1,0:T(8,128)(2,1)}, bf16[512,768]{1,0:T(8,128)(2,1)S(1)}, u32[]{:S(2)}, u32[]{:S(2)}) collective-permute-start(bf16[512,768]{1,0:T(8,128)(2,1)} %get-tuple-element.110), channel_id=1, source_target_pairs={{0,16},{8,24},{16,0},{24,8},{1,17},{9,25},{17,1},{25,9},{2,18},{10... | collective-permute-start | bytes 2359304 | tf_op jit(solution)/shard_map/ppermute | solution.py:739
  538.5 34.3 %copy-start.5 = (bf16[512,768]{1,0:T(8,128)(2,1)S(1)}, bf16[512,768]{1,0:T(8,128)(2,1)}, u32[]{:S(2)}) copy-start(bf16[512,768]{1,0:T(8,128)(2,1)} %get-tuple-element.107) | copy-start | bytes 2359300
  574.5 48.2 %all-to-all-start.2 = ((bf16[8,64,1792]{2,1,0:T(8,128)(2,1)}), bf16[8,64,1792]{2,1,0:T(8,128)(2,1)}, u32[]{:S(2)}, u32[]{:S(2)}) async-start(bf16[8,64,1792]{2,1,0:T(8,128)(2,1)} %bitcast.49), calls=%async_computation.5 | async-start | bytes 3670016 | tf_op jit(solution)/shard_map/all_to_all | solution.py:825
  (4 other events, 4.0 us)
Sparse Core Ops, SparseCore 0:
  11.6 49.5 all-gather.3
  77.4 53.6 all-gather.7
  136.1 49.3 all-gather.5
  280.7 49.2 reduce-scatter.4
  366.4 35.4 reduce-scatter.10
  404.0 56.7 reduce-scatter.6
  464.5 73.6 reduce-scatter.8

commit v2 on v1

--- a/solution.py
+++ b/solution.py
@@ -141,10 +141,15 @@
 
 
 def attention_backward_kernel(
-    block, count, per_row, q_ref, k_ref, v_ref, attn_ref, grad_ref, lse_ref, cos_ref, sin_ref, *refs
+    block, count, per_row, paired, group_ref,
+    q_ref, k_ref, v_ref, attn_ref, grad_ref, lse_ref, cos_ref, sin_ref, *refs
 ):
     pieces, refs = refs[:count], refs[count:]
-    out_ref, dxn_ref, weight_ref, dq_ref, dk_ref, dv_ref, delta_ref, flat_ref, sems = refs
+    if paired:
+        out_ref, mine_ref, theirs_ref, dxn_ref, half_sems, *refs = refs
+    else:
+        out_ref, dxn_ref, *refs = refs
+    weight_ref, dq_ref, dk_ref, dv_ref, delta_ref, flat_ref, sems = refs
     head = pl.program_id(0)
     length, width = q_ref.shape
     tokens = attn_ref.shape[3]
@@ -202,6 +207,21 @@
                     out_ref[at, target + c * 128 : target + (c + 1) * 128] = turned.astype(BF)
             out_ref[at, 2 * width : 3 * width] = dv_ref[at, :].astype(BF)
             dxn_ref[at, :] = contract_last(out_ref[at, :], weight_ref[...]).astype(BF)
+
+        if paired:
+            copies = []
+            for i in range(length // (2 * tokens)):
+                to = pl.ds(i * tokens, tokens)
+                for target, odd in ((theirs_ref, 1), (mine_ref, 0)):
+                    row = 2 * i * tokens + (group_ref[0] % 2 ^ odd) * tokens
+                    source = dxn_ref.at[pl.ds(pl.multiple_of(row, tokens), tokens)]
+                    copies.append(
+                        pltpu.make_async_copy(source, target.at[to], half_sems.at[len(copies)])
+                    )
+            for copy in copies:
+                copy.start()
+            for copy in copies:
+                copy.wait()
 
 
 def resident(shape):
@@ -239,26 +259,39 @@
     )(xn, *pieces, cosine, sine)
 
 
-def attention_backward(query, key, value, attn, grad, lse, cosine, sine, pieces, per_row):
+def attention_backward(
+    group, paired, query, key, value, attn, grad, lse, cosine, sine, pieces, per_row
+):
     length, width = query.shape
+    tokens = attn.shape[3]
     model_width = sum(piece.shape[0] for piece in pieces[::per_row])
     heads = width // HD
     block = min(256, length)
     pairs = heads * length * length
     flat = resident((length, width))
+    anywhere = pl.BlockSpec(memory_space=pl.ANY)
+    if paired:
+        dxn_specs, dxn_shapes = [anywhere] * 2, [(length // 2, model_width)] * 2
+        dxn_scratch = [
+            pltpu.VMEM((length, model_width), BF), pltpu.SemaphoreType.DMA((length // tokens,))
+        ]
+    else:
+        dxn_specs, dxn_shapes = [resident((length, model_width))], [(length, model_width)]
+        dxn_scratch = []
     return pl.pallas_call(
-        functools.partial(attention_backward_kernel, block, len(pieces), per_row),
+        functools.partial(attention_backward_kernel, block, len(pieces), per_row, paired),
         grid=(heads,),
-        in_specs=[flat, flat, flat, resident(attn.shape), resident(attn.shape)]
+        in_specs=[pl.BlockSpec(memory_space=pltpu.SMEM)]
+        + [flat, flat, flat, resident(attn.shape), resident(attn.shape)]
         + [resident((8, length))]
         + [resident(cosine.shape)] * 2
-        + [pl.BlockSpec(memory_space=pl.ANY)] * len(pieces),
-        out_specs=[resident((length, 3 * width)), resident((length, model_width))],
+        + [anywhere] * len(pieces),
+        out_specs=[resident((length, 3 * width))] + dxn_specs,
         out_shape=[
-            jax.ShapeDtypeStruct((length, 3 * width), BF),
-            jax.ShapeDtypeStruct((length, model_width), BF),
+            jax.ShapeDtypeStruct(shape, BF) for shape in [(length, 3 * width)] + dxn_shapes
         ],
-        scratch_shapes=[pltpu.VMEM((model_width, 3 * width), BF)]
+        scratch_shapes=dxn_scratch
+        + [pltpu.VMEM((model_width, 3 * width), BF)]
         + [pltpu.VMEM((length, width), F32)] * 3
         + [
             pltpu.VMEM((1, length), F32),
@@ -271,7 +304,7 @@
             transcendentals=pairs // 2,
         ),
         name="attention_backward",
-    )(query, key, value, attn, grad, lse, cosine, sine, *pieces)
+    )(group.reshape(1), query, key, value, attn, grad, lse, cosine, sine, *pieces)
 
 
 def strided_heads_kernel(which_ref, *refs):
@@ -563,14 +596,13 @@
 def outer_kernel(layouts, left_ref, right_ref, *out_refs):
     step = pl.program_id(0)
     steps = pl.num_programs(0) // 4
-    turned = left_ref[...].T
+    product = contract_first(left_ref[...], right_ref[...]).astype(BF)
     column = 0
     refs = iter(out_refs)
     for layout in layouts:
         targets = [next(refs) for _ in layout]
         width = targets[0].shape[1]
-        right = right_ref[:, column : column + width]
-        block = jnp.dot(turned, right, preferred_element_type=F32).astype(BF)
+        block = product[:, column : column + width]
         column += width
         for target, (first, end) in zip(targets, layout):
 
@@ -650,9 +682,10 @@
     )(xn, dy, *part_a, *part_b)
 
 
-def feed_out_kernel(count, act_ref, *refs):
-    pieces, (out_ref, down_ref, sems) = refs[:count], refs[count:]
+def feed_out_kernel(count, group_ref, act_ref, *refs):
+    pieces, (mine_ref, theirs_ref, out_ref, down_ref, sems) = refs[:count], refs[count:]
     hidden = act_ref.shape[1]
+    tokens = mine_ref.shape[0]
 
     @pl.when(pl.program_id(0) == 0)
     def _():
@@ -664,21 +697,28 @@
             copy.wait()
 
     columns_last(act_ref, down_ref, out_ref)
-
-
-def feed_out(act, part_b, model_width):
+    odd = group_ref[0] % 2
+    mine_ref[...] = out_ref[pl.ds(pl.multiple_of(odd * tokens, tokens), tokens), :]
+    theirs_ref[...] = out_ref[pl.ds(pl.multiple_of((1 - odd) * tokens, tokens), tokens), :]
+
+
+def feed_out(act, part_b, model_width, group, run):
     tokens, hidden = act.shape
-    block = min(256, tokens)
+    block = 2 * run
     pieces = in_order(part_b)
+    half = jax.ShapeDtypeStruct((tokens // 2, model_width), BF)
     return pl.pallas_call(
         functools.partial(feed_out_kernel, len(pieces)),
         grid=(tokens // block,),
-        in_specs=[pl.BlockSpec((block, hidden), lambda i: (i, 0))]
+        in_specs=[pl.BlockSpec(memory_space=pltpu.SMEM)]
+        + [pl.BlockSpec((block, hidden), lambda i: (i, 0))]
         + [pl.BlockSpec(memory_space=pl.ANY)] * len(pieces),
-        out_specs=pl.BlockSpec((block, model_width), lambda i: (i, 0)),
-        out_shape=jax.ShapeDtypeStruct((tokens, model_width), BF),
+        out_specs=[pl.BlockSpec((run, model_width), lambda i: (i, 0))] * 2,
+        out_shape=[half, half],
         scratch_shapes=[
-            pltpu.VMEM((model_width, hidden), BF), pltpu.SemaphoreType.DMA((len(pieces),))
+            pltpu.VMEM((block, model_width), BF),
+            pltpu.VMEM((model_width, hidden), BF),
+            pltpu.SemaphoreType.DMA((len(pieces),)),
         ],
         cost_estimate=pl.CostEstimate(
             flops=2 * tokens * model_width * hidden,
@@ -686,7 +726,7 @@
             transcendentals=0,
         ),
         name="feed_out",
-    )(act, *pieces)
+    )(group.reshape(1), act, *pieces)
 
 
 def rows_by_member(pieces, places_ref, target_ref, sems):
@@ -819,6 +859,15 @@
 
 def sum_over_seq(values):
     return lax.psum_scatter(values.astype(BF), "seq", scatter_dimension=0, tiled=True)
+
+
+def sum_over_pairs(mine, theirs, group_count, *earlier):
+    received = lax.ppermute(theirs, "seq", [(i, i ^ 1) for i in range(group_count)])
+    total = after(add(mine, received), *earlier)
+    return lax.psum_scatter(
+        total, "seq", scatter_dimension=0, tiled=True,
+        axis_index_groups=[list(range(odd, group_count, 2)) for odd in range(2)],
+    )
 
 
 def exchange(values, axes):
@@ -955,18 +1004,20 @@
     if quad:
         part_a, part_b = rest_of_weights(*partials)
         act, grad_gate_up, partial_xn2 = feed_forward(xn2, dy, part_a, part_b, hidden)
-        feed_sum = feed_out(after(act, partial_xn2), part_b, model_width)
+        feed_halves = feed_out(after(act, partial_xn2), part_b, model_width, group, token_rows)
     else:
         act, grad_gate_up, partial_xn2 = feed_forward_plain(
             xn2, dy, gate_up_full, down_full, hidden
         )
         feed_sum = contract_last(act, down_full).astype(BF)
     raw_xn2 = sum_over_seq(partial_xn2)
-    feed_sum = after(feed_sum, raw_xn2)
     grad_hidden, hidden_low = on_rows(
         norm_grad_kernel, places, (hidden_res, cotangent, raw_xn2, gain2), (F32, BF)
     )
-    feed_sum = sum_over_seq(feed_sum)
+    if quad:
+        feed_sum = sum_over_pairs(*feed_halves, group_count, raw_xn2)
+    else:
+        feed_sum = sum_over_seq(after(feed_sum, raw_xn2))
     if quad:
         sides = (OVER_X_FIRST, OVER_Y_FIRST)
         down_sum = PairSum(*outer_blocks(dy, act, sides, 1))
@@ -999,14 +1050,15 @@
         ).astype(BF)
     out_grad = sum_over_seq(out_rows).astype(F32)
     grad_qkv, partial_xn1 = attention_backward(
-        query, key, value, attn, grad_attn, lse, cosine, sine, qkv_pieces, per_row
+        group, False,
+        query, key, value, attn, grad_attn, lse, cosine, sine, qkv_pieces, per_row,
     )
     raw_xn1 = sum_over_seq(partial_xn1)
     (input_grad,) = on_rows(
         norm_grad_kernel, places, (layer_in, grad_hidden, raw_xn1, gain1), (F32,)
     )
     (layer_out,) = on_rows(
-        add_placed_kernel, places, (hidden_res, after(feed_sum, partial_xn1)), (F32,)
+        add_placed_kernel, places, (hidden_res, after(feed_sum, grad_qkv)), (F32,)
     )
 
     if quad:

time: 646 us -> 632 us (0.978)
  waiting for transfers between devices: 352 us -> 336 us
    reduce_scatter x4 -> x3, waiting for transfers between devices: 48.6 us -> 30.2 us  [sum_over_seq(): lax.psum_scatter(values.astype(BF), 'seq', scatter_dimension=0, tiled=True)]
    convert_element_type x13 -> x14, other arithmetic: 20.1 us -> 23.8 us  [add(): return total.astype(BF)]
  transfers between devices with their start and end apart: 46 -> 47, of which waited for: 23 -> 24; matrix products, arithmetic and copies ran while one was open for 7% -> 8% of each run, Pallas kernels for 15% -> 17%
where the time goes in v2:
time: 632 us; the launch traced here: 630 us
  waiting for transfers between devices  336 us (53%)
  Pallas kernels  162 us (26%)
  starting transfers between devices  62.5 us (10%)
  other arithmetic  32 us (5%)
  local copies, waits for them, and re-layouts  15.5 us (2%)
  between operations  14.5 us (2%)
  matrix products  7.77 us (1%)
    ppermute x35, waiting for transfers between devices, partner(): return lax.ppermute(array, 'dp', [(i, i ^ bits) for i in range(4)])  231 us
    all_to_all x4, waiting for transfers between devices, exchange(): return lax.all_to_all(values, axes, split_axis=0, concat_axis=0, tiled=True)  57.9 us
    ppermute x35, starting transfers between devices, partner(): return lax.ppermute(array, 'dp', [(i, i ^ bits) for i in range(4)])  46.2 us
    pallas_call x4, Pallas kernels, outer_blocks(): pl.pallas_call(functools.partial(outer_kernel, layouts), grid=(4 * steps,...  38.1 us
    pallas_call x1, Pallas kernels, feed_forward(): pl.pallas_call(functools.partial(feed_kernel, len(part_a), len(part_b)),...  32.3 us
    reduce_scatter x3, waiting for transfers between devices, sum_over_seq(): lax.psum_scatter(values.astype(BF), 'seq', scatter_dimension=0, tiled=True)  30.2 us
    convert_element_type x14, other arithmetic, add(): return total.astype(BF)  23.8 us
    pallas_call x1, Pallas kernels, attention_backward(): pl.pallas_call(functools.partial(attention_backward_kernel, block, len(pi...  21 us
  transfers between devices with their start and end apart: 47, of which 24 were waited for; matrix products, arithmetic and copies ran while one was open for 8% of the time, Pallas kernels for 17%

profile of v2, /device:TPU:0, one launch (start us, length us, event | category | flops | bytes accessed | tf_op | source)
XLA Modules:
  0.0 630.0 jit_solution(3152286482385998052)
XLA Ops:
  7.8 3.7 shard_map.143
  11.6 2.7 strided_heads.1
  14.2 3.0 collective-permute-start.2
  19.3 2.2 constant_dynamic-slice_fusion.2
  22.9 2.3 constant_dynamic-slice_fusion.1
  25.2 11.4 %collective-permute-done.refs_2_ = bf16[512,384]{1,0:T(8,128)(2,1)} collective-permute-done((bf16[512,384]{1,0:T(8,128)(2,1)}, bf16[512,384]{1,0:T(8,128)(2,1)}, u32[]{:S(2)}, u32[]{:S(2)}) %collective-permute-start) | collective-permute-done | bytes 393248 | tf_op jit(solution)/shard_map/ppermute | solution.py:779
  36.9 1.7 collective-permute-start.3
  39.2 4.3 rotary.1
  43.5 1.8 pad_maximum_fusion.2
  49.0 12.3 %all-gather.4.cloned.1.call-done.xn_ref.left_ref = bf16[1024,2048]{1,0:T(8,128)(2,1)} async-done(((bf16[128,2048]{1,0:T(8,128)(2,1)}), bf16[1024,2048]{1,0:T(8,128)(2,1)}) %all-gather.4.cloned.1.call-update) | async-done | bytes 4194320 | tf_op jit(solution)/shard_map/all_gather | solution.py:857
  61.3 16.0 %attention_forward.1 = (bf16[4,8,64,128]{3,2,1,0:T(8,128)(2,1)}, bf16[1024,256]{1,0:T(8,128)(2,1)}, bf16[1024,256]{1,0:T(8,128)(2,1)}, bf16[1024,256]{1,0:T(8,128)(2,1)}, f32[8,1024]{1,0:T(8,128)}) custom-call(bf16[1024,2048]{1,0:T(8,128)(2,1)} %all-gather.4.cloned.1.call-done.xn_ref.left_ref, bf16[512,384]{1,0:T(8,128)(2,1)} %get-tuple-element.71.refs_0_, ...), custom_call_target="tpu_custom_call" | custom-call | flops 3758096384 | bytes 9437184 | tf_op jit(solution)/shard_map/attention_forward/pallas_call | solution.py:238
  77.3 3.4 all-to-all-start
  80.8 25.0 %all-to-all-done = bf16[32,64,128]{2,1,0:T(8,128)(2,1)S(1)} async-done(((bf16[32,64,128]{2,1,0:T(8,128)(2,1)}), bf16[32,64,128]{2,1,0:T(8,128)(2,1)S(1)}, u32[]{:S(2)}, u32[]{:S(2)}) %all-to-all-start) | async-done | bytes 524320 | tf_op jit(solution)/shard_map/all_to_all | solution.py:874
  110.7 2.4 collective-permute-start.8
  114.5 6.6 %collective-permute-done.6.refs_1_ = bf16[128,2048]{1,0:T(8,128)(2,1)} collective-permute-done((bf16[128,2048]{1,0:T(8,128)(2,1)}, bf16[128,2048]{1,0:T(8,128)(2,1)}, u32[]{:S(2)}, u32[]{:S(2)}) %collective-permute-start.6) | collective-permute-done | bytes 524320 | tf_op jit(solution)/shard_map/ppermute | solution.py:779
  122.3 9.1 %collective-permute-done.8.refs_3_ = bf16[128,2048]{1,0:T(8,128)(2,1)} collective-permute-done((bf16[128,2048]{1,0:T(8,128)(2,1)}, bf16[128,2048]{1,0:T(8,128)(2,1)}, u32[]{:S(2)}, u32[]{:S(2)}) %collective-permute-start.8) | collective-permute-done | bytes 524320 | tf_op jit(solution)/shard_map/ppermute | solution.py:779
  131.4 4.5 shard_map.144
  136.0 2.5 collective-permute-start.15
  138.5 2.1 collective-permute-start.9
  140.6 1.9 collective-permute-start.11
  142.6 30.3 %collective-permute-done.15.refs_9_.refs_4_ = bf16[512,1536]{1,0:T(8,128)(2,1)S(1)} collective-permute-done((bf16[512,1536]{1,0:T(8,128)(2,1)}, bf16[512,1536]{1,0:T(8,128)(2,1)S(1)}, u32[]{:S(2)}, u32[]{:S(2)}) %collective-permute-start.15) | collective-permute-done | bytes 1572896 | tf_op jit(solution)/shard_map/ppermute | solution.py:779
  172.9 5.1 collective-permute-start.16
  180.1 9.6 %collective-permute-done.11.refs_3_ = bf16[256,1536]{1,0:T(8,128)(2,1)S(1)} collective-permute-done((bf16[256,1536]{1,0:T(8,128)(2,1)}, bf16[256,1536]{1,0:T(8,128)(2,1)S(1)}, u32[]{:S(2)}, u32[]{:S(2)}) %collective-permute-start.11) | collective-permute-done | bytes 786464 | tf_op jit(solution)/shard_map/ppermute | solution.py:779
  189.7 2.4 collective-permute-start.12
  192.1 38.0 %collective-permute-done.13.refs_6_.refs_1_ = bf16[256,1536]{1,0:T(8,128)(2,1)S(1)} collective-permute-done((bf16[256,1536]{1,0:T(8,128)(2,1)}, bf16[256,1536]{1,0:T(8,128)(2,1)S(1)}, u32[]{:S(2)}, u32[]{:S(2)}) %collective-permute-start.13) | collective-permute-done | bytes 786464 | tf_op jit(solution)/shard_map/ppermute | solution.py:779
  230.1 15.7 %collective-permute-done.14.refs_7_.refs_2_ = bf16[256,1536]{1,0:T(8,128)(2,1)S(1)} collective-permute-done((bf16[256,1536]{1,0:T(8,128)(2,1)}, bf16[256,1536]{1,0:T(8,128)(2,1)S(1)}, u32[]{:S(2)}, u32[]{:S(2)}) %collective-permute-start.14) | collective-permute-done | bytes 786464 | tf_op jit(solution)/shard_map/ppermute | solution.py:779
  248.2 32.3 %feed_forward.1 = (bf16[1024,1024]{1,0:T(8,128)(2,1)}, bf16[1024,2048]{1,0:T(8,128)(2,1)}, bf16[1024,2048]{1,0:T(8,128)(2,1)}) custom-call(bf16[1024,2048]{1,0:T(8,128)(2,1)} %all-gather.6.cloned.1.call-done.xn_ref.left_ref, bf16[1024,2048]{1,0:T(8,128)(2,1)} %all-gather.8.cloned.1.call-done.dy_ref.left_ref, bf16[512,1536]{1,0:T(8,128)(2,1)} %copy-done.2, ...), custom_call_target="tpu_custom_call" | custom-call | flops 21474836480 | bytes 29360128 | tf_op jit(solution)/shard_map/feed_forward/pallas_call | solution.py:661
  280.7 10.6 %feed_out.1 = (bf16[512,2048]{1,0:T(8,128)(2,1)}, bf16[512,2048]{1,0:T(8,128)(2,1)}) custom-call(s32[1]{0:T(128)} %bitcast.1.which_ref.group_ref, bf16[1024,1024]{1,0:T(8,128)(2,1)} %get-tuple-element.91.act_ref.right_ref, bf16[512,1536]{1,0:T(8,128)(2,1)} %copy-done.1, bf16[256,1536]{1,0:T(8,128)(2,1)} %copy-done.17, bf16[256,1536]{1,0:T(8,128)(2,1)} %copy-done.19, ...), custom_call_target="tpu_custom_call" | custom-call | flops 4294967296 | bytes 10485760 | tf_op jit(solution)/shard_map/feed_out/pallas_call | solution.py:710
  291.4 4.5 collective-permute-done.17
  296.0 3.7 add_convert_fusion
  299.7 30.2 %reduce-scatter.5.cloned.1.call-done.refs_1_ = bf16[128,2048]{1,0:T(8,128)(2,1)} async-done(((bf16[1024,2048]{1,0:T(8,128)(2,1)}), bf16[128,2048]{1,0:T(8,128)(2,1)}) %reduce-scatter.5.cloned.1.call-update) | async-done | bytes 524304 | tf_op jit(solution)/shard_map/reduce_scatter | solution.py:861
  330.5 4.6 shard_map.145
  339.1 11.0 %collective-permute-done.18.refs_1_ = bf16[128,2048]{1,0:T(8,128)(2,1)S(1)} collective-permute-done((bf16[128,2048]{1,0:T(8,128)(2,1)}, bf16[128,2048]{1,0:T(8,128)(2,1)S(1)}, u32[]{:S(2)}, u32[]{:S(2)}) %collective-permute-start.18) | collective-permute-done | bytes 524320 | tf_op jit(solution)/shard_map/ppermute | solution.py:779
  350.1 9.4 %collective-permute-done.19.refs_2_ = bf16[128,2048]{1,0:T(8,128)(2,1)S(1)} collective-permute-done((bf16[128,2048]{1,0:T(8,128)(2,1)}, bf16[128,2048]{1,0:T(8,128)(2,1)S(1)}, u32[]{:S(2)}, u32[]{:S(2)}) %collective-permute-start.19) | collective-permute-done | bytes 524320 | tf_op jit(solution)/shard_map/ppermute | solution.py:779
  360.3 6.4 %out_rows.1 = bf16[512,2048]{1,0:T(8,128)(2,1)} custom-call(s32[4]{0:T(128)} %iota_xor_fusion.members_ref, bf16[4,512,128]{2,1,0:T(8,128)(2,1)} %bitcast.54, bf16[128,2048]{1,0:T(8,128)(2,1)} %get-tuple-element.98.refs_0_, bf16[128,2048]{1,0:T(8,128)(2,1)} %copy-done.7, bf16[128,2048]{1,0:T(8,128)(2,1)} %copy-done.9, ...), custom_call_target="tpu_custom_call" | custom-call | tf_op jit(solution)/shard_map/out_rows/pallas_call | solution.py:763
  366.7 9.4 %outer_blocks.6 = (bf16[1024,512]{1,0:T(8,128)(2,1)}, bf16[512,512]{1,0:T(8,128)(2,1)}, bf16[512,512]{1,0:T(8,128)(2,1)}, bf16[1024,512]{1,0:T(8,128)(2,1)}, bf1...) custom-call(bf16[1024,2048]{1,0:T(8,128)(2,1)} %all-gather.8.cloned.1.call-done.dy_ref.left_ref, ...), custom_call_target="tpu_custom_call" | custom-call | flops 4294967296 | bytes 10485760 | tf_op jit(solution)/shard_map/outer_blocks/pallas_call | solution.py:627
  378.2 9.5 %outer_blocks.7 = (bf16[1024,512]{1,0:T(8,128)(2,1)}, bf16[512,512]{1,0:T(8,128)(2,1)}, bf16[512,512]{1,0:T(8,128)(2,1)}, bf16[1024,512]{1,0:T(8,128)(2,1)}, bf1...) custom-call(bf16[1024,2048]{1,0:T(8,128)(2,1)} %all-gather.6.cloned.1.call-done.xn_ref.left_ref, ...), custom_call_target="tpu_custom_call" | custom-call | flops 4294967296 | bytes 10485760 | tf_op jit(solution)/shard_map/outer_blocks/pallas_call | solution.py:627
  389.1 2.5 fusion.9
  392.7 3.3 all-to-all-start.1
  396.3 1.7 collective-permute-start.34
  398.1 5.4 collective-permute-done.28
  403.5 2.1 add_convert_fusion.9
  407.2 2.1 add_convert_fusion.7
  409.8 19.3 %collective-permute-done.32 = bf16[1024,512]{1,0:T(8,128)(2,1)} collective-permute-done((bf16[1024,512]{1,0:T(8,128)(2,1)}, bf16[1024,512]{1,0:T(8,128)(2,1)}, u32[]{:S(2)}, u32[]{:S(2)}) %collective-permute-start.32) | collective-permute-done | bytes 1048608 | tf_op jit(solution)/shard_map/ppermute | solution.py:779
  429.2 2.1 add_convert_fusion.5
  432.7 21.0 %attention_backward.1 = (bf16[1024,768]{1,0:T(8,128)(2,1)}, bf16[1024,2048]{1,0:T(8,128)(2,1)}) custom-call(s32[1]{0:T(128)} %bitcast.1.which_ref.group_ref, bf16[1024,256]{1,0:T(8,128)(2,1)} %get-tuple-element.95.q_ref, bf16[1024,256]{1,0:T(8,128)(2,1)} %get-tuple-element.96.k_ref, bf16[1024,256]{1,0:T(8,128)(2,1)} %get-tuple-element.97.v_ref, ...), custom_call_target="tpu_custom_call" | custom-call | flops 4563402752 | bytes 12582912 | tf_op jit(solution)/shard_map/attention_backward/pallas_call | solution.py:281
  460.4 6.3 %collective-permute-done.35 = bf16[512,512]{1,0:T(8,128)(2,1)S(1)} collective-permute-done((bf16[512,512]{1,0:T(8,128)(2,1)S(1)}, bf16[512,512]{1,0:T(8,128)(2,1)S(1)}, u32[]{:S(2)}, u32[]{:S(2)}) %collective-permute-start.35) | collective-permute-done | bytes 524320 | tf_op jit(solution)/shard_map/ppermute | solution.py:779
  468.6 4.4 all-to-all-start.3
  472.9 9.4 %outer_blocks.4 = (bf16[1024,512]{1,0:T(8,128)(2,1)}, bf16[512,512]{1,0:T(8,128)(2,1)}, bf16[512,512]{1,0:T(8,128)(2,1)}, bf16[1024,512]{1,0:T(8,128)(2,1)}, bf1...) custom-call(bf16[1024,2048]{1,0:T(8,128)(2,1)} %all-gather.6.cloned.1.call-done.xn_ref.left_ref, ...), custom_call_target="tpu_custom_call" | custom-call | flops 4294967296 | bytes 10485760 | tf_op jit(solution)/shard_map/outer_blocks/pallas_call | solution.py:627
  483.9 24.1 %collective-permute-done.21 = bf16[1024,512]{1,0:T(8,128)(2,1)S(1)} collective-permute-done((bf16[1024,512]{1,0:T(8,128)(2,1)}, bf16[1024,512]{1,0:T(8,128)(2,1)S(1)}, u32[]{:S(2)}, u32[]{:S(2)}) %collective-permute-start.21) | collective-permute-done | bytes 1048608 | tf_op jit(solution)/shard_map/ppermute | solution.py:779
  508.0 2.4 add_convert_fusion.13
  511.7 2.0 add_convert_fusion.11
  513.9 9.8 %outer_blocks.5 = (bf16[512,768]{1,0:T(8,128)(2,1)}, bf16[512,768]{1,0:T(8,128)(2,1)}, bf16[512,768]{1,0:T(8,128)(2,1)}, bf16[512,768]{1,0:T(8,128)(2,1)}) custom-call(bf16[1024,2048]{1,0:T(8,128)(2,1)} %all-gather.4.cloned.1.call-done.xn_ref.left_ref, bf16[1024,768]{1,0:T(8,128)(2,1)} %get-tuple-element.100.right_ref), custom_call_target="tpu_custom_call" | custom-call | flops 3221225472 | bytes 8912896 | tf_op jit(solution)/shard_map/outer_blocks/pallas_call | solution.py:627
  523.7 1.7 collective-permute-start.25
  530.1 15.1 %collective-permute-done.25 = bf16[512,768]{1,0:T(8,128)(2,1)S(1)} collective-permute-done((bf16[512,768]{1,0:T(8,128)(2,1)}, bf16[512,768]{1,0:T(8,128)(2,1)S(1)}, u32[]{:S(2)}, u32[]{:S(2)}) %collective-permute-start.25) | collective-permute-done | bytes 786464 | tf_op jit(solution)/shard_map/ppermute | solution.py:779
  545.2 15.8 %collective-permute-done.26 = bf16[512,768]{1,0:T(8,128)(2,1)S(1)} collective-permute-done((bf16[512,768]{1,0:T(8,128)(2,1)}, bf16[512,768]{1,0:T(8,128)(2,1)S(1)}, u32[]{:S(2)}, u32[]{:S(2)}) %collective-permute-start.26) | collective-permute-done | bytes 786464 | tf_op jit(solution)/shard_map/ppermute | solution.py:779
  563.4 4.4 all-to-all-start.2
  570.4 3.2 side_rows.3
  573.6 3.1 shard_map.146
  576.7 1.8 convert_element_type.200
  578.5 32.9 %all-to-all-done.2.in_ref.refs_1_ = bf16[8,64,1792]{2,1,0:T(8,128)(2,1)} async-done(((bf16[8,64,1792]{2,1,0:T(8,128)(2,1)}), bf16[8,64,1792]{2,1,0:T(8,128)(2,1)}, u32[]{:S(2)}, u32[]{:S(2)}) %all-to-all-start.2) | async-done | bytes 1835040 | tf_op jit(solution)/shard_map/all_to_all | solution.py:874
  611.4 4.3 side_rows.2
  615.7 3.2 strided_rows.1
  618.9 4.3 shard_map.147
  (139 shorter events, 55.9 us)
Async XLA Ops:
  7.2 98.6 %copy-start = (bf16[512,2048]{1,0:T(8,128)(2,1)S(1)}, bf16[512,2048]{1,0:T(8,128)(2,1)}, u32[]{:S(2)}) copy-start(bf16[512,2048]{1,0:T(8,128)(2,1)} %param.11) | copy-start | bytes 6291460
  7.2 54.1 %all-gather.4.cloned.1.call-start = ((), (), s32[]{:S(2)}) async-start(), calls=%async_computation.8 | async-start | bytes 4718592 | tf_op jit(solution)/shard_map/all_gather | solution.py:857
  11.5 236.7 %all-gather.8.cloned.1.call-start = ((), (), s32[]{:S(2)}) async-start(), calls=%async_computation.10 | async-start | bytes 4718592 | tf_op jit(solution)/shard_map/all_gather | solution.py:857
  14.2 22.6 %collective-permute-start.2 = (bf16[512,384]{1,0:T(8,128)(2,1)}, bf16[512,384]{1,0:T(8,128)(2,1)S(1)}, u32[]{:S(2)}, u32[]{:S(2)}) collective-permute-start(bf16[512,384]{1,0:T(8,128)(2,1)} %get-tuple-element.72.refs_1_), channel_id=1, source_target_pairs={{0,16},{8,24},{16,0},{24,8},{1,17},{9,25},{17,1},{25,9},{2,18},{10... | collective-permute-start | bytes 1179656 | tf_op jit(solution)/shard_map/ppermute | solution.py:779
  17.2 44.0 %collective-permute-start.4 = (bf16[512,384]{1,0:T(8,128)(2,1)}, bf16[512,384]{1,0:T(8,128)(2,1)}, u32[]{:S(2)}, u32[]{:S(2)}) collective-permute-start(bf16[512,384]{1,0:T(8,128)(2,1)} %get-tuple-element.72.refs_1_), channel_id=1, source_target_pairs={{0,8},{8,0},{16,24},{24,16},{1,9},{9,1},{17,25},{25,17},{2,10},{10... | collective-permute-start | bytes 1179656 | tf_op jit(solution)/shard_map/ppermute | solution.py:779
  18.7 17.8 %collective-permute-start = (bf16[512,384]{1,0:T(8,128)(2,1)}, bf16[512,384]{1,0:T(8,128)(2,1)}, u32[]{:S(2)}, u32[]{:S(2)}) collective-permute-start(bf16[512,384]{1,0:T(8,128)(2,1)} %get-tuple-element.71.refs_0_), channel_id=1, source_target_pairs={{0,8},{8,0},{16,24},{24,16},{1,9},{9,1},{17,25},{25,17},{2,10},{10... | collective-permute-start | bytes 1179656 | tf_op jit(solution)/shard_map/ppermute | solution.py:779
  19.3 42.0 %collective-permute-start.5 = (bf16[512,384]{1,0:T(8,128)(2,1)}, bf16[512,384]{1,0:T(8,128)(2,1)}, u32[]{:S(2)}, u32[]{:S(2)}) collective-permute-start(bf16[512,384]{1,0:T(8,128)(2,1)} %get-tuple-element.71.refs_0_), channel_id=1, source_target_pairs={{0,16},{8,24},{16,0},{24,8},{1,17},{9,25},{17,1},{25,9},{2,18},{10... | collective-permute-start | bytes 1179656 | tf_op jit(solution)/shard_map/ppermute | solution.py:779
  36.6 10.0 %collective-permute-start.1 = (bf16[512,384]{1,0:T(8,128)(2,1)}, bf16[512,384]{1,0:T(8,128)(2,1)}, u32[]{:S(2)}, u32[]{:S(2)}) collective-permute-start(bf16[512,384]{1,0:T(8,128)(2,1)} %collective-permute-done.refs_2_), channel_id=1, source_target_pairs={{0,16},{8,24},{16,0},{24,8},{1,17},{9,25},{17,1},{25,9},{2,18},{10... | collective-permute-start | bytes 1179656 | tf_op jit(solution)/shard_map/ppermute | solution.py:779
  36.9 8.4 %copy-start.21 = (bf16[512,384]{1,0:T(8,128)(2,1)}, bf16[512,384]{1,0:T(8,128)(2,1)S(1)}, u32[]{:S(2)}) copy-start(bf16[512,384]{1,0:T(8,128)(2,1)S(1)} %collective-permute-done.2.refs_7_) | copy-start | bytes 1179652
  36.9 9.8 %collective-permute-start.3 = (bf16[512,384]{1,0:T(8,128)(2,1)S(1)}, bf16[512,384]{1,0:T(8,128)(2,1)}, u32[]{:S(2)}, u32[]{:S(2)}) collective-permute-start(bf16[512,384]{1,0:T(8,128)(2,1)S(1)} %collective-permute-done.2.refs_7_), channel_id=1, source_target_pairs={{0,8},{8,0},{16,24},{24,16},{1,9},{9,1},{17,25},{25,17},{2,10},{10... | collective-permute-start | bytes 1179656 | tf_op jit(solution)/shard_map/ppermute | solution.py:779
  45.3 2.7 copy-start.2
  77.3 28.5 %all-to-all-start = ((bf16[32,64,128]{2,1,0:T(8,128)(2,1)}), bf16[32,64,128]{2,1,0:T(8,128)(2,1)S(1)}, u32[]{:S(2)}, u32[]{:S(2)}) async-start(bf16[32,64,128]{2,1,0:T(8,128)(2,1)} %bitcast.58), calls=%async_computation | async-start | bytes 1048576 | tf_op jit(solution)/shard_map/all_to_all | solution.py:874
  80.7 167.5 %all-gather.6.cloned.1.call-start = ((), (), s32[]{:S(2)}) async-start(), calls=%async_computation.9 | async-start | bytes 4718592 | tf_op jit(solution)/shard_map/all_gather | solution.py:857
  105.7 7.3 %copy-start.3 = (bf16[32,64,128]{2,1,0:T(8,128)(2,1)}, bf16[32,64,128]{2,1,0:T(8,128)(2,1)S(1)}, u32[]{:S(2)}) copy-start(bf16[32,64,128]{2,1,0:T(8,128)(2,1)S(1)} %all-to-all-done) | copy-start | bytes 1572868
  107.0 14.1 %collective-permute-start.6 = (bf16[128,2048]{1,0:T(8,128)(2,1)}, bf16[128,2048]{1,0:T(8,128)(2,1)}, u32[]{:S(2)}, u32[]{:S(2)}) collective-permute-start(bf16[128,2048]{1,0:T(8,128)(2,1)} %convolution_convert_fusion.2), channel_id=1, source_target_pairs={{0,8},{8,0},{16,24},{24,16},{1,9},{9,1},{17,25},{25,17},{2,10},{10... | collective-permute-start | bytes 1572872 | tf_op jit(solution)/shard_map/ppermute | solution.py:779
  108.3 14.0 %collective-permute-start.7 = (bf16[128,2048]{1,0:T(8,128)(2,1)}, bf16[128,2048]{1,0:T(8,128)(2,1)}, u32[]{:S(2)}, u32[]{:S(2)}) collective-permute-start(bf16[128,2048]{1,0:T(8,128)(2,1)} %convolution_convert_fusion.1), channel_id=1, source_target_pairs={{0,16},{8,24},{16,0},{24,8},{1,17},{9,25},{17,1},{25,9},{2,18},{10... | collective-permute-start | bytes 1572872 | tf_op jit(solution)/shard_map/ppermute | solution.py:779
  110.7 20.7 %collective-permute-start.8 = (bf16[128,2048]{1,0:T(8,128)(2,1)}, bf16[128,2048]{1,0:T(8,128)(2,1)}, u32[]{:S(2)}, u32[]{:S(2)}) collective-permute-start(bf16[128,2048]{1,0:T(8,128)(2,1)} %convolution_convert_fusion), channel_id=1, source_target_pairs={{0,24},{8,16},{16,8},{24,0},{1,25},{9,17},{17,9},{25,1},{2,26},{10... | collective-permute-start | bytes 1572872 | tf_op jit(solution)/shard_map/ppermute | solution.py:779
  135.9 194.0 %reduce-scatter.5.cloned.1.call-start = ((), (), s32[]{:S(2)}) async-start(), calls=%async_computation.11 | async-start | bytes 4718592 | tf_op jit(solution)/shard_map/reduce_scatter | solution.py:861
  136.0 36.9 %collective-permute-start.15 = (bf16[512,1536]{1,0:T(8,128)(2,1)}, bf16[512,1536]{1,0:T(8,128)(2,1)S(1)}, u32[]{:S(2)}, u32[]{:S(2)}) collective-permute-start(bf16[512,1536]{1,0:T(8,128)(2,1)} %copy-done.1), channel_id=1, source_target_pairs={{0,16},{8,24},{16,0},{24,8},{1,17},{9,25},{17,1},{25,9},{2,18},{10... | collective-permute-start | bytes 4718600 | tf_op jit(solution)/shard_map/ppermute | solution.py:779
  138.5 39.5 %collective-permute-start.9 = (bf16[512,1536]{1,0:T(8,128)(2,1)}, bf16[512,1536]{1,0:T(8,128)(2,1)S(1)}, u32[]{:S(2)}, u32[]{:S(2)}) collective-permute-start(bf16[512,1536]{1,0:T(8,128)(2,1)} %copy-done.2), channel_id=1, source_target_pairs={{0,8},{8,0},{16,24},{24,16},{1,9},{9,1},{17,25},{25,17},{2,10},{10... | collective-permute-start | bytes 4718600 | tf_op jit(solution)/shard_map/ppermute | solution.py:779
  140.6 49.1 %collective-permute-start.11 = (bf16[256,1536]{1,0:T(8,128)(2,1)}, bf16[256,1536]{1,0:T(8,128)(2,1)S(1)}, u32[]{:S(2)}, u32[]{:S(2)}) collective-permute-start(bf16[256,1536]{1,0:T(8,128)(2,1)} %get-tuple-element.84), channel_id=1, source_target_pairs={{0,16},{8,24},{16,0},{24,8},{1,17},{9,25},{17,1},{25,9},{2,18},{10... | collective-permute-start | bytes 2359304 | tf_op jit(solution)/shard_map/ppermute | solution.py:779
  172.9 73.0 %copy-start.14 = (bf16[512,1536]{1,0:T(8,128)(2,1)}, bf16[512,1536]{1,0:T(8,128)(2,1)S(1)}, u32[]{:S(2)}) copy-start(bf16[512,1536]{1,0:T(8,128)(2,1)S(1)} %collective-permute-done.15.refs_9_.refs_4_) | copy-start | bytes 4718596
  172.9 73.0 %collective-permute-start.16 = (bf16[512,1536]{1,0:T(8,128)(2,1)S(1)}, bf16[512,1536]{1,0:T(8,128)(2,1)S(1)}, u32[]{:S(2)}, u32[]{:S(2)}) collective-permute-start(bf16[512,1536]{1,0:T(8,128)(2,1)S(1)} %collective-permute-done.15.refs_9_.refs_4_), channel_id=1, source_target_pairs={{0,8},{8,0},{16,24},{24,16},{1,9},{9,1},{17,25},{25,17},{2,10},{10... | collective-permute-start | bytes 4718600 | tf_op jit(solution)/shard_map/ppermute | solution.py:779
  178.0 67.8 %copy-start.16 = (bf16[512,1536]{1,0:T(8,128)(2,1)}, bf16[512,1536]{1,0:T(8,128)(2,1)S(1)}, u32[]{:S(2)}) copy-start(bf16[512,1536]{1,0:T(8,128)(2,1)S(1)} %collective-permute-done.9.refs_1_) | copy-start | bytes 4718596
  178.0 70.1 %collective-permute-start.10 = (bf16[512,1536]{1,0:T(8,128)(2,1)S(1)}, bf16[512,1536]{1,0:T(8,128)(2,1)}, u32[]{:S(2)}, u32[]{:S(2)}) collective-permute-start(bf16[512,1536]{1,0:T(8,128)(2,1)S(1)} %collective-permute-done.9.refs_1_), channel_id=1, source_target_pairs={{0,16},{8,24},{16,0},{24,8},{1,17},{9,25},{17,1},{25,9},{2,18},{10... | collective-permute-start | bytes 4718600 | tf_op jit(solution)/shard_map/ppermute | solution.py:779
  178.0 52.1 %collective-permute-start.13 = (bf16[256,1536]{1,0:T(8,128)(2,1)}, bf16[256,1536]{1,0:T(8,128)(2,1)S(1)}, u32[]{:S(2)}, u32[]{:S(2)}) collective-permute-start(bf16[256,1536]{1,0:T(8,128)(2,1)} %get-tuple-element.86), channel_id=1, source_target_pairs={{0,8},{8,0},{16,24},{24,16},{1,9},{9,1},{17,25},{25,17},{2,10},{10... | collective-permute-start | bytes 2359304 | tf_op jit(solution)/shard_map/ppermute | solution.py:779
  179.4 66.5 %collective-permute-start.14 = (bf16[256,1536]{1,0:T(8,128)(2,1)}, bf16[256,1536]{1,0:T(8,128)(2,1)S(1)}, u32[]{:S(2)}, u32[]{:S(2)}) collective-permute-start(bf16[256,1536]{1,0:T(8,128)(2,1)} %get-tuple-element.87), channel_id=1, source_target_pairs={{0,8},{8,0},{16,24},{24,16},{1,9},{9,1},{17,25},{25,17},{2,10},{10... | collective-permute-start | bytes 2359304 | tf_op jit(solution)/shard_map/ppermute | solution.py:779
  189.7 56.1 %copy-start.18 = (bf16[256,1536]{1,0:T(8,128)(2,1)}, bf16[256,1536]{1,0:T(8,128)(2,1)S(1)}, u32[]{:S(2)}) copy-start(bf16[256,1536]{1,0:T(8,128)(2,1)S(1)} %collective-permute-done.11.refs_3_) | copy-start | bytes 2359300
  189.7 56.1 %collective-permute-start.12 = (bf16[256,1536]{1,0:T(8,128)(2,1)S(1)}, bf16[256,1536]{1,0:T(8,128)(2,1)S(1)}, u32[]{:S(2)}, u32[]{:S(2)}) collective-permute-start(bf16[256,1536]{1,0:T(8,128)(2,1)S(1)} %get-tuple-element.85), channel_id=1, source_target_pairs={{0,16},{8,24},{16,0},{24,8},{1,17},{9,25},{17,1},{25,9},{2,18},{10... | collective-permute-start | bytes 2359304 | tf_op jit(solution)/shard_map/ppermute | solution.py:779
  230.1 15.8 %copy-start.17 = (bf16[256,1536]{1,0:T(8,128)(2,1)}, bf16[256,1536]{1,0:T(8,128)(2,1)S(1)}, u32[]{:S(2)}) copy-start(bf16[256,1536]{1,0:T(8,128)(2,1)S(1)} %collective-permute-done.13.refs_6_.refs_1_) | copy-start | bytes 2359300
  280.5 293.1 %reduce-scatter.7.cloned.1.call-start = ((), (), s32[]{:S(2)}) async-start(), calls=%async_computation.12 | async-start | bytes 2621440 | tf_op jit(solution)/shard_map/reduce_scatter | solution.py:867
  291.4 4.6 collective-permute-start.17
  329.9 246.8 %reduce-scatter.11.cloned.1.call-start = ((), (), s32[]{:S(2)}) async-start(), calls=%async_computation.14 | async-start | bytes 2359296 | tf_op jit(solution)/shard_map/reduce_scatter | solution.py:861
  335.1 15.0 %collective-permute-start.18 = (bf16[128,2048]{1,0:T(8,128)(2,1)}, bf16[128,2048]{1,0:T(8,128)(2,1)S(1)}, u32[]{:S(2)}, u32[]{:S(2)}) collective-permute-start(bf16[128,2048]{1,0:T(8,128)(2,1)} %get-tuple-element.98.refs_0_), channel_id=1, source_target_pairs={{0,8},{8,0},{16,24},{24,16},{1,9},{9,1},{17,25},{25,17},{2,10},{10... | collective-permute-start | bytes 1572872 | tf_op jit(solution)/shard_map/ppermute | solution.py:779
  336.5 23.0 %collective-permute-start.19 = (bf16[128,2048]{1,0:T(8,128)(2,1)}, bf16[128,2048]{1,0:T(8,128)(2,1)S(1)}, u32[]{:S(2)}, u32[]{:S(2)}) collective-permute-start(bf16[128,2048]{1,0:T(8,128)(2,1)} %get-tuple-element.98.refs_0_), channel_id=1, source_target_pairs={{0,16},{8,24},{16,0},{24,8},{1,17},{9,25},{17,1},{25,9},{2,18},{10... | collective-permute-start | bytes 1572872 | tf_op jit(solution)/shard_map/ppermute | solution.py:779
  338.0 21.5 %collective-permute-start.20 = (bf16[128,2048]{1,0:T(8,128)(2,1)}, bf16[128,2048]{1,0:T(8,128)(2,1)}, u32[]{:S(2)}, u32[]{:S(2)}) collective-permute-start(bf16[128,2048]{1,0:T(8,128)(2,1)} %get-tuple-element.98.refs_0_), channel_id=1, source_target_pairs={{0,24},{8,16},{16,8},{24,0},{1,25},{9,17},{17,9},{25,1},{2,26},{10... | collective-permute-start | bytes 1572872 | tf_op jit(solution)/shard_map/ppermute | solution.py:779
  350.1 9.4 %copy-start.7 = (bf16[128,2048]{1,0:T(8,128)(2,1)}, bf16[128,2048]{1,0:T(8,128)(2,1)S(1)}, u32[]{:S(2)}) copy-start(bf16[128,2048]{1,0:T(8,128)(2,1)S(1)} %collective-permute-done.18.refs_1_) | copy-start | bytes 1572868
  376.1 27.4 %collective-permute-start.28 = (bf16[1024,512]{1,0:T(8,128)(2,1)}, bf16[1024,512]{1,0:T(8,128)(2,1)}, u32[]{:S(2)}, u32[]{:S(2)}) collective-permute-start(bf16[1024,512]{1,0:T(8,128)(2,1)} %get-tuple-element.118), channel_id=1, source_target_pairs={{0,8},{8,0},{16,24},{24,16},{1,9},{9,1},{17,25},{25,17},{2,10},{10... | collective-permute-start | bytes 3145736 | tf_op jit(solution)/shard_map/ppermute | solution.py:779
  376.6 30.5 %collective-permute-start.30 = (bf16[1024,512]{1,0:T(8,128)(2,1)}, bf16[1024,512]{1,0:T(8,128)(2,1)}, u32[]{:S(2)}, u32[]{:S(2)}) collective-permute-start(bf16[1024,512]{1,0:T(8,128)(2,1)} %get-tuple-element.121), channel_id=1, source_target_pairs={{0,16},{8,24},{16,0},{24,8},{1,17},{9,25},{17,1},{25,9},{2,18},{10... | collective-permute-start | bytes 3145736 | tf_op jit(solution)/shard_map/ppermute | solution.py:779
  378.2 10.9 %copy-start.6 = (bf16[128,2048]{1,0:T(8,128)(2,1)S(1)}, bf16[128,2048]{1,0:T(8,128)(2,1)}, u32[]{:S(2)}) copy-start(bf16[128,2048]{1,0:T(8,128)(2,1)} %get-tuple-element.98.refs_0_) | copy-start | bytes 1572868
  378.2 10.9 %copy-start.8 = (bf16[128,2048]{1,0:T(8,128)(2,1)S(1)}, bf16[128,2048]{1,0:T(8,128)(2,1)}, u32[]{:S(2)}) copy-start(bf16[128,2048]{1,0:T(8,128)(2,1)} %copy-done.7) | copy-start | bytes 1572868
  387.6 41.5 %collective-permute-start.32 = (bf16[1024,512]{1,0:T(8,128)(2,1)}, bf16[1024,512]{1,0:T(8,128)(2,1)}, u32[]{:S(2)}, u32[]{:S(2)}) collective-permute-start(bf16[1024,512]{1,0:T(8,128)(2,1)} %get-tuple-element.124), channel_id=1, source_target_pairs={{0,8},{8,0},{16,24},{24,16},{1,9},{9,1},{17,25},{25,17},{2,10},{10... | collective-permute-start | bytes 3145736 | tf_op jit(solution)/shard_map/ppermute | solution.py:779
  392.7 40.0 %all-to-all-start.1 = ((bf16[32,64,128]{2,1,0:T(8,128)(2,1)}), bf16[32,64,128]{2,1,0:T(8,128)(2,1)}, u32[]{:S(2)}, u32[]{:S(2)}) async-start(bf16[32,64,128]{2,1,0:T(8,128)(2,1)} %bitcast.18), calls=%async_computation.3 | async-start | bytes 1048576 | tf_op jit(solution)/shard_map/all_to_all | solution.py:874
  396.1 222.8 %reduce-scatter.9.cloned.1.call-start = ((), (), s32[]{:S(2)}) async-start(), calls=%async_computation.13 | async-start | bytes 4718592 | tf_op jit(solution)/shard_map/reduce_scatter | solution.py:861
  396.3 57.4 %collective-permute-start.34 = (bf16[1024,512]{1,0:T(8,128)(2,1)}, bf16[1024,512]{1,0:T(8,128)(2,1)S(1)}, u32[]{:S(2)}, u32[]{:S(2)}) collective-permute-start(bf16[1024,512]{1,0:T(8,128)(2,1)} %get-tuple-element.127), channel_id=1, source_target_pairs={{0,16},{8,24},{16,0},{24,8},{1,17},{9,25},{17,1},{25,9},{2,18},{10... | collective-permute-start | bytes 3145736 | tf_op jit(solution)/shard_map/ppermute | solution.py:779
  405.6 50.1 %collective-permute-start.29 = (bf16[512,512]{1,0:T(8,128)(2,1)}, bf16[512,512]{1,0:T(8,128)(2,1)}, u32[]{:S(2)}, u32[]{:S(2)}) collective-permute-start(bf16[512,512]{1,0:T(8,128)(2,1)} %add_convert_fusion.9), channel_id=1, source_target_pairs={{0,16},{8,24},{16,0},{24,8},{1,17},{9,25},{17,1},{25,9},{2,18},{10... | collective-permute-start | bytes 1572872 | tf_op jit(solution)/shard_map/ppermute | solution.py:779
  409.3 48.0 %collective-permute-start.31 = (bf16[512,512]{1,0:T(8,128)(2,1)}, bf16[512,512]{1,0:T(8,128)(2,1)}, u32[]{:S(2)}, u32[]{:S(2)}) collective-permute-start(bf16[512,512]{1,0:T(8,128)(2,1)} %add_convert_fusion.7), channel_id=1, source_target_pairs={{0,8},{8,0},{16,24},{24,16},{1,9},{9,1},{17,25},{25,17},{2,10},{10... | collective-permute-start | bytes 1572872 | tf_op jit(solution)/shard_map/ppermute | solution.py:779
  431.3 27.7 %collective-permute-start.33 = (bf16[512,512]{1,0:T(8,128)(2,1)}, bf16[512,512]{1,0:T(8,128)(2,1)}, u32[]{:S(2)}, u32[]{:S(2)}) collective-permute-start(bf16[512,512]{1,0:T(8,128)(2,1)} %add_convert_fusion.5), channel_id=1, source_target_pairs={{0,16},{8,24},{16,0},{24,8},{1,17},{9,25},{17,1},{25,9},{2,18},{10... | collective-permute-start | bytes 1572872 | tf_op jit(solution)/shard_map/ppermute | solution.py:779
  453.8 3.5 copy-start.10
  455.0 11.7 %collective-permute-start.35 = (bf16[512,512]{1,0:T(8,128)(2,1)S(1)}, bf16[512,512]{1,0:T(8,128)(2,1)S(1)}, u32[]{:S(2)}, u32[]{:S(2)}) collective-permute-start(bf16[512,512]{1,0:T(8,128)(2,1)S(1)} %add_convert_fusion.3), channel_id=1, source_target_pairs={{0,8},{8,0},{16,24},{24,16},{1,9},{9,1},{17,25},{25,17},{2,10},{10... | collective-permute-start | bytes 1572872 | tf_op jit(solution)/shard_map/ppermute | solution.py:779
  455.7 3.3 copy-start.12
  457.3 9.4 %copy-start.11 = (bf16[512,512]{1,0:T(8,128)(2,1)S(1)}, bf16[512,512]{1,0:T(8,128)(2,1)}, u32[]{:S(2)}) copy-start(bf16[512,512]{1,0:T(8,128)(2,1)} %get-tuple-element.126) | copy-start | bytes 1572868
  468.6 94.8 %all-to-all-start.3 = ((bf16[8,64,2048]{2,1,0:T(8,128)(2,1)}), bf16[8,64,2048]{2,1,0:T(8,128)(2,1)}, u32[]{:S(2)}, u32[]{:S(2)}) async-start(bf16[8,64,2048]{2,1,0:T(8,128)(2,1)} %bitcast.48), calls=%async_computation.7 | async-start | bytes 4194304 | tf_op jit(solution)/shard_map/all_to_all | solution.py:874
  482.4 25.6 %collective-permute-start.21 = (bf16[1024,512]{1,0:T(8,128)(2,1)}, bf16[1024,512]{1,0:T(8,128)(2,1)S(1)}, u32[]{:S(2)}, u32[]{:S(2)}) collective-permute-start(bf16[1024,512]{1,0:T(8,128)(2,1)} %get-tuple-element.106), channel_id=1, source_target_pairs={{0,8},{8,0},{16,24},{24,16},{1,9},{9,1},{17,25},{25,17},{2,10},{10... | collective-permute-start | bytes 3145736 | tf_op jit(solution)/shard_map/ppermute | solution.py:779
  483.3 28.3 %collective-permute-start.23 = (bf16[1024,512]{1,0:T(8,128)(2,1)}, bf16[1024,512]{1,0:T(8,128)(2,1)S(1)}, u32[]{:S(2)}, u32[]{:S(2)}) collective-permute-start(bf16[1024,512]{1,0:T(8,128)(2,1)} %get-tuple-element.109), channel_id=1, source_target_pairs={{0,16},{8,24},{16,0},{24,8},{1,17},{9,25},{17,1},{25,9},{2,18},{10... | collective-permute-start | bytes 3145736 | tf_op jit(solution)/shard_map/ppermute | solution.py:779
  508.0 3.7 copy-start.4
  510.4 16.8 %collective-permute-start.22 = (bf16[512,512]{1,0:T(8,128)(2,1)}, bf16[512,512]{1,0:T(8,128)(2,1)}, u32[]{:S(2)}, u32[]{:S(2)}) collective-permute-start(bf16[512,512]{1,0:T(8,128)(2,1)} %add_convert_fusion.13), channel_id=1, source_target_pairs={{0,16},{8,24},{16,0},{24,8},{1,17},{9,25},{17,1},{25,9},{2,18},{10... | collective-permute-start | bytes 1572872 | tf_op jit(solution)/shard_map/ppermute | solution.py:779
  513.6 15.2 %collective-permute-start.24 = (bf16[512,512]{1,0:T(8,128)(2,1)}, bf16[512,512]{1,0:T(8,128)(2,1)}, u32[]{:S(2)}, u32[]{:S(2)}) collective-permute-start(bf16[512,512]{1,0:T(8,128)(2,1)} %add_convert_fusion.11), channel_id=1, source_target_pairs={{0,8},{8,0},{16,24},{24,16},{1,9},{9,1},{17,25},{25,17},{2,10},{10... | collective-permute-start | bytes 1572872 | tf_op jit(solution)/shard_map/ppermute | solution.py:779
  523.7 5.1 copy-start.13
  523.7 21.5 %collective-permute-start.25 = (bf16[512,768]{1,0:T(8,128)(2,1)}, bf16[512,768]{1,0:T(8,128)(2,1)S(1)}, u32[]{:S(2)}, u32[]{:S(2)}) collective-permute-start(bf16[512,768]{1,0:T(8,128)(2,1)} %get-tuple-element.112), channel_id=1, source_target_pairs={{0,8},{8,0},{16,24},{24,16},{1,9},{9,1},{17,25},{25,17},{2,10},{10... | collective-permute-start | bytes 2359304 | tf_op jit(solution)/shard_map/ppermute | solution.py:779
  525.4 35.6 %collective-permute-start.26 = (bf16[512,768]{1,0:T(8,128)(2,1)}, bf16[512,768]{1,0:T(8,128)(2,1)S(1)}, u32[]{:S(2)}, u32[]{:S(2)}) collective-permute-start(bf16[512,768]{1,0:T(8,128)(2,1)} %get-tuple-element.113), channel_id=1, source_target_pairs={{0,24},{8,16},{16,8},{24,0},{1,25},{9,17},{17,9},{25,1},{2,26},{10... | collective-permute-start | bytes 2359304 | tf_op jit(solution)/shard_map/ppermute | solution.py:779
  526.6 35.1 %collective-permute-start.27 = (bf16[512,768]{1,0:T(8,128)(2,1)}, bf16[512,768]{1,0:T(8,128)(2,1)S(1)}, u32[]{:S(2)}, u32[]{:S(2)}) collective-permute-start(bf16[512,768]{1,0:T(8,128)(2,1)} %get-tuple-element.114), channel_id=1, source_target_pairs={{0,16},{8,24},{16,0},{24,8},{1,17},{9,25},{17,1},{25,9},{2,18},{10... | collective-permute-start | bytes 2359304 | tf_op jit(solution)/shard_map/ppermute | solution.py:779
  527.2 34.5 %copy-start.5 = (bf16[512,768]{1,0:T(8,128)(2,1)S(1)}, bf16[512,768]{1,0:T(8,128)(2,1)}, u32[]{:S(2)}) copy-start(bf16[512,768]{1,0:T(8,128)(2,1)} %get-tuple-element.111) | copy-start | bytes 2359300
  563.4 48.0 %all-to-all-start.2 = ((bf16[8,64,1792]{2,1,0:T(8,128)(2,1)}), bf16[8,64,1792]{2,1,0:T(8,128)(2,1)}, u32[]{:S(2)}, u32[]{:S(2)}) async-start(bf16[8,64,1792]{2,1,0:T(8,128)(2,1)} %bitcast.49), calls=%async_computation.5 | async-start | bytes 3670016 | tf_op jit(solution)/shard_map/all_to_all | solution.py:874
  (5 other events, 5.4 us)
Sparse Core Ops, SparseCore 0:
  11.6 49.5 all-gather.3
  77.4 53.6 all-gather.7
  136.0 49.3 all-gather.5
  280.6 49.2 reduce-scatter.4
  332.0 42.1 reduce-scatter.6
  376.3 40.3 reduce-scatter.10
  453.9 73.5 reduce-scatter.8

commit v3 on v2

--- a/solution.py
+++ b/solution.py
@@ -350,44 +350,68 @@
     return jnp.sum(values.T, axis=0, keepdims=True)
 
 
-def strided_rows_kernel(first, which_ref, in_ref, weight_ref, gain_ref, out_ref, sum_ref):
+def last_rows_kernel(
+    piece, which_ref, in_ref, up_ref, qkv_ref, gain1_ref, gain2_ref, part_ref, before_ref,
+    out_ref, sum2_ref, strided_ref, sum1_ref,
+):
     groups, rows, width = in_ref.shape
+
+    def step(s, total):
+        values = in_ref[s, :, :piece].astype(F32)
+        cols = pl.ds(pl.multiple_of(s * piece, piece), piece)
+        out_ref[:, cols] = values
+        product = values * up_ref[:, cols].astype(F32)
+        for c in range(piece // 128):
+            total = total + product[:, c * 128 : (c + 1) * 128]
+        return total
+
+    total = lax.fori_loop(0, groups, step, jnp.zeros((rows, 128), F32))
+    sum2_ref[...] = part_ref[...] + lane_sums(total) / gain2_ref[...]
+
     total = jnp.zeros((rows, 128), F32)
-    for b in range((width - first) // HD):
-        cols = slice(first + b * HD, first + (b + 1) * HD)
+    for b in range((width - piece) // HD):
+        cols = slice(piece + b * HD, piece + (b + 1) * HD)
         for pair in range(groups // 2):
             both = jnp.concatenate(
                 [in_ref[2 * pair, :, cols], in_ref[2 * pair + 1, :, cols]], 1
             ).astype(F32)
             at = (b * groups + 2 * pair) * HD
-            out_ref[:, at : at + 128] = both
-            total = total + both * weight_ref[:, at : at + 128].astype(F32)
-    sum_ref[...] = lane_sums(total) / gain_ref[...]
-
-
-def strided_rows(parts, first, weight, gain, group):
-    _, rows, _ = parts.shape
+            strided_ref[:, at : at + 128] = both
+            total = total + both * qkv_ref[:, at : at + 128].astype(F32)
+    sum1_ref[...] = lane_sums(total) / gain1_ref[...]
+
+
+def last_rows(parts, piece, up_weight, qkv_weight, gain1, gain2, part, before, group):
+    groups, rows, _ = parts.shape
+    half = groups * piece
+
+    def spec(columns, row=False, place=0):
+        return pl.BlockSpec((rows, columns), lambda g, w: (w[0] if row else 0, place))
+
+    line = pl.BlockSpec((1, rows), lambda g, w: (0, 0))
     return pl.pallas_call(
-        functools.partial(strided_rows_kernel, first),
+        functools.partial(last_rows_kernel, piece),
         grid_spec=pltpu.PrefetchScalarGridSpec(
             num_scalar_prefetch=1,
             grid=(1,),
             in_specs=[
                 pl.BlockSpec(parts.shape, lambda g, w: (0, 0, 0)),
-                pl.BlockSpec((rows, weight.shape[1]), lambda g, w: (w[0], 0)),
-                pl.BlockSpec((1, rows), lambda g, w: (0, 0)),
+                spec(half, True, 1),
+                spec(qkv_weight.shape[1], True),
+                line, line, line,
+                pl.BlockSpec(memory_space=pl.ANY),
             ],
-            out_specs=[
-                pl.BlockSpec((rows, weight.shape[1]), lambda g, w: (0, 0)),
-                pl.BlockSpec((1, rows), lambda g, w: (0, 0)),
-            ],
+            out_specs=[spec(half, False, 1), line, spec(qkv_weight.shape[1]), line],
         ),
         out_shape=[
-            jax.ShapeDtypeStruct((rows, weight.shape[1]), F32),
+            jax.ShapeDtypeStruct((rows, 2 * half), F32),
+            jax.ShapeDtypeStruct((1, rows), F32),
+            jax.ShapeDtypeStruct((rows, qkv_weight.shape[1]), F32),
             jax.ShapeDtypeStruct((1, rows), F32),
         ],
-        name="strided_rows",
-    )(group.reshape(1), parts, weight, gain)
+        input_output_aliases={7: 0},
+        name="last_rows",
+    )(group.reshape(1), parts, up_weight, qkv_weight, gain1, gain2, part, before)
 
 
 def side_rows_kernel(runs, which_ref, *refs):
@@ -415,9 +439,10 @@
             sum_ref[...] += lane_sums(total) / gain_ref[...]
 
 
-def side_rows(parts, piece, weight, gain, group):
+def side_rows(parts, piece, weight, gain, group, columns=None):
     groups, rows, _ = parts[0][0].shape
     runs = len(parts)
+    columns = columns or runs * groups * piece
 
     def spec(place):
         return pl.BlockSpec((groups, rows, piece), lambda c, w: (0, 0, place))
@@ -438,7 +463,7 @@
             ],
         ),
         out_shape=[
-            jax.ShapeDtypeStruct((rows, runs * groups * piece), F32),
+            jax.ShapeDtypeStruct((rows, columns), F32),
             jax.ShapeDtypeStruct((1, rows), F32),
         ],
         name="side_rows",
@@ -729,6 +754,41 @@
     )(group.reshape(1), act, *pieces)
 
 
+def project_kernel(members_ref, features_ref, weight_ref, own_ref, *other_refs):
+    product = contract_first(features_ref[0], weight_ref[...])
+
+    @pl.when(pl.program_id(0) == 0)
+    def _():
+        own_ref[...] = product
+
+    for k, other in enumerate(other_refs):
+
+        @pl.when(pl.program_id(0) == k + 1)
+        def _():
+            other[...] = product.astype(BF)
+
+
+def project(features, weight, members):
+    _, count, tokens = features.shape
+    width = weight.shape[1]
+    place = pl.BlockSpec((tokens, width), lambda k, m: (0, 0))
+    return pl.pallas_call(
+        project_kernel,
+        grid_spec=pltpu.PrefetchScalarGridSpec(
+            num_scalar_prefetch=1,
+            grid=(4,),
+            in_specs=[
+                pl.BlockSpec((1, count, tokens), lambda k, m: (m[k], 0, 0)),
+                pl.BlockSpec(weight.shape, lambda k, m: (0, 0)),
+            ],
+            out_specs=[place] * 4,
+        ),
+        out_shape=[jax.ShapeDtypeStruct((tokens, width), F32)]
+        + [jax.ShapeDtypeStruct((tokens, width), BF)] * 3,
+        name="project",
+    )(members, features, weight)
+
+
 def rows_by_member(pieces, places_ref, target_ref, sems):
     height = pieces[0].shape[0]
     copies = [
@@ -981,13 +1041,8 @@
 
     features = to_features(attn)
     if quad:
-        parts = [
-            contract_first(
-                lax.dynamic_index_in_dim(features, member ^ k, 0, False), out_weight
-            )
-            for k in range(4)
-        ]
-        others = [partner(parts[k].astype(BF), k) for k in (1, 2, 3)]
+        parts = project(features, out_weight, blocks_at ^ member)
+        others = [partner(parts[k], k) for k in (1, 2, 3)]
         partials = (parts[0], *others)
     else:
         partials = (
@@ -1049,11 +1104,14 @@
             "kft,ktn->fn", features, jnp.stack(rows_low), preferred_element_type=F32
         ).astype(BF)
     out_grad = sum_over_seq(out_rows).astype(F32)
-    grad_qkv, partial_xn1 = attention_backward(
-        group, False,
+    grad_qkv, *partial_xn1 = attention_backward(
+        group, quad is not None,
         query, key, value, attn, grad_attn, lse, cosine, sine, qkv_pieces, per_row,
     )
-    raw_xn1 = sum_over_seq(partial_xn1)
+    if quad:
+        raw_xn1 = sum_over_pairs(*partial_xn1, group_count)
+    else:
+        raw_xn1 = sum_over_seq(partial_xn1[0])
     (input_grad,) = on_rows(
         norm_grad_kernel, places, (layer_in, grad_hidden, raw_xn1, gain1), (F32,)
     )
@@ -1073,12 +1131,17 @@
     own1 = lax.dynamic_slice_in_dim(gain1, own_at, shard_rows, 1)
     own2 = lax.dynamic_slice_in_dim(gain2, own_at, shard_rows, 1)
     down_grad, _ = side_rows([(near_parts, 0)], hidden, down_weight, own2, group)
-    gate_up_grad, norm2_grad = side_rows(
-        [(near_parts, 1), (far_parts, 0)], hidden, gate_up_weight, own2, group
-    )
     if strided:
-        qkv_grad, norm1_grad = strided_rows(far_parts, hidden, qkv_weight, own1, group)
-    else:
+        before, part = side_rows(
+            [(near_parts, 1)], hidden, gate_up_weight, own2, group, 2 * hidden_units
+        )
+        gate_up_grad, norm2_grad, qkv_grad, norm1_grad = last_rows(
+            far_parts, hidden, gate_up_weight, qkv_weight, own1, own2, part, before, group
+        )
+    else:
+        gate_up_grad, norm2_grad = side_rows(
+            [(near_parts, 1), (far_parts, 0)], hidden, gate_up_weight, own2, group
+        )
         qkv_parts = far_parts[:, :, hidden:]
         qkv_grad, norm1_grad = side_rows(
             [(qkv_parts, i) for i in range(3)], width, qkv_weight, own1, group

time: 632 us -> 635 us (level)
  starting transfers between devices: 62.5 us -> 54 us
  Pallas kernels: 162 us -> 169 us
  other arithmetic: 32 us -> 38.7 us
  matrix products: 7.77 us -> 1.29 us
    ppermute x35, starting transfers between devices: 46.2 us -> 38.5 us  [partner(): return lax.ppermute(array, 'dp', [(i, i ^ bits) for i in range(4)])]
    pallas_call x1 -> x2, Pallas kernels: 3.19 us -> 10.6 us  [the longest x1 6.4 us: project(): pl.pallas_call(project_kernel, grid_spec=pltpu.PrefetchScalarGridSpec(num...]
    convert_element_type x14 -> x15, other arithmetic: 23.8 us -> 30.1 us  [add(): return total.astype(BF)]
    reduce_scatter x3 -> x2, waiting for transfers between devices: 30.2 us -> 29.7 us  [sum_over_seq(): lax.psum_scatter(values.astype(BF), 'seq', scatter_dimension=0, tiled=True)]
  transfers between devices with their start and end apart: 47 -> 48, of which waited for: 24 -> 26; matrix products, arithmetic and copies ran while one was open for 8% -> 8% of each run, Pallas kernels for 17% -> 18%
where the time goes in v3:
time: 635 us; the launch traced here: 634 us
  waiting for transfers between devices  338 us (53%)
  Pallas kernels  169 us (27%)
  starting transfers between devices  54 us (9%)
  other arithmetic  38.7 us (6%)
  local copies, waits for them, and re-layouts  18.4 us (3%)
  between operations  14.5 us (2%)
    ppermute x35, waiting for transfers between devices, partner(): return lax.ppermute(array, 'dp', [(i, i ^ bits) for i in range(4)])  231 us
    all_to_all x4, waiting for transfers between devices, exchange(): return lax.all_to_all(values, axes, split_axis=0, concat_axis=0, tiled=True)  60.8 us
    ppermute x35, starting transfers between devices, partner(): return lax.ppermute(array, 'dp', [(i, i ^ bits) for i in range(4)])  38.5 us
    pallas_call x4, Pallas kernels, outer_blocks(): pl.pallas_call(functools.partial(outer_kernel, layouts), grid=(4 * steps,...  37.9 us
    pallas_call x1, Pallas kernels, feed_forward(): pl.pallas_call(functools.partial(feed_kernel, len(part_a), len(part_b)),...  32.3 us
    convert_element_type x15, other arithmetic, add(): return total.astype(BF)  30.1 us
    reduce_scatter x2, waiting for transfers between devices, sum_over_seq(): lax.psum_scatter(values.astype(BF), 'seq', scatter_dimension=0, tiled=True)  29.7 us
    pallas_call x1, Pallas kernels, attention_backward(): pl.pallas_call(functools.partial(attention_backward_kernel, block, len(pi...  21.7 us
  transfers between devices with their start and end apart: 48, of which 26 were waited for; matrix products, arithmetic and copies ran while one was open for 8% of the time, Pallas kernels for 18%

profile of v3, /device:TPU:0, one launch (start us, length us, event | category | flops | bytes accessed | tf_op | source)
XLA Modules:
  0.0 633.5 jit_solution(5283364366077631350)
XLA Ops:
  7.7 3.6 shard_map.143
  11.4 2.7 strided_heads.1
  14.1 3.0 collective-permute-start.2
  19.1 2.2 constant_dynamic-slice_fusion.2
  21.4 2.3 constant_dynamic-slice_fusion.3
  23.7 2.3 constant_dynamic-slice_fusion.1
  25.9 10.4 %collective-permute-done.refs_2_ = bf16[512,384]{1,0:T(8,128)(2,1)} collective-permute-done((bf16[512,384]{1,0:T(8,128)(2,1)}, bf16[512,384]{1,0:T(8,128)(2,1)}, u32[]{:S(2)}, u32[]{:S(2)}) %collective-permute-start) | collective-permute-done | bytes 393248 | tf_op jit(solution)/shard_map/ppermute | solution.py:839
  39.0 4.3 rotary.1
  43.3 2.1 pad_maximum_fusion.2
  49.2 11.9 %all-gather.4.cloned.1.call-done.xn_ref.left_ref = bf16[1024,2048]{1,0:T(8,128)(2,1)} async-done(((bf16[128,2048]{1,0:T(8,128)(2,1)}), bf16[1024,2048]{1,0:T(8,128)(2,1)}) %all-gather.4.cloned.1.call-update) | async-done | bytes 4194320 | tf_op jit(solution)/shard_map/all_gather | solution.py:917
  61.1 16.0 %attention_forward.1 = (bf16[4,8,64,128]{3,2,1,0:T(8,128)(2,1)}, bf16[1024,256]{1,0:T(8,128)(2,1)}, bf16[1024,256]{1,0:T(8,128)(2,1)}, bf16[1024,256]{1,0:T(8,128)(2,1)}, f32[8,1024]{1,0:T(8,128)}) custom-call(bf16[1024,2048]{1,0:T(8,128)(2,1)} %all-gather.4.cloned.1.call-done.xn_ref.left_ref, bf16[512,384]{1,0:T(8,128)(2,1)} %get-tuple-element.78.refs_0_, ...), custom_call_target="tpu_custom_call" | custom-call | flops 3758096384 | bytes 9437184 | tf_op jit(solution)/shard_map/attention_forward/pallas_call | solution.py:238
  77.1 3.5 all-to-all-start
  81.2 24.5 %all-to-all-done = bf16[32,64,128]{2,1,0:T(8,128)(2,1)} async-done(((bf16[32,64,128]{2,1,0:T(8,128)(2,1)}), bf16[32,64,128]{2,1,0:T(8,128)(2,1)}, u32[]{:S(2)}, u32[]{:S(2)}) %all-to-all-start) | async-done | bytes 524320 | tf_op jit(solution)/shard_map/all_to_all | solution.py:934
  105.7 6.4 %project.1 = (f32[128,2048]{1,0:T(8,128)}, bf16[128,2048]{1,0:T(8,128)(2,1)}, bf16[128,2048]{1,0:T(8,128)(2,1)}, bf16[128,2048]{1,0:T(8,128)(2,1)}) custom-call(s32[4]{0:T(128)} %iota_xor_fusion.members_ref, bf16[4,512,128]{2,1,0:T(8,128)(2,1)} %bitcast.3.features_ref, bf16[512,2048]{1,0:T(8,128)(2,1)} %weight_ref.1), custom_call_target="tpu_custom_call" | custom-call | tf_op jit(solution)/shard_map/project/pallas_call | solution.py:775
  113.2 2.3 collective-permute-start.8
  115.6 10.6 %collective-permute-done.6.refs_1_ = bf16[128,2048]{1,0:T(8,128)(2,1)} collective-permute-done((bf16[128,2048]{1,0:T(8,128)(2,1)}, bf16[128,2048]{1,0:T(8,128)(2,1)}, u32[]{:S(2)}, u32[]{:S(2)}) %collective-permute-start.6) | collective-permute-done | bytes 524320 | tf_op jit(solution)/shard_map/ppermute | solution.py:839
  126.2 10.3 %collective-permute-done.8.refs_3_ = bf16[128,2048]{1,0:T(8,128)(2,1)} collective-permute-done((bf16[128,2048]{1,0:T(8,128)(2,1)}, bf16[128,2048]{1,0:T(8,128)(2,1)}, u32[]{:S(2)}, u32[]{:S(2)}) %collective-permute-start.8) | collective-permute-done | bytes 524320 | tf_op jit(solution)/shard_map/ppermute | solution.py:839
  136.4 4.5 shard_map.144
  141.0 3.4 collective-permute-start.9
  144.3 2.0 collective-permute-start.11
  146.4 33.1 %collective-permute-done.9.refs_1_ = bf16[512,1536]{1,0:T(8,128)(2,1)S(1)} collective-permute-done((bf16[512,1536]{1,0:T(8,128)(2,1)S(1)}, bf16[512,1536]{1,0:T(8,128)(2,1)S(1)}, u32[]{:S(2)}, u32[]{:S(2)}) %collective-permute-start.9) | collective-permute-done | bytes 1572896 | tf_op jit(solution)/shard_map/ppermute | solution.py:839
  183.0 1.9 collective-permute-start.13
  184.9 13.6 %collective-permute-done.11.refs_3_ = bf16[256,1536]{1,0:T(8,128)(2,1)S(1)} collective-permute-done((bf16[256,1536]{1,0:T(8,128)(2,1)}, bf16[256,1536]{1,0:T(8,128)(2,1)S(1)}, u32[]{:S(2)}, u32[]{:S(2)}) %collective-permute-start.11) | collective-permute-done | bytes 786464 | tf_op jit(solution)/shard_map/ppermute | solution.py:839
  198.5 38.4 %collective-permute-done.13.refs_6_.refs_1_ = bf16[256,1536]{1,0:T(8,128)(2,1)S(1)} collective-permute-done((bf16[256,1536]{1,0:T(8,128)(2,1)}, bf16[256,1536]{1,0:T(8,128)(2,1)S(1)}, u32[]{:S(2)}, u32[]{:S(2)}) %collective-permute-start.13) | collective-permute-done | bytes 786464 | tf_op jit(solution)/shard_map/ppermute | solution.py:839
  237.0 11.4 %collective-permute-done.12.refs_4_ = bf16[256,1536]{1,0:T(8,128)(2,1)S(1)} collective-permute-done((bf16[256,1536]{1,0:T(8,128)(2,1)}, bf16[256,1536]{1,0:T(8,128)(2,1)S(1)}, u32[]{:S(2)}, u32[]{:S(2)}) %collective-permute-start.12) | collective-permute-done | bytes 786464 | tf_op jit(solution)/shard_map/ppermute | solution.py:839
  248.3 3.4 collective-permute-done.14.refs_7_.refs_2_
  254.4 32.3 %feed_forward.1 = (bf16[1024,1024]{1,0:T(8,128)(2,1)}, bf16[1024,2048]{1,0:T(8,128)(2,1)}, bf16[1024,2048]{1,0:T(8,128)(2,1)}) custom-call(bf16[1024,2048]{1,0:T(8,128)(2,1)} %all-gather.6.cloned.1.call-done.xn_ref.left_ref, bf16[1024,2048]{1,0:T(8,128)(2,1)} %all-gather.8.cloned.1.call-done.dy_ref.left_ref, bf16[512,1536]{1,0:T(8,128)(2,1)} %copy-done.2, ...), custom_call_target="tpu_custom_call" | custom-call | flops 21474836480 | bytes 29360128 | tf_op jit(solution)/shard_map/feed_forward/pallas_call | solution.py:686
  286.9 10.6 %feed_out.1 = (bf16[512,2048]{1,0:T(8,128)(2,1)}, bf16[512,2048]{1,0:T(8,128)(2,1)}) custom-call(s32[1]{0:T(128)} %bitcast.1.which_ref.group_ref, bf16[1024,1024]{1,0:T(8,128)(2,1)} %get-tuple-element.102.act_ref.right_ref, bf16[512,1536]{1,0:T(8,128)(2,1)} %copy-done.1, bf16[256,1536]{1,0:T(8,128)(2,1)} %copy-done.21, bf16[256,1536]{1,0:T(8,128)(2,1)} %copy-done.23, ...), custom_call_target="tpu_custom_call" | custom-call | flops 4294967296 | bytes 10485760 | tf_op jit(solution)/shard_map/feed_out/pallas_call | solution.py:735
  297.6 4.5 collective-permute-done.17
  302.2 3.7 add_convert_fusion.1
  305.9 29.7 %reduce-scatter.5.cloned.1.call-done.refs_1_ = bf16[128,2048]{1,0:T(8,128)(2,1)} async-done(((bf16[1024,2048]{1,0:T(8,128)(2,1)}), bf16[128,2048]{1,0:T(8,128)(2,1)}) %reduce-scatter.5.cloned.1.call-update) | async-done | bytes 524304 | tf_op jit(solution)/shard_map/reduce_scatter | solution.py:921
  335.6 9.4 %outer_blocks.7 = (bf16[1024,512]{1,0:T(8,128)(2,1)}, bf16[512,512]{1,0:T(8,128)(2,1)}, bf16[512,512]{1,0:T(8,128)(2,1)}, bf16[1024,512]{1,0:T(8,128)(2,1)}, bf1...) custom-call(bf16[1024,2048]{1,0:T(8,128)(2,1)} %all-gather.6.cloned.1.call-done.xn_ref.left_ref, ...), custom_call_target="tpu_custom_call" | custom-call | flops 4294967296 | bytes 10485760 | tf_op jit(solution)/shard_map/outer_blocks/pallas_call | solution.py:652
  348.0 9.4 %outer_blocks.6 = (bf16[1024,512]{1,0:T(8,128)(2,1)}, bf16[512,512]{1,0:T(8,128)(2,1)}, bf16[512,512]{1,0:T(8,128)(2,1)}, bf16[1024,512]{1,0:T(8,128)(2,1)}, bf1...) custom-call(bf16[1024,2048]{1,0:T(8,128)(2,1)} %all-gather.8.cloned.1.call-done.dy_ref.left_ref, ...), custom_call_target="tpu_custom_call" | custom-call | flops 4294967296 | bytes 10485760 | tf_op jit(solution)/shard_map/outer_blocks/pallas_call | solution.py:652
  358.9 12.4 %collective-permute-done.35 = bf16[1024,512]{1,0:T(8,128)(2,1)} collective-permute-done((bf16[1024,512]{1,0:T(8,128)(2,1)}, bf16[1024,512]{1,0:T(8,128)(2,1)}, u32[]{:S(2)}, u32[]{:S(2)}) %collective-permute-start.35) | collective-permute-done | bytes 1048608 | tf_op jit(solution)/shard_map/ppermute | solution.py:839
  371.3 2.1 add_convert_fusion.4
  374.9 2.0 add_convert_fusion.6
  378.4 15.3 %collective-permute-done.31 = bf16[1024,512]{1,0:T(8,128)(2,1)S(1)} collective-permute-done((bf16[1024,512]{1,0:T(8,128)(2,1)}, bf16[1024,512]{1,0:T(8,128)(2,1)S(1)}, u32[]{:S(2)}, u32[]{:S(2)}) %collective-permute-start.31) | collective-permute-done | bytes 1048608 | tf_op jit(solution)/shard_map/ppermute | solution.py:839
  394.8 4.5 shard_map.145
  399.3 2.5 collective-permute-start.20
  402.8 2.0 add_convert_fusion.10
  409.6 8.1 %collective-permute-done.20.refs_3_ = bf16[128,2048]{1,0:T(8,128)(2,1)S(1)} collective-permute-done((bf16[128,2048]{1,0:T(8,128)(2,1)}, bf16[128,2048]{1,0:T(8,128)(2,1)S(1)}, u32[]{:S(2)}, u32[]{:S(2)}) %collective-permute-start.20) | collective-permute-done | bytes 524320 | tf_op jit(solution)/shard_map/ppermute | solution.py:839
  419.2 8.3 %collective-permute-done.19.refs_2_ = bf16[128,2048]{1,0:T(8,128)(2,1)S(1)} collective-permute-done((bf16[128,2048]{1,0:T(8,128)(2,1)}, bf16[128,2048]{1,0:T(8,128)(2,1)S(1)}, u32[]{:S(2)}, u32[]{:S(2)}) %collective-permute-start.19) | collective-permute-done | bytes 524320 | tf_op jit(solution)/shard_map/ppermute | solution.py:839
  431.4 2.6 all-to-all-start.1
  434.1 6.4 %out_rows.1 = bf16[512,2048]{1,0:T(8,128)(2,1)} custom-call(s32[4]{0:T(128)} %iota_xor_fusion.members_ref, bf16[4,512,128]{2,1,0:T(8,128)(2,1)} %bitcast.3.features_ref, bf16[128,2048]{1,0:T(8,128)(2,1)} %get-tuple-element.109.refs_0_, bf16[128,2048]{1,0:T(8,128)(2,1)} %copy-done.12, bf16[128,2048]{1,0:T(8,128)(2,1)} %copy-done.11, bf16[128,2048]{1,0:T(8,128)(2,1)} %copy-done.10), custom_call_target="tpu_custom_call" | custom-call | tf_op jit(solution)/shard_map/out_rows/pallas_call | solution.py:823
  446.4 3.9 all-to-all-done.1
  451.0 3.6 all-to-all-start.3
  454.9 21.7 %attention_backward.1 = (bf16[1024,768]{1,0:T(8,128)(2,1)}, bf16[512,2048]{1,0:T(8,128)(2,1)}, bf16[512,2048]{1,0:T(8,128)(2,1)}) custom-call(s32[1]{0:T(128)} %bitcast.1.which_ref.group_ref, bf16[1024,256]{1,0:T(8,128)(2,1)} %get-tuple-element.106.q_ref, bf16[1024,256]{1,0:T(8,128)(2,1)} %get-tuple-element.107.k_ref, ...), custom_call_target="tpu_custom_call" | custom-call | flops 4563402752 | bytes 12582912 | tf_op jit(solution)/shard_map/attention_backward/pallas_call | solution.py:281
  476.8 9.4 %outer_blocks.4 = (bf16[1024,512]{1,0:T(8,128)(2,1)}, bf16[512,512]{1,0:T(8,128)(2,1)}, bf16[512,512]{1,0:T(8,128)(2,1)}, bf16[1024,512]{1,0:T(8,128)(2,1)}, bf1...) custom-call(bf16[1024,2048]{1,0:T(8,128)(2,1)} %all-gather.6.cloned.1.call-done.xn_ref.left_ref, ...), custom_call_target="tpu_custom_call" | custom-call | flops 4294967296 | bytes 10485760 | tf_op jit(solution)/shard_map/outer_blocks/pallas_call | solution.py:652
  487.4 24.4 %collective-permute-done.24 = bf16[1024,512]{1,0:T(8,128)(2,1)S(1)} collective-permute-done((bf16[1024,512]{1,0:T(8,128)(2,1)}, bf16[1024,512]{1,0:T(8,128)(2,1)S(1)}, u32[]{:S(2)}, u32[]{:S(2)}) %collective-permute-start.24) | collective-permute-done | bytes 1048608 | tf_op jit(solution)/shard_map/ppermute | solution.py:839
  511.9 2.3 add_convert_fusion.12
  514.7 2.0 add_convert_fusion.14
  517.3 9.7 %outer_blocks.5 = (bf16[512,768]{1,0:T(8,128)(2,1)}, bf16[512,768]{1,0:T(8,128)(2,1)}, bf16[512,768]{1,0:T(8,128)(2,1)}, bf16[512,768]{1,0:T(8,128)(2,1)}) custom-call(bf16[1024,2048]{1,0:T(8,128)(2,1)} %all-gather.4.cloned.1.call-done.xn_ref.left_ref, bf16[1024,768]{1,0:T(8,128)(2,1)} %get-tuple-element.111.right_ref), custom_call_target="tpu_custom_call" | custom-call | flops 3221225472 | bytes 8912896 | tf_op jit(solution)/shard_map/outer_blocks/pallas_call | solution.py:652
  530.5 4.4 add_convert_fusion
  536.6 9.2 %collective-permute-done.23 = bf16[512,512]{1,0:T(8,128)(2,1)} collective-permute-done((bf16[512,512]{1,0:T(8,128)(2,1)}, bf16[512,512]{1,0:T(8,128)(2,1)}, u32[]{:S(2)}, u32[]{:S(2)}) %collective-permute-start.23) | collective-permute-done | bytes 524320 | tf_op jit(solution)/shard_map/ppermute | solution.py:839
  547.1 16.5 %collective-permute-done.28 = bf16[512,768]{1,0:T(8,128)(2,1)} collective-permute-done((bf16[512,768]{1,0:T(8,128)(2,1)}, bf16[512,768]{1,0:T(8,128)(2,1)}, u32[]{:S(2)}, u32[]{:S(2)}) %collective-permute-start.28) | collective-permute-done | bytes 786464 | tf_op jit(solution)/shard_map/ppermute | solution.py:839
  563.7 2.0 add_convert_fusion.2
  567.1 4.9 all-to-all-start.2
  574.5 3.2 side_rows.2
  577.7 3.2 side_rows.3
  580.9 3.1 shard_map.146
  583.9 1.8 convert_element_type.228
  585.7 32.5 %all-to-all-done.2.in_ref = bf16[8,64,1792]{2,1,0:T(8,128)(2,1)} async-done(((bf16[8,64,1792]{2,1,0:T(8,128)(2,1)}), bf16[8,64,1792]{2,1,0:T(8,128)(2,1)}, u32[]{:S(2)}, u32[]{:S(2)}) %all-to-all-start.2) | async-done | bytes 1835040 | tf_op jit(solution)/shard_map/all_to_all | solution.py:934
  618.2 4.2 last_rows.1
  622.4 4.3 shard_map.147
  (147 shorter events, 56.9 us)
Async XLA Ops:
  7.2 53.9 %all-gather.4.cloned.1.call-start = ((), (), s32[]{:S(2)}) async-start(), calls=%async_computation.8 | async-start | bytes 4718592 | tf_op jit(solution)/shard_map/all_gather | solution.py:917
  11.4 241.3 %all-gather.8.cloned.1.call-start = ((), (), s32[]{:S(2)}) async-start(), calls=%async_computation.10 | async-start | bytes 4718592 | tf_op jit(solution)/shard_map/all_gather | solution.py:917
  14.1 22.6 %collective-permute-start.2 = (bf16[512,384]{1,0:T(8,128)(2,1)}, bf16[512,384]{1,0:T(8,128)(2,1)S(1)}, u32[]{:S(2)}, u32[]{:S(2)}) collective-permute-start(bf16[512,384]{1,0:T(8,128)(2,1)} %get-tuple-element.79.refs_1_), channel_id=1, source_target_pairs={{0,16},{8,24},{16,0},{24,8},{1,17},{9,25},{17,1},{25,9},{2,18},{10... | collective-permute-start | bytes 1179656 | tf_op jit(solution)/shard_map/ppermute | solution.py:839
  17.1 44.0 %collective-permute-start.4 = (bf16[512,384]{1,0:T(8,128)(2,1)}, bf16[512,384]{1,0:T(8,128)(2,1)}, u32[]{:S(2)}, u32[]{:S(2)}) collective-permute-start(bf16[512,384]{1,0:T(8,128)(2,1)} %get-tuple-element.79.refs_1_), channel_id=1, source_target_pairs={{0,8},{8,0},{16,24},{24,16},{1,9},{9,1},{17,25},{25,17},{2,10},{10... | collective-permute-start | bytes 1179656 | tf_op jit(solution)/shard_map/ppermute | solution.py:839
  18.6 17.8 %collective-permute-start = (bf16[512,384]{1,0:T(8,128)(2,1)}, bf16[512,384]{1,0:T(8,128)(2,1)}, u32[]{:S(2)}, u32[]{:S(2)}) collective-permute-start(bf16[512,384]{1,0:T(8,128)(2,1)} %get-tuple-element.78.refs_0_), channel_id=1, source_target_pairs={{0,8},{8,0},{16,24},{24,16},{1,9},{9,1},{17,25},{25,17},{2,10},{10... | collective-permute-start | bytes 1179656 | tf_op jit(solution)/shard_map/ppermute | solution.py:839
  19.1 42.0 %collective-permute-start.5 = (bf16[512,384]{1,0:T(8,128)(2,1)}, bf16[512,384]{1,0:T(8,128)(2,1)}, u32[]{:S(2)}, u32[]{:S(2)}) collective-permute-start(bf16[512,384]{1,0:T(8,128)(2,1)} %get-tuple-element.78.refs_0_), channel_id=1, source_target_pairs={{0,16},{8,24},{16,0},{24,8},{1,17},{9,25},{17,1},{25,9},{2,18},{10... | collective-permute-start | bytes 1179656 | tf_op jit(solution)/shard_map/ppermute | solution.py:839
  36.4 10.0 %collective-permute-start.1 = (bf16[512,384]{1,0:T(8,128)(2,1)}, bf16[512,384]{1,0:T(8,128)(2,1)}, u32[]{:S(2)}, u32[]{:S(2)}) collective-permute-start(bf16[512,384]{1,0:T(8,128)(2,1)} %collective-permute-done.refs_2_), channel_id=1, source_target_pairs={{0,16},{8,24},{16,0},{24,8},{1,17},{9,25},{17,1},{25,9},{2,18},{10... | collective-permute-start | bytes 1179656 | tf_op jit(solution)/shard_map/ppermute | solution.py:839
  36.7 8.7 %copy-start.25 = (bf16[512,384]{1,0:T(8,128)(2,1)}, bf16[512,384]{1,0:T(8,128)(2,1)S(1)}, u32[]{:S(2)}) copy-start(bf16[512,384]{1,0:T(8,128)(2,1)S(1)} %collective-permute-done.2.refs_7_) | copy-start | bytes 1179652
  36.7 9.8 %collective-permute-start.3 = (bf16[512,384]{1,0:T(8,128)(2,1)S(1)}, bf16[512,384]{1,0:T(8,128)(2,1)}, u32[]{:S(2)}, u32[]{:S(2)}) collective-permute-start(bf16[512,384]{1,0:T(8,128)(2,1)S(1)} %collective-permute-done.2.refs_7_), channel_id=1, source_target_pairs={{0,8},{8,0},{16,24},{24,16},{1,9},{9,1},{17,25},{25,17},{2,10},{10... | collective-permute-start | bytes 1179656 | tf_op jit(solution)/shard_map/ppermute | solution.py:839
  45.4 95.5 %copy-start.2 = (bf16[512,1536]{1,0:T(8,128)(2,1)}, bf16[512,1536]{1,0:T(8,128)(2,1)S(1)}, u32[]{:S(2)}) copy-start(bf16[512,1536]{1,0:T(8,128)(2,1)S(1)} %get-tuple-element.80.refs_0_) | copy-start | bytes 4718596
  45.4 98.9 %copy-start.1 = (bf16[512,1536]{1,0:T(8,128)(2,1)}, bf16[512,1536]{1,0:T(8,128)(2,1)S(1)}, u32[]{:S(2)}) copy-start(bf16[512,1536]{1,0:T(8,128)(2,1)S(1)} %get-tuple-element.81.refs_5_.refs_0_) | copy-start | bytes 4718596
  77.1 28.6 %all-to-all-start = ((bf16[32,64,128]{2,1,0:T(8,128)(2,1)}), bf16[32,64,128]{2,1,0:T(8,128)(2,1)}, u32[]{:S(2)}, u32[]{:S(2)}) async-start(bf16[32,64,128]{2,1,0:T(8,128)(2,1)} %bitcast.38), calls=%async_computation | async-start | bytes 1048576 | tf_op jit(solution)/shard_map/all_to_all | solution.py:934
  80.7 172.0 %all-gather.6.cloned.1.call-start = ((), (), s32[]{:S(2)}) async-start(), calls=%async_computation.9 | async-start | bytes 4718592 | tf_op jit(solution)/shard_map/all_gather | solution.py:917
  112.1 14.1 %collective-permute-start.6 = (bf16[128,2048]{1,0:T(8,128)(2,1)}, bf16[128,2048]{1,0:T(8,128)(2,1)}, u32[]{:S(2)}, u32[]{:S(2)}) collective-permute-start(bf16[128,2048]{1,0:T(8,128)(2,1)} %get-tuple-element.87), channel_id=1, source_target_pairs={{0,8},{8,0},{16,24},{24,16},{1,9},{9,1},{17,25},{25,17},{2,10},{10... | collective-permute-start | bytes 1572872 | tf_op jit(solution)/shard_map/ppermute | solution.py:839
  112.1 14.1 %collective-permute-start.7 = (bf16[128,2048]{1,0:T(8,128)(2,1)}, bf16[128,2048]{1,0:T(8,128)(2,1)}, u32[]{:S(2)}, u32[]{:S(2)}) collective-permute-start(bf16[128,2048]{1,0:T(8,128)(2,1)} %get-tuple-element.88), channel_id=1, source_target_pairs={{0,16},{8,24},{16,0},{24,8},{1,17},{9,25},{17,1},{25,9},{2,18},{10... | collective-permute-start | bytes 1572872 | tf_op jit(solution)/shard_map/ppermute | solution.py:839
  113.2 23.2 %collective-permute-start.8 = (bf16[128,2048]{1,0:T(8,128)(2,1)}, bf16[128,2048]{1,0:T(8,128)(2,1)}, u32[]{:S(2)}, u32[]{:S(2)}) collective-permute-start(bf16[128,2048]{1,0:T(8,128)(2,1)} %get-tuple-element.89), channel_id=1, source_target_pairs={{0,24},{8,16},{16,8},{24,0},{1,25},{9,17},{17,9},{25,1},{2,26},{10... | collective-permute-start | bytes 1572872 | tf_op jit(solution)/shard_map/ppermute | solution.py:839
  140.9 194.7 %reduce-scatter.5.cloned.1.call-start = ((), (), s32[]{:S(2)}) async-start(), calls=%async_computation.11 | async-start | bytes 4718592 | tf_op jit(solution)/shard_map/reduce_scatter | solution.py:921
  141.0 38.5 %collective-permute-start.9 = (bf16[512,1536]{1,0:T(8,128)(2,1)S(1)}, bf16[512,1536]{1,0:T(8,128)(2,1)S(1)}, u32[]{:S(2)}, u32[]{:S(2)}) collective-permute-start(bf16[512,1536]{1,0:T(8,128)(2,1)S(1)} %get-tuple-element.80.refs_0_), channel_id=1, source_target_pairs={{0,8},{8,0},{16,24},{24,16},{1,9},{9,1},{17,25},{25,17},{2,10},{10... | collective-permute-start | bytes 4718600 | tf_op jit(solution)/shard_map/ppermute | solution.py:839
  144.3 37.3 %collective-permute-start.15 = (bf16[512,1536]{1,0:T(8,128)(2,1)S(1)}, bf16[512,1536]{1,0:T(8,128)(2,1)S(1)}, u32[]{:S(2)}, u32[]{:S(2)}) collective-permute-start(bf16[512,1536]{1,0:T(8,128)(2,1)S(1)} %get-tuple-element.81.refs_5_.refs_0_), channel_id=1, source_target_pairs={{0,16},{8,24},{16,0},{24,8},{1,17},{9,25},{17,1},{25,9},{2,18},{10... | collective-permute-start | bytes 4718600 | tf_op jit(solution)/shard_map/ppermute | solution.py:839
  144.3 54.1 %collective-permute-start.11 = (bf16[256,1536]{1,0:T(8,128)(2,1)}, bf16[256,1536]{1,0:T(8,128)(2,1)S(1)}, u32[]{:S(2)}, u32[]{:S(2)}) collective-permute-start(bf16[256,1536]{1,0:T(8,128)(2,1)} %get-tuple-element.95), channel_id=1, source_target_pairs={{0,16},{8,24},{16,0},{24,8},{1,17},{9,25},{17,1},{25,9},{2,18},{10... | collective-permute-start | bytes 2359304 | tf_op jit(solution)/shard_map/ppermute | solution.py:839
  179.5 3.5 copy-start.18
  179.5 72.3 %collective-permute-start.10 = (bf16[512,1536]{1,0:T(8,128)(2,1)S(1)}, bf16[512,1536]{1,0:T(8,128)(2,1)S(1)}, u32[]{:S(2)}, u32[]{:S(2)}) collective-permute-start(bf16[512,1536]{1,0:T(8,128)(2,1)S(1)} %collective-permute-done.9.refs_1_), channel_id=1, source_target_pairs={{0,16},{8,24},{16,0},{24,8},{1,17},{9,25},{17,1},{25,9},{2,18},{10... | collective-permute-start | bytes 4718600 | tf_op jit(solution)/shard_map/ppermute | solution.py:839
  182.8 69.8 %collective-permute-start.16 = (bf16[512,1536]{1,0:T(8,128)(2,1)S(1)}, bf16[512,1536]{1,0:T(8,128)(2,1)S(1)}, u32[]{:S(2)}, u32[]{:S(2)}) collective-permute-start(bf16[512,1536]{1,0:T(8,128)(2,1)S(1)} %collective-permute-done.15.refs_9_.refs_4_), channel_id=1, source_target_pairs={{0,8},{8,0},{16,24},{24,16},{1,9},{9,1},{17,25},{25,17},{2,10},{10... | collective-permute-start | bytes 4718600 | tf_op jit(solution)/shard_map/ppermute | solution.py:839
  183.0 54.0 %collective-permute-start.13 = (bf16[256,1536]{1,0:T(8,128)(2,1)}, bf16[256,1536]{1,0:T(8,128)(2,1)S(1)}, u32[]{:S(2)}, u32[]{:S(2)}) collective-permute-start(bf16[256,1536]{1,0:T(8,128)(2,1)} %get-tuple-element.97), channel_id=1, source_target_pairs={{0,8},{8,0},{16,24},{24,16},{1,9},{9,1},{17,25},{25,17},{2,10},{10... | collective-permute-start | bytes 2359304 | tf_op jit(solution)/shard_map/ppermute | solution.py:839
  184.9 63.5 %collective-permute-start.12 = (bf16[256,1536]{1,0:T(8,128)(2,1)}, bf16[256,1536]{1,0:T(8,128)(2,1)S(1)}, u32[]{:S(2)}, u32[]{:S(2)}) collective-permute-start(bf16[256,1536]{1,0:T(8,128)(2,1)} %get-tuple-element.96), channel_id=1, source_target_pairs={{0,16},{8,24},{16,0},{24,8},{1,17},{9,25},{17,1},{25,9},{2,18},{10... | collective-permute-start | bytes 2359304 | tf_op jit(solution)/shard_map/ppermute | solution.py:839
  198.5 53.3 %copy-start.22 = (bf16[256,1536]{1,0:T(8,128)(2,1)}, bf16[256,1536]{1,0:T(8,128)(2,1)S(1)}, u32[]{:S(2)}) copy-start(bf16[256,1536]{1,0:T(8,128)(2,1)S(1)} %collective-permute-done.11.refs_3_) | copy-start | bytes 2359300
  198.5 53.3 %collective-permute-start.14 = (bf16[256,1536]{1,0:T(8,128)(2,1)}, bf16[256,1536]{1,0:T(8,128)(2,1)S(1)}, u32[]{:S(2)}, u32[]{:S(2)}) collective-permute-start(bf16[256,1536]{1,0:T(8,128)(2,1)} %get-tuple-element.98), channel_id=1, source_target_pairs={{0,8},{8,0},{16,24},{24,16},{1,9},{9,1},{17,25},{25,17},{2,10},{10... | collective-permute-start | bytes 2359304 | tf_op jit(solution)/shard_map/ppermute | solution.py:839
  237.0 14.8 %copy-start.21 = (bf16[256,1536]{1,0:T(8,128)(2,1)}, bf16[256,1536]{1,0:T(8,128)(2,1)S(1)}, u32[]{:S(2)}) copy-start(bf16[256,1536]{1,0:T(8,128)(2,1)S(1)} %collective-permute-done.13.refs_6_.refs_1_) | copy-start | bytes 2359300
  248.3 3.4 copy-start.24
  286.7 294.2 %reduce-scatter.7.cloned.1.call-start = ((), (), s32[]{:S(2)}) async-start(), calls=%async_computation.12 | async-start | bytes 2621440 | tf_op jit(solution)/shard_map/reduce_scatter | solution.py:927
  297.6 4.6 collective-permute-start.17
  345.0 26.4 %collective-permute-start.35 = (bf16[1024,512]{1,0:T(8,128)(2,1)}, bf16[1024,512]{1,0:T(8,128)(2,1)}, u32[]{:S(2)}, u32[]{:S(2)}) collective-permute-start(bf16[1024,512]{1,0:T(8,128)(2,1)} %get-tuple-element.137), channel_id=1, source_target_pairs={{0,16},{8,24},{16,0},{24,8},{1,17},{9,25},{17,1},{25,9},{2,18},{10... | collective-permute-start | bytes 3145736 | tf_op jit(solution)/shard_map/ppermute | solution.py:839
  346.5 28.5 %collective-permute-start.33 = (bf16[1024,512]{1,0:T(8,128)(2,1)}, bf16[1024,512]{1,0:T(8,128)(2,1)S(1)}, u32[]{:S(2)}, u32[]{:S(2)}) collective-permute-start(bf16[1024,512]{1,0:T(8,128)(2,1)} %get-tuple-element.134), channel_id=1, source_target_pairs={{0,8},{8,0},{16,24},{24,16},{1,9},{9,1},{17,25},{25,17},{2,10},{10... | collective-permute-start | bytes 3145736 | tf_op jit(solution)/shard_map/ppermute | solution.py:839
  357.3 36.4 %collective-permute-start.31 = (bf16[1024,512]{1,0:T(8,128)(2,1)}, bf16[1024,512]{1,0:T(8,128)(2,1)S(1)}, u32[]{:S(2)}, u32[]{:S(2)}) collective-permute-start(bf16[1024,512]{1,0:T(8,128)(2,1)} %get-tuple-element.131), channel_id=1, source_target_pairs={{0,16},{8,24},{16,0},{24,8},{1,17},{9,25},{17,1},{25,9},{2,18},{10... | collective-permute-start | bytes 3145736 | tf_op jit(solution)/shard_map/ppermute | solution.py:839
  357.9 44.4 %collective-permute-start.29 = (bf16[1024,512]{1,0:T(8,128)(2,1)}, bf16[1024,512]{1,0:T(8,128)(2,1)S(1)}, u32[]{:S(2)}, u32[]{:S(2)}) collective-permute-start(bf16[1024,512]{1,0:T(8,128)(2,1)} %get-tuple-element.128), channel_id=1, source_target_pairs={{0,8},{8,0},{16,24},{24,16},{1,9},{9,1},{17,25},{25,17},{2,10},{10... | collective-permute-start | bytes 3145736 | tf_op jit(solution)/shard_map/ppermute | solution.py:839
  358.4 35.3 %copy-start.9 = (bf16[512,512]{1,0:T(8,128)(2,1)S(1)}, bf16[512,512]{1,0:T(8,128)(2,1)}, u32[]{:S(2)}) copy-start(bf16[512,512]{1,0:T(8,128)(2,1)} %get-tuple-element.132) | copy-start | bytes 1572868
  373.5 33.0 %collective-permute-start.36 = (bf16[512,512]{1,0:T(8,128)(2,1)}, bf16[512,512]{1,0:T(8,128)(2,1)}, u32[]{:S(2)}, u32[]{:S(2)}) collective-permute-start(bf16[512,512]{1,0:T(8,128)(2,1)} %add_convert_fusion.4), channel_id=1, source_target_pairs={{0,8},{8,0},{16,24},{24,16},{1,9},{9,1},{17,25},{25,17},{2,10},{10... | collective-permute-start | bytes 1572872 | tf_op jit(solution)/shard_map/ppermute | solution.py:839
  376.9 63.6 %collective-permute-start.34 = (bf16[512,512]{1,0:T(8,128)(2,1)}, bf16[512,512]{1,0:T(8,128)(2,1)}, u32[]{:S(2)}, u32[]{:S(2)}) collective-permute-start(bf16[512,512]{1,0:T(8,128)(2,1)} %add_convert_fusion.6), channel_id=1, source_target_pairs={{0,16},{8,24},{16,0},{24,8},{1,17},{9,25},{17,1},{25,9},{2,18},{10... | collective-permute-start | bytes 1572872 | tf_op jit(solution)/shard_map/ppermute | solution.py:839
  393.7 5.6 copy-start.4
  399.3 29.7 %copy-start.3 = (bf16[512,2048]{1,0:T(8,128)(2,1)S(1)}, bf16[512,2048]{1,0:T(8,128)(2,1)}, u32[]{:S(2)}) copy-start(bf16[512,2048]{1,0:T(8,128)(2,1)} %weight_ref.1) | copy-start | bytes 6291460
  399.3 29.7 %copy-start.8 = (bf16[128,2048]{1,0:T(8,128)(2,1)S(1)}, bf16[128,2048]{1,0:T(8,128)(2,1)}, u32[]{:S(2)}) copy-start(bf16[128,2048]{1,0:T(8,128)(2,1)} %get-tuple-element.109.refs_0_) | copy-start | bytes 1572868
  399.3 18.4 %collective-permute-start.20 = (bf16[128,2048]{1,0:T(8,128)(2,1)}, bf16[128,2048]{1,0:T(8,128)(2,1)S(1)}, u32[]{:S(2)}, u32[]{:S(2)}) collective-permute-start(bf16[128,2048]{1,0:T(8,128)(2,1)} %get-tuple-element.109.refs_0_), channel_id=1, source_target_pairs={{0,24},{8,16},{16,8},{24,0},{1,25},{9,17},{17,9},{25,1},{2,26},{10... | collective-permute-start | bytes 1572872 | tf_op jit(solution)/shard_map/ppermute | solution.py:839
  401.7 25.7 %collective-permute-start.19 = (bf16[128,2048]{1,0:T(8,128)(2,1)}, bf16[128,2048]{1,0:T(8,128)(2,1)S(1)}, u32[]{:S(2)}, u32[]{:S(2)}) collective-permute-start(bf16[128,2048]{1,0:T(8,128)(2,1)} %get-tuple-element.109.refs_0_), channel_id=1, source_target_pairs={{0,16},{8,24},{16,0},{24,8},{1,17},{9,25},{17,1},{25,9},{2,18},{10... | collective-permute-start | bytes 1572872 | tf_op jit(solution)/shard_map/ppermute | solution.py:839
  402.3 26.6 %collective-permute-start.18 = (bf16[128,2048]{1,0:T(8,128)(2,1)}, bf16[128,2048]{1,0:T(8,128)(2,1)S(1)}, u32[]{:S(2)}, u32[]{:S(2)}) collective-permute-start(bf16[128,2048]{1,0:T(8,128)(2,1)} %get-tuple-element.109.refs_0_), channel_id=1, source_target_pairs={{0,8},{8,0},{16,24},{24,16},{1,9},{9,1},{17,25},{25,17},{2,10},{10... | collective-permute-start | bytes 1572872 | tf_op jit(solution)/shard_map/ppermute | solution.py:839
  406.5 35.5 %collective-permute-start.32 = (bf16[512,512]{1,0:T(8,128)(2,1)}, bf16[512,512]{1,0:T(8,128)(2,1)}, u32[]{:S(2)}, u32[]{:S(2)}) collective-permute-start(bf16[512,512]{1,0:T(8,128)(2,1)} %add_convert_fusion.8), channel_id=1, source_target_pairs={{0,8},{8,0},{16,24},{24,16},{1,9},{9,1},{17,25},{25,17},{2,10},{10... | collective-permute-start | bytes 1572872 | tf_op jit(solution)/shard_map/ppermute | solution.py:839
  417.7 12.5 %copy-start.10 = (bf16[128,2048]{1,0:T(8,128)(2,1)}, bf16[128,2048]{1,0:T(8,128)(2,1)S(1)}, u32[]{:S(2)}) copy-start(bf16[128,2048]{1,0:T(8,128)(2,1)S(1)} %collective-permute-done.20.refs_3_) | copy-start | bytes 1572868
  417.7 25.7 %collective-permute-start.30 = (bf16[512,512]{1,0:T(8,128)(2,1)}, bf16[512,512]{1,0:T(8,128)(2,1)}, u32[]{:S(2)}, u32[]{:S(2)}) collective-permute-start(bf16[512,512]{1,0:T(8,128)(2,1)} %add_convert_fusion.10), channel_id=1, source_target_pairs={{0,16},{8,24},{16,0},{24,8},{1,17},{9,25},{17,1},{25,9},{2,18},{10... | collective-permute-start | bytes 1572872 | tf_op jit(solution)/shard_map/ppermute | solution.py:839
  431.4 18.8 %all-to-all-start.1 = ((bf16[32,64,128]{2,1,0:T(8,128)(2,1)}), bf16[32,64,128]{2,1,0:T(8,128)(2,1)S(1)}, u32[]{:S(2)}, u32[]{:S(2)}) async-start(bf16[32,64,128]{2,1,0:T(8,128)(2,1)} %bitcast.14), calls=%async_computation.3 | async-start | bytes 1048576 | tf_op jit(solution)/shard_map/all_to_all | solution.py:934
  434.0 149.9 %reduce-scatter.11.cloned.1.call-start = ((), (), s32[]{:S(2)}) async-start(), calls=%async_computation.14 | async-start | bytes 2359296 | tf_op jit(solution)/shard_map/reduce_scatter | solution.py:921
  440.5 2.9 copy-start.14
  451.0 116.0 %all-to-all-start.3 = ((bf16[8,64,2048]{2,1,0:T(8,128)(2,1)}), bf16[8,64,2048]{2,1,0:T(8,128)(2,1)S(1)}, u32[]{:S(2)}, u32[]{:S(2)}) async-start(bf16[8,64,2048]{2,1,0:T(8,128)(2,1)} %bitcast.32), calls=%async_computation.6 | async-start | bytes 4194304 | tf_op jit(solution)/shard_map/all_to_all | solution.py:934
  454.7 167.7 %reduce-scatter.9.cloned.1.call-start = ((), (), s32[]{:S(2)}) async-start(), calls=%async_computation.13 | async-start | bytes 2621440 | tf_op jit(solution)/shard_map/reduce_scatter | solution.py:927
  476.6 53.3 %collective-permute-start.21 = (bf16[512,2048]{1,0:T(8,128)(2,1)}, bf16[512,2048]{1,0:T(8,128)(2,1)}, u32[]{:S(2)}, u32[]{:S(2)}) collective-permute-start(bf16[512,2048]{1,0:T(8,128)(2,1)} %get-tuple-element.115), channel_id=1, source_target_pairs={{0,1},{1,0},{2,3},{3,2},{4,5},{5,4},{6,7},{7,6},{8,9},{9,8},{10,11... | collective-permute-start | bytes 6291464 | tf_op jit(solution)/shard_map/ppermute | solution.py:925
  486.2 25.7 %collective-permute-start.24 = (bf16[1024,512]{1,0:T(8,128)(2,1)}, bf16[1024,512]{1,0:T(8,128)(2,1)S(1)}, u32[]{:S(2)}, u32[]{:S(2)}) collective-permute-start(bf16[1024,512]{1,0:T(8,128)(2,1)} %get-tuple-element.121), channel_id=1, source_target_pairs={{0,16},{8,24},{16,0},{24,8},{1,17},{9,25},{17,1},{25,9},{2,18},{10... | collective-permute-start | bytes 3145736 | tf_op jit(solution)/shard_map/ppermute | solution.py:839
  487.0 27.7 %collective-permute-start.22 = (bf16[1024,512]{1,0:T(8,128)(2,1)}, bf16[1024,512]{1,0:T(8,128)(2,1)S(1)}, u32[]{:S(2)}, u32[]{:S(2)}) collective-permute-start(bf16[1024,512]{1,0:T(8,128)(2,1)} %get-tuple-element.118), channel_id=1, source_target_pairs={{0,8},{8,0},{16,24},{24,16},{1,9},{9,1},{17,25},{25,17},{2,10},{10... | collective-permute-start | bytes 3145736 | tf_op jit(solution)/shard_map/ppermute | solution.py:839
  514.2 20.7 %collective-permute-start.25 = (bf16[512,512]{1,0:T(8,128)(2,1)}, bf16[512,512]{1,0:T(8,128)(2,1)}, u32[]{:S(2)}, u32[]{:S(2)}) collective-permute-start(bf16[512,512]{1,0:T(8,128)(2,1)} %add_convert_fusion.12), channel_id=1, source_target_pairs={{0,8},{8,0},{16,24},{24,16},{1,9},{9,1},{17,25},{25,17},{2,10},{10... | collective-permute-start | bytes 1572872 | tf_op jit(solution)/shard_map/ppermute | solution.py:839
  516.6 29.2 %collective-permute-start.23 = (bf16[512,512]{1,0:T(8,128)(2,1)}, bf16[512,512]{1,0:T(8,128)(2,1)}, u32[]{:S(2)}, u32[]{:S(2)}) collective-permute-start(bf16[512,512]{1,0:T(8,128)(2,1)} %add_convert_fusion.14), channel_id=1, source_target_pairs={{0,16},{8,24},{16,0},{24,8},{1,17},{9,25},{17,1},{25,9},{2,18},{10... | collective-permute-start | bytes 1572872 | tf_op jit(solution)/shard_map/ppermute | solution.py:839
  527.0 36.6 %collective-permute-start.28 = (bf16[512,768]{1,0:T(8,128)(2,1)}, bf16[512,768]{1,0:T(8,128)(2,1)}, u32[]{:S(2)}, u32[]{:S(2)}) collective-permute-start(bf16[512,768]{1,0:T(8,128)(2,1)} %get-tuple-element.126), channel_id=1, source_target_pairs={{0,16},{8,24},{16,0},{24,8},{1,17},{9,25},{17,1},{25,9},{2,18},{10... | collective-permute-start | bytes 2359304 | tf_op jit(solution)/shard_map/ppermute | solution.py:839
  528.4 35.2 %collective-permute-start.27 = (bf16[512,768]{1,0:T(8,128)(2,1)}, bf16[512,768]{1,0:T(8,128)(2,1)}, u32[]{:S(2)}, u32[]{:S(2)}) collective-permute-start(bf16[512,768]{1,0:T(8,128)(2,1)} %get-tuple-element.125), channel_id=1, source_target_pairs={{0,24},{8,16},{16,8},{24,0},{1,25},{9,17},{17,9},{25,1},{2,26},{10... | collective-permute-start | bytes 2359304 | tf_op jit(solution)/shard_map/ppermute | solution.py:839
  529.9 33.7 %collective-permute-start.26 = (bf16[512,768]{1,0:T(8,128)(2,1)}, bf16[512,768]{1,0:T(8,128)(2,1)}, u32[]{:S(2)}, u32[]{:S(2)}) collective-permute-start(bf16[512,768]{1,0:T(8,128)(2,1)} %get-tuple-element.124), channel_id=1, source_target_pairs={{0,8},{8,0},{16,24},{24,16},{1,9},{9,1},{17,25},{25,17},{2,10},{10... | collective-permute-start | bytes 2359304 | tf_op jit(solution)/shard_map/ppermute | solution.py:839
  535.0 10.9 %copy-start.16 = (bf16[512,512]{1,0:T(8,128)(2,1)S(1)}, bf16[512,512]{1,0:T(8,128)(2,1)}, u32[]{:S(2)}) copy-start(bf16[512,512]{1,0:T(8,128)(2,1)} %get-tuple-element.117) | copy-start | bytes 1572868
  535.0 28.7 %copy-start.7 = (bf16[512,768]{1,0:T(8,128)(2,1)S(1)}, bf16[512,768]{1,0:T(8,128)(2,1)}, u32[]{:S(2)}) copy-start(bf16[512,768]{1,0:T(8,128)(2,1)} %get-tuple-element.123) | copy-start | bytes 2359300
  567.1 7.4 %copy-start = (bf16[8,64,2048]{2,1,0:T(8,128)(2,1)}, bf16[8,64,2048]{2,1,0:T(8,128)(2,1)S(1)}, u32[]{:S(2)}) copy-start(bf16[8,64,2048]{2,1,0:T(8,128)(2,1)S(1)} %all-to-all-done.3.refs_0_) | copy-start | bytes 6291460
  567.1 51.1 %all-to-all-start.2 = ((bf16[8,64,1792]{2,1,0:T(8,128)(2,1)}), bf16[8,64,1792]{2,1,0:T(8,128)(2,1)}, u32[]{:S(2)}, u32[]{:S(2)}) async-start(bf16[8,64,1792]{2,1,0:T(8,128)(2,1)} %bitcast.33), calls=%async_computation.5 | async-start | bytes 3670016 | tf_op jit(solution)/shard_map/all_to_all | solution.py:934
  (10 other events, 16.0 us)
Sparse Core Ops, SparseCore 0:
  11.5 49.5 all-gather.3
  77.2 53.6 all-gather.7
  141.0 48.5 all-gather.5
  286.8 48.7 reduce-scatter.4
  337.7 42.0 reduce-scatter.6
  440.6 52.3 reduce-scatter.10
  535.1 46.0 reduce-scatter.8

commit v4 on v3

--- a/solution.py
+++ b/solution.py
@@ -492,14 +492,18 @@
 ALL = slice(None)
 
 
-def norm_in_kernel(rows, orders_ref, x_ref, gain_ref, grad_ref, xn_ref, dy_ref):
+def cast_kernel(rows, orders_ref, grad_ref, dy_ref):
+    for p in range(BLOCKS):
+        at_block(dy_ref, rows, p)[...] = at_block(grad_ref, rows, orders_ref[p])[...].astype(BF)
+
+
+def norm_in_kernel(rows, orders_ref, x_ref, gain_ref, xn_ref):
     x = x_ref[rows, :]
     inv = lax.rsqrt(jnp.mean(x * x, axis=1, keepdims=True) + EPS)
     for p in range(BLOCKS):
         block = orders_ref[p]
         normed = at_block(x_ref, rows, block)[...] * inv * at_block(gain_ref, ALL, block)[...]
         at_block(xn_ref, rows, p)[...] = normed.astype(BF)
-        at_block(dy_ref, rows, p)[...] = at_block(grad_ref, rows, block)[...].astype(BF)
 
 
 def norm_mid_kernel(rows, orders_ref, x_ref, own_ref, *refs):
@@ -978,8 +982,9 @@
         orders, places = blocks_at, blocks_at
     gain1, gain2 = norm1_gain[None, :], norm2_gain[None, :]
 
-    xn1_own, dy_own = on_rows(norm_in_kernel, orders, (layer_in, gain1, cotangent), (BF, BF))
+    (xn1_own,) = on_rows(norm_in_kernel, orders, (layer_in, gain1), (BF,))
     xn1 = over_seq(xn1_own)
+    (dy_own,) = on_rows(cast_kernel, orders, (cotangent,), (BF,))
 
     if strided:
         left, right = strided_heads(qkv_weight, group, group_count)

time: 635 us -> 635 us (level)
    pallas_call x5 -> x6, Pallas kernels: 19.9 us -> 22.3 us  [on_rows(): pl.pallas_call(by_rows(kernel), grid_spec=pltpu.PrefetchScalarGridSpec(nu...]
  transfers between devices with their start and end apart: 48 -> 48, of which waited for: 26 -> 24; matrix products, arithmetic and copies ran while one was open for 8% -> 8% of each run, Pallas kernels for 18% -> 18%
where the time goes in v4:
time: 635 us; the launch traced here: 633 us
  waiting for transfers between devices  335 us (53%)
  Pallas kernels  171 us (27%)
  starting transfers between devices  54.2 us (9%)
  other arithmetic  38.7 us (6%)
  local copies, waits for them, and re-layouts  18.6 us (3%)
  between operations  14.5 us (2%)
    ppermute x35, waiting for transfers between devices, partner(): return lax.ppermute(array, 'dp', [(i, i ^ bits) for i in range(4)])  230 us
    all_to_all x4, waiting for transfers between devices, exchange(): return lax.all_to_all(values, axes, split_axis=0, concat_axis=0, tiled=True)  60.6 us
    ppermute x35, starting transfers between devices, partner(): return lax.ppermute(array, 'dp', [(i, i ^ bits) for i in range(4)])  38.6 us
    pallas_call x4, Pallas kernels, outer_blocks(): pl.pallas_call(functools.partial(outer_kernel, layouts), grid=(4 * steps,...  37.9 us
    pallas_call x1, Pallas kernels, feed_forward(): pl.pallas_call(functools.partial(feed_kernel, len(part_a), len(part_b)),...  32.3 us
    convert_element_type x15, other arithmetic, add(): return total.astype(BF)  30.1 us
    reduce_scatter x2, waiting for transfers between devices, sum_over_seq(): lax.psum_scatter(values.astype(BF), 'seq', scatter_dimension=0, tiled=True)  29.7 us
    pallas_call x6, Pallas kernels, on_rows(): pl.pallas_call(by_rows(kernel), grid_spec=pltpu.PrefetchScalarGridSpec(nu...  22.3 us
  transfers between devices with their start and end apart: 48, of which 24 were waited for; matrix products, arithmetic and copies ran while one was open for 8% of the time, Pallas kernels for 18%

profile of v4, /device:TPU:0, one launch (start us, length us, event | category | flops | bytes accessed | tf_op | source)
XLA Modules:
  0.0 633.1 jit_solution(1750260903142034567)
XLA Ops:
  7.7 3.2 shard_map.143
  11.0 2.7 strided_heads.1
  13.6 3.0 collective-permute-start.2
  18.7 2.2 constant_dynamic-slice_fusion.2
  20.9 2.3 constant_dynamic-slice_fusion.3
  23.3 2.3 constant_dynamic-slice_fusion.1
  25.5 10.4 %collective-permute-done.refs_2_ = bf16[512,384]{1,0:T(8,128)(2,1)} collective-permute-done((bf16[512,384]{1,0:T(8,128)(2,1)}, bf16[512,384]{1,0:T(8,128)(2,1)}, u32[]{:S(2)}, u32[]{:S(2)}) %collective-permute-start) | collective-permute-done | bytes 393248 | tf_op jit(solution)/shard_map/ppermute | solution.py:843
  38.6 4.3 rotary.1
  42.9 2.8 shard_map.145
  45.7 2.1 pad_maximum_fusion.2
  50.6 10.1 %all-gather.4.cloned.1.call-done.xn_ref.left_ref = bf16[1024,2048]{1,0:T(8,128)(2,1)} async-done(((bf16[128,2048]{1,0:T(8,128)(2,1)}), bf16[1024,2048]{1,0:T(8,128)(2,1)}) %all-gather.4.cloned.1.call-update) | async-done | bytes 4194320 | tf_op jit(solution)/shard_map/all_gather | solution.py:921
  60.7 16.0 %attention_forward.1 = (bf16[4,8,64,128]{3,2,1,0:T(8,128)(2,1)}, bf16[1024,256]{1,0:T(8,128)(2,1)}, bf16[1024,256]{1,0:T(8,128)(2,1)}, bf16[1024,256]{1,0:T(8,128)(2,1)}, f32[8,1024]{1,0:T(8,128)}) custom-call(bf16[1024,2048]{1,0:T(8,128)(2,1)} %all-gather.4.cloned.1.call-done.xn_ref.left_ref, bf16[512,384]{1,0:T(8,128)(2,1)} %get-tuple-element.75.refs_0_, ...), custom_call_target="tpu_custom_call" | custom-call | flops 3758096384 | bytes 9437184 | tf_op jit(solution)/shard_map/attention_forward/pallas_call | solution.py:238
  76.7 3.5 all-to-all-start
  80.8 24.5 %all-to-all-done = bf16[32,64,128]{2,1,0:T(8,128)(2,1)} async-done(((bf16[32,64,128]{2,1,0:T(8,128)(2,1)}), bf16[32,64,128]{2,1,0:T(8,128)(2,1)}, u32[]{:S(2)}, u32[]{:S(2)}) %all-to-all-start) | async-done | bytes 524320 | tf_op jit(solution)/shard_map/all_to_all | solution.py:938
  105.3 6.4 %project.1 = (f32[128,2048]{1,0:T(8,128)}, bf16[128,2048]{1,0:T(8,128)(2,1)}, bf16[128,2048]{1,0:T(8,128)(2,1)}, bf16[128,2048]{1,0:T(8,128)(2,1)}) custom-call(s32[4]{0:T(128)} %iota_xor_fusion.members_ref, bf16[4,512,128]{2,1,0:T(8,128)(2,1)} %bitcast.3.features_ref, bf16[512,2048]{1,0:T(8,128)(2,1)} %weight_ref.1), custom_call_target="tpu_custom_call" | custom-call | tf_op jit(solution)/shard_map/project/pallas_call | solution.py:779
  112.8 2.3 collective-permute-start.8
  115.2 10.6 %collective-permute-done.6.refs_1_ = bf16[128,2048]{1,0:T(8,128)(2,1)} collective-permute-done((bf16[128,2048]{1,0:T(8,128)(2,1)}, bf16[128,2048]{1,0:T(8,128)(2,1)}, u32[]{:S(2)}, u32[]{:S(2)}) %collective-permute-start.6) | collective-permute-done | bytes 524320 | tf_op jit(solution)/shard_map/ppermute | solution.py:843
  125.7 10.3 %collective-permute-done.8.refs_3_ = bf16[128,2048]{1,0:T(8,128)(2,1)} collective-permute-done((bf16[128,2048]{1,0:T(8,128)(2,1)}, bf16[128,2048]{1,0:T(8,128)(2,1)}, u32[]{:S(2)}, u32[]{:S(2)}) %collective-permute-start.8) | collective-permute-done | bytes 524320 | tf_op jit(solution)/shard_map/ppermute | solution.py:843
  136.0 4.5 shard_map.144
  140.6 3.3 collective-permute-start.9
  143.9 2.0 collective-permute-start.11
  145.9 33.1 %collective-permute-done.9.refs_1_ = bf16[512,1536]{1,0:T(8,128)(2,1)S(1)} collective-permute-done((bf16[512,1536]{1,0:T(8,128)(2,1)S(1)}, bf16[512,1536]{1,0:T(8,128)(2,1)S(1)}, u32[]{:S(2)}, u32[]{:S(2)}) %collective-permute-start.9) | collective-permute-done | bytes 1572896 | tf_op jit(solution)/shard_map/ppermute | solution.py:843
  182.6 1.9 collective-permute-start.13
  184.4 13.6 %collective-permute-done.11.refs_3_ = bf16[256,1536]{1,0:T(8,128)(2,1)S(1)} collective-permute-done((bf16[256,1536]{1,0:T(8,128)(2,1)}, bf16[256,1536]{1,0:T(8,128)(2,1)S(1)}, u32[]{:S(2)}, u32[]{:S(2)}) %collective-permute-start.11) | collective-permute-done | bytes 786464 | tf_op jit(solution)/shard_map/ppermute | solution.py:843
  198.1 38.4 %collective-permute-done.13.refs_6_.refs_1_ = bf16[256,1536]{1,0:T(8,128)(2,1)S(1)} collective-permute-done((bf16[256,1536]{1,0:T(8,128)(2,1)}, bf16[256,1536]{1,0:T(8,128)(2,1)S(1)}, u32[]{:S(2)}, u32[]{:S(2)}) %collective-permute-start.13) | collective-permute-done | bytes 786464 | tf_op jit(solution)/shard_map/ppermute | solution.py:843
  236.5 11.4 %collective-permute-done.12.refs_4_ = bf16[256,1536]{1,0:T(8,128)(2,1)S(1)} collective-permute-done((bf16[256,1536]{1,0:T(8,128)(2,1)}, bf16[256,1536]{1,0:T(8,128)(2,1)S(1)}, u32[]{:S(2)}, u32[]{:S(2)}) %collective-permute-start.12) | collective-permute-done | bytes 786464 | tf_op jit(solution)/shard_map/ppermute | solution.py:843
  247.9 3.4 collective-permute-done.14.refs_7_.refs_2_
  254.0 32.3 %feed_forward.1 = (bf16[1024,1024]{1,0:T(8,128)(2,1)}, bf16[1024,2048]{1,0:T(8,128)(2,1)}, bf16[1024,2048]{1,0:T(8,128)(2,1)}) custom-call(bf16[1024,2048]{1,0:T(8,128)(2,1)} %all-gather.6.cloned.1.call-done.xn_ref.left_ref, bf16[1024,2048]{1,0:T(8,128)(2,1)} %all-gather.8.cloned.1.call-done.dy_ref.left_ref, bf16[512,1536]{1,0:T(8,128)(2,1)} %copy-done.2, ...), custom_call_target="tpu_custom_call" | custom-call | flops 21474836480 | bytes 29360128 | tf_op jit(solution)/shard_map/feed_forward/pallas_call | solution.py:690
  286.5 10.7 %feed_out.1 = (bf16[512,2048]{1,0:T(8,128)(2,1)}, bf16[512,2048]{1,0:T(8,128)(2,1)}) custom-call(s32[1]{0:T(128)} %bitcast.1.which_ref.group_ref, bf16[1024,1024]{1,0:T(8,128)(2,1)} %get-tuple-element.98.act_ref.right_ref, bf16[512,1536]{1,0:T(8,128)(2,1)} %copy-done.1, bf16[256,1536]{1,0:T(8,128)(2,1)} %copy-done.21, bf16[256,1536]{1,0:T(8,128)(2,1)} %copy-done.23, ...), custom_call_target="tpu_custom_call" | custom-call | flops 4294967296 | bytes 10485760 | tf_op jit(solution)/shard_map/feed_out/pallas_call | solution.py:739
  297.2 4.5 collective-permute-done.17
  301.8 3.7 add_convert_fusion.1
  305.5 29.7 %reduce-scatter.5.cloned.1.call-done.refs_1_ = bf16[128,2048]{1,0:T(8,128)(2,1)} async-done(((bf16[1024,2048]{1,0:T(8,128)(2,1)}), bf16[128,2048]{1,0:T(8,128)(2,1)}) %reduce-scatter.5.cloned.1.call-update) | async-done | bytes 524304 | tf_op jit(solution)/shard_map/reduce_scatter | solution.py:925
  335.2 9.4 %outer_blocks.7 = (bf16[1024,512]{1,0:T(8,128)(2,1)}, bf16[512,512]{1,0:T(8,128)(2,1)}, bf16[512,512]{1,0:T(8,128)(2,1)}, bf16[1024,512]{1,0:T(8,128)(2,1)}, bf1...) custom-call(bf16[1024,2048]{1,0:T(8,128)(2,1)} %all-gather.6.cloned.1.call-done.xn_ref.left_ref, ...), custom_call_target="tpu_custom_call" | custom-call | flops 4294967296 | bytes 10485760 | tf_op jit(solution)/shard_map/outer_blocks/pallas_call | solution.py:656
  347.5 9.4 %outer_blocks.6 = (bf16[1024,512]{1,0:T(8,128)(2,1)}, bf16[512,512]{1,0:T(8,128)(2,1)}, bf16[512,512]{1,0:T(8,128)(2,1)}, bf16[1024,512]{1,0:T(8,128)(2,1)}, bf1...) custom-call(bf16[1024,2048]{1,0:T(8,128)(2,1)} %all-gather.8.cloned.1.call-done.dy_ref.left_ref, ...), custom_call_target="tpu_custom_call" | custom-call | flops 4294967296 | bytes 10485760 | tf_op jit(solution)/shard_map/outer_blocks/pallas_call | solution.py:656
  358.5 12.4 %collective-permute-done.35 = bf16[1024,512]{1,0:T(8,128)(2,1)} collective-permute-done((bf16[1024,512]{1,0:T(8,128)(2,1)}, bf16[1024,512]{1,0:T(8,128)(2,1)}, u32[]{:S(2)}, u32[]{:S(2)}) %collective-permute-start.35) | collective-permute-done | bytes 1048608 | tf_op jit(solution)/shard_map/ppermute | solution.py:843
  370.9 2.1 add_convert_fusion.4
  374.5 2.0 add_convert_fusion.6
  378.0 15.3 %collective-permute-done.31 = bf16[1024,512]{1,0:T(8,128)(2,1)S(1)} collective-permute-done((bf16[1024,512]{1,0:T(8,128)(2,1)}, bf16[1024,512]{1,0:T(8,128)(2,1)S(1)}, u32[]{:S(2)}, u32[]{:S(2)}) %collective-permute-start.31) | collective-permute-done | bytes 1048608 | tf_op jit(solution)/shard_map/ppermute | solution.py:843
  394.4 4.5 shard_map.146
  398.9 2.4 collective-permute-start.20
  402.4 2.0 add_convert_fusion.10
  409.2 8.1 %collective-permute-done.20.refs_3_ = bf16[128,2048]{1,0:T(8,128)(2,1)S(1)} collective-permute-done((bf16[128,2048]{1,0:T(8,128)(2,1)}, bf16[128,2048]{1,0:T(8,128)(2,1)S(1)}, u32[]{:S(2)}, u32[]{:S(2)}) %collective-permute-start.20) | collective-permute-done | bytes 524320 | tf_op jit(solution)/shard_map/ppermute | solution.py:843
  418.8 8.2 %collective-permute-done.19.refs_2_ = bf16[128,2048]{1,0:T(8,128)(2,1)S(1)} collective-permute-done((bf16[128,2048]{1,0:T(8,128)(2,1)}, bf16[128,2048]{1,0:T(8,128)(2,1)S(1)}, u32[]{:S(2)}, u32[]{:S(2)}) %collective-permute-start.19) | collective-permute-done | bytes 524320 | tf_op jit(solution)/shard_map/ppermute | solution.py:843
  431.0 2.6 all-to-all-start.1
  433.7 6.4 %out_rows.1 = bf16[512,2048]{1,0:T(8,128)(2,1)} custom-call(s32[4]{0:T(128)} %iota_xor_fusion.members_ref, bf16[4,512,128]{2,1,0:T(8,128)(2,1)} %bitcast.3.features_ref, bf16[128,2048]{1,0:T(8,128)(2,1)} %get-tuple-element.105.refs_0_, bf16[128,2048]{1,0:T(8,128)(2,1)} %copy-done.12, bf16[128,2048]{1,0:T(8,128)(2,1)} %copy-done.11, bf16[128,2048]{1,0:T(8,128)(2,1)} %copy-done.10), custom_call_target="tpu_custom_call" | custom-call | tf_op jit(solution)/shard_map/out_rows/pallas_call | solution.py:827
  446.0 3.9 all-to-all-done.1
  450.6 3.6 all-to-all-start.3
  454.5 21.7 %attention_backward.1 = (bf16[1024,768]{1,0:T(8,128)(2,1)}, bf16[512,2048]{1,0:T(8,128)(2,1)}, bf16[512,2048]{1,0:T(8,128)(2,1)}) custom-call(s32[1]{0:T(128)} %bitcast.1.which_ref.group_ref, bf16[1024,256]{1,0:T(8,128)(2,1)} %get-tuple-element.102.q_ref, bf16[1024,256]{1,0:T(8,128)(2,1)} %get-tuple-element.103.k_ref, ...), custom_call_target="tpu_custom_call" | custom-call | flops 4563402752 | bytes 12582912 | tf_op jit(solution)/shard_map/attention_backward/pallas_call | solution.py:281
  476.4 9.4 %outer_blocks.4 = (bf16[1024,512]{1,0:T(8,128)(2,1)}, bf16[512,512]{1,0:T(8,128)(2,1)}, bf16[512,512]{1,0:T(8,128)(2,1)}, bf16[1024,512]{1,0:T(8,128)(2,1)}, bf1...) custom-call(bf16[1024,2048]{1,0:T(8,128)(2,1)} %all-gather.6.cloned.1.call-done.xn_ref.left_ref, ...), custom_call_target="tpu_custom_call" | custom-call | flops 4294967296 | bytes 10485760 | tf_op jit(solution)/shard_map/outer_blocks/pallas_call | solution.py:656
  487.1 24.4 %collective-permute-done.24 = bf16[1024,512]{1,0:T(8,128)(2,1)S(1)} collective-permute-done((bf16[1024,512]{1,0:T(8,128)(2,1)}, bf16[1024,512]{1,0:T(8,128)(2,1)S(1)}, u32[]{:S(2)}, u32[]{:S(2)}) %collective-permute-start.24) | collective-permute-done | bytes 1048608 | tf_op jit(solution)/shard_map/ppermute | solution.py:843
  511.5 2.3 add_convert_fusion.12
  514.2 2.0 add_convert_fusion.14
  516.9 9.7 %outer_blocks.5 = (bf16[512,768]{1,0:T(8,128)(2,1)}, bf16[512,768]{1,0:T(8,128)(2,1)}, bf16[512,768]{1,0:T(8,128)(2,1)}, bf16[512,768]{1,0:T(8,128)(2,1)}) custom-call(bf16[1024,2048]{1,0:T(8,128)(2,1)} %all-gather.4.cloned.1.call-done.xn_ref.left_ref, bf16[1024,768]{1,0:T(8,128)(2,1)} %get-tuple-element.107.right_ref), custom_call_target="tpu_custom_call" | custom-call | flops 3221225472 | bytes 8912896 | tf_op jit(solution)/shard_map/outer_blocks/pallas_call | solution.py:656
  530.1 4.4 add_convert_fusion
  536.3 9.2 %collective-permute-done.23 = bf16[512,512]{1,0:T(8,128)(2,1)} collective-permute-done((bf16[512,512]{1,0:T(8,128)(2,1)}, bf16[512,512]{1,0:T(8,128)(2,1)}, u32[]{:S(2)}, u32[]{:S(2)}) %collective-permute-start.23) | collective-permute-done | bytes 524320 | tf_op jit(solution)/shard_map/ppermute | solution.py:843
  546.7 16.5 %collective-permute-done.28 = bf16[512,768]{1,0:T(8,128)(2,1)} collective-permute-done((bf16[512,768]{1,0:T(8,128)(2,1)}, bf16[512,768]{1,0:T(8,128)(2,1)}, u32[]{:S(2)}, u32[]{:S(2)}) %collective-permute-start.28) | collective-permute-done | bytes 786464 | tf_op jit(solution)/shard_map/ppermute | solution.py:843
  563.3 2.0 add_convert_fusion.2
  566.7 5.0 all-to-all-start.2
  574.2 3.2 side_rows.2
  577.4 3.2 side_rows.3
  580.6 3.1 shard_map.147
  585.5 32.3 %all-to-all-done.2.in_ref = bf16[8,64,1792]{2,1,0:T(8,128)(2,1)} async-done(((bf16[8,64,1792]{2,1,0:T(8,128)(2,1)}), bf16[8,64,1792]{2,1,0:T(8,128)(2,1)}, u32[]{:S(2)}, u32[]{:S(2)}) %all-to-all-start.2) | async-done | bytes 1835040 | tf_op jit(solution)/shard_map/all_to_all | solution.py:938
  617.8 4.2 last_rows.1
  622.0 4.3 shard_map.148
  (148 shorter events, 58.0 us)
Async XLA Ops:
  7.2 53.5 %all-gather.4.cloned.1.call-start = ((), (), s32[]{:S(2)}) async-start(), calls=%async_computation.8 | async-start | bytes 4718592 | tf_op jit(solution)/shard_map/all_gather | solution.py:921
  10.9 241.3 %all-gather.8.cloned.1.call-start = ((), (), s32[]{:S(2)}) async-start(), calls=%async_computation.10 | async-start | bytes 4718592 | tf_op jit(solution)/shard_map/all_gather | solution.py:921
  13.6 22.6 %collective-permute-start.2 = (bf16[512,384]{1,0:T(8,128)(2,1)}, bf16[512,384]{1,0:T(8,128)(2,1)S(1)}, u32[]{:S(2)}, u32[]{:S(2)}) collective-permute-start(bf16[512,384]{1,0:T(8,128)(2,1)} %get-tuple-element.76.refs_1_), channel_id=1, source_target_pairs={{0,16},{8,24},{16,0},{24,8},{1,17},{9,25},{17,1},{25,9},{2,18},{10... | collective-permute-start | bytes 1179656 | tf_op jit(solution)/shard_map/ppermute | solution.py:843
  16.6 44.0 %collective-permute-start.4 = (bf16[512,384]{1,0:T(8,128)(2,1)}, bf16[512,384]{1,0:T(8,128)(2,1)}, u32[]{:S(2)}, u32[]{:S(2)}) collective-permute-start(bf16[512,384]{1,0:T(8,128)(2,1)} %get-tuple-element.76.refs_1_), channel_id=1, source_target_pairs={{0,8},{8,0},{16,24},{24,16},{1,9},{9,1},{17,25},{25,17},{2,10},{10... | collective-permute-start | bytes 1179656 | tf_op jit(solution)/shard_map/ppermute | solution.py:843
  18.1 17.8 %collective-permute-start = (bf16[512,384]{1,0:T(8,128)(2,1)}, bf16[512,384]{1,0:T(8,128)(2,1)}, u32[]{:S(2)}, u32[]{:S(2)}) collective-permute-start(bf16[512,384]{1,0:T(8,128)(2,1)} %get-tuple-element.75.refs_0_), channel_id=1, source_target_pairs={{0,8},{8,0},{16,24},{24,16},{1,9},{9,1},{17,25},{25,17},{2,10},{10... | collective-permute-start | bytes 1179656 | tf_op jit(solution)/shard_map/ppermute | solution.py:843
  18.7 42.0 %collective-permute-start.5 = (bf16[512,384]{1,0:T(8,128)(2,1)}, bf16[512,384]{1,0:T(8,128)(2,1)}, u32[]{:S(2)}, u32[]{:S(2)}) collective-permute-start(bf16[512,384]{1,0:T(8,128)(2,1)} %get-tuple-element.75.refs_0_), channel_id=1, source_target_pairs={{0,16},{8,24},{16,0},{24,8},{1,17},{9,25},{17,1},{25,9},{2,18},{10... | collective-permute-start | bytes 1179656 | tf_op jit(solution)/shard_map/ppermute | solution.py:843
  36.0 11.9 %collective-permute-start.1 = (bf16[512,384]{1,0:T(8,128)(2,1)}, bf16[512,384]{1,0:T(8,128)(2,1)}, u32[]{:S(2)}, u32[]{:S(2)}) collective-permute-start(bf16[512,384]{1,0:T(8,128)(2,1)} %collective-permute-done.refs_2_), channel_id=1, source_target_pairs={{0,16},{8,24},{16,0},{24,8},{1,17},{9,25},{17,1},{25,9},{2,18},{10... | collective-permute-start | bytes 1179656 | tf_op jit(solution)/shard_map/ppermute | solution.py:843
  36.3 11.5 %copy-start.25 = (bf16[512,384]{1,0:T(8,128)(2,1)}, bf16[512,384]{1,0:T(8,128)(2,1)S(1)}, u32[]{:S(2)}) copy-start(bf16[512,384]{1,0:T(8,128)(2,1)S(1)} %collective-permute-done.2.refs_7_) | copy-start | bytes 1179652
  36.3 11.5 %collective-permute-start.3 = (bf16[512,384]{1,0:T(8,128)(2,1)S(1)}, bf16[512,384]{1,0:T(8,128)(2,1)}, u32[]{:S(2)}, u32[]{:S(2)}) collective-permute-start(bf16[512,384]{1,0:T(8,128)(2,1)S(1)} %collective-permute-done.2.refs_7_), channel_id=1, source_target_pairs={{0,8},{8,0},{16,24},{24,16},{1,9},{9,1},{17,25},{25,17},{2,10},{10... | collective-permute-start | bytes 1179656 | tf_op jit(solution)/shard_map/ppermute | solution.py:843
  47.8 92.8 %copy-start.2 = (bf16[512,1536]{1,0:T(8,128)(2,1)}, bf16[512,1536]{1,0:T(8,128)(2,1)S(1)}, u32[]{:S(2)}) copy-start(bf16[512,1536]{1,0:T(8,128)(2,1)S(1)} %get-tuple-element.77.refs_0_) | copy-start | bytes 4718596
  47.8 96.1 %copy-start.1 = (bf16[512,1536]{1,0:T(8,128)(2,1)}, bf16[512,1536]{1,0:T(8,128)(2,1)S(1)}, u32[]{:S(2)}) copy-start(bf16[512,1536]{1,0:T(8,128)(2,1)S(1)} %get-tuple-element.78.refs_5_.refs_0_) | copy-start | bytes 4718596
  76.7 28.6 %all-to-all-start = ((bf16[32,64,128]{2,1,0:T(8,128)(2,1)}), bf16[32,64,128]{2,1,0:T(8,128)(2,1)}, u32[]{:S(2)}, u32[]{:S(2)}) async-start(bf16[32,64,128]{2,1,0:T(8,128)(2,1)} %bitcast.38), calls=%async_computation | async-start | bytes 1048576 | tf_op jit(solution)/shard_map/all_to_all | solution.py:938
  80.3 172.0 %all-gather.6.cloned.1.call-start = ((), (), s32[]{:S(2)}) async-start(), calls=%async_computation.9 | async-start | bytes 4718592 | tf_op jit(solution)/shard_map/all_gather | solution.py:921
  111.7 14.1 %collective-permute-start.6 = (bf16[128,2048]{1,0:T(8,128)(2,1)}, bf16[128,2048]{1,0:T(8,128)(2,1)}, u32[]{:S(2)}, u32[]{:S(2)}) collective-permute-start(bf16[128,2048]{1,0:T(8,128)(2,1)} %get-tuple-element.84), channel_id=1, source_target_pairs={{0,8},{8,0},{16,24},{24,16},{1,9},{9,1},{17,25},{25,17},{2,10},{10... | collective-permute-start | bytes 1572872 | tf_op jit(solution)/shard_map/ppermute | solution.py:843
  111.7 14.1 %collective-permute-start.7 = (bf16[128,2048]{1,0:T(8,128)(2,1)}, bf16[128,2048]{1,0:T(8,128)(2,1)}, u32[]{:S(2)}, u32[]{:S(2)}) collective-permute-start(bf16[128,2048]{1,0:T(8,128)(2,1)} %get-tuple-element.85), channel_id=1, source_target_pairs={{0,16},{8,24},{16,0},{24,8},{1,17},{9,25},{17,1},{25,9},{2,18},{10... | collective-permute-start | bytes 1572872 | tf_op jit(solution)/shard_map/ppermute | solution.py:843
  112.8 23.2 %collective-permute-start.8 = (bf16[128,2048]{1,0:T(8,128)(2,1)}, bf16[128,2048]{1,0:T(8,128)(2,1)}, u32[]{:S(2)}, u32[]{:S(2)}) collective-permute-start(bf16[128,2048]{1,0:T(8,128)(2,1)} %get-tuple-element.86), channel_id=1, source_target_pairs={{0,24},{8,16},{16,8},{24,0},{1,25},{9,17},{17,9},{25,1},{2,26},{10... | collective-permute-start | bytes 1572872 | tf_op jit(solution)/shard_map/ppermute | solution.py:843
  140.5 194.7 %reduce-scatter.5.cloned.1.call-start = ((), (), s32[]{:S(2)}) async-start(), calls=%async_computation.11 | async-start | bytes 4718592 | tf_op jit(solution)/shard_map/reduce_scatter | solution.py:925
  140.6 38.5 %collective-permute-start.9 = (bf16[512,1536]{1,0:T(8,128)(2,1)S(1)}, bf16[512,1536]{1,0:T(8,128)(2,1)S(1)}, u32[]{:S(2)}, u32[]{:S(2)}) collective-permute-start(bf16[512,1536]{1,0:T(8,128)(2,1)S(1)} %get-tuple-element.77.refs_0_), channel_id=1, source_target_pairs={{0,8},{8,0},{16,24},{24,16},{1,9},{9,1},{17,25},{25,17},{2,10},{10... | collective-permute-start | bytes 4718600 | tf_op jit(solution)/shard_map/ppermute | solution.py:843
  143.9 37.3 %collective-permute-start.15 = (bf16[512,1536]{1,0:T(8,128)(2,1)S(1)}, bf16[512,1536]{1,0:T(8,128)(2,1)S(1)}, u32[]{:S(2)}, u32[]{:S(2)}) collective-permute-start(bf16[512,1536]{1,0:T(8,128)(2,1)S(1)} %get-tuple-element.78.refs_5_.refs_0_), channel_id=1, source_target_pairs={{0,16},{8,24},{16,0},{24,8},{1,17},{9,25},{17,1},{25,9},{2,18},{10... | collective-permute-start | bytes 4718600 | tf_op jit(solution)/shard_map/ppermute | solution.py:843
  143.9 54.1 %collective-permute-start.11 = (bf16[256,1536]{1,0:T(8,128)(2,1)}, bf16[256,1536]{1,0:T(8,128)(2,1)S(1)}, u32[]{:S(2)}, u32[]{:S(2)}) collective-permute-start(bf16[256,1536]{1,0:T(8,128)(2,1)} %get-tuple-element.91), channel_id=1, source_target_pairs={{0,16},{8,24},{16,0},{24,8},{1,17},{9,25},{17,1},{25,9},{2,18},{10... | collective-permute-start | bytes 2359304 | tf_op jit(solution)/shard_map/ppermute | solution.py:843
  179.0 3.5 copy-start.18
  179.0 72.3 %collective-permute-start.10 = (bf16[512,1536]{1,0:T(8,128)(2,1)S(1)}, bf16[512,1536]{1,0:T(8,128)(2,1)S(1)}, u32[]{:S(2)}, u32[]{:S(2)}) collective-permute-start(bf16[512,1536]{1,0:T(8,128)(2,1)S(1)} %collective-permute-done.9.refs_1_), channel_id=1, source_target_pairs={{0,16},{8,24},{16,0},{24,8},{1,17},{9,25},{17,1},{25,9},{2,18},{10... | collective-permute-start | bytes 4718600 | tf_op jit(solution)/shard_map/ppermute | solution.py:843
  182.4 69.8 %collective-permute-start.16 = (bf16[512,1536]{1,0:T(8,128)(2,1)S(1)}, bf16[512,1536]{1,0:T(8,128)(2,1)S(1)}, u32[]{:S(2)}, u32[]{:S(2)}) collective-permute-start(bf16[512,1536]{1,0:T(8,128)(2,1)S(1)} %collective-permute-done.15.refs_9_.refs_4_), channel_id=1, source_target_pairs={{0,8},{8,0},{16,24},{24,16},{1,9},{9,1},{17,25},{25,17},{2,10},{10... | collective-permute-start | bytes 4718600 | tf_op jit(solution)/shard_map/ppermute | solution.py:843
  182.6 54.0 %collective-permute-start.13 = (bf16[256,1536]{1,0:T(8,128)(2,1)}, bf16[256,1536]{1,0:T(8,128)(2,1)S(1)}, u32[]{:S(2)}, u32[]{:S(2)}) collective-permute-start(bf16[256,1536]{1,0:T(8,128)(2,1)} %get-tuple-element.93), channel_id=1, source_target_pairs={{0,8},{8,0},{16,24},{24,16},{1,9},{9,1},{17,25},{25,17},{2,10},{10... | collective-permute-start | bytes 2359304 | tf_op jit(solution)/shard_map/ppermute | solution.py:843
  184.4 63.5 %collective-permute-start.12 = (bf16[256,1536]{1,0:T(8,128)(2,1)}, bf16[256,1536]{1,0:T(8,128)(2,1)S(1)}, u32[]{:S(2)}, u32[]{:S(2)}) collective-permute-start(bf16[256,1536]{1,0:T(8,128)(2,1)} %get-tuple-element.92), channel_id=1, source_target_pairs={{0,16},{8,24},{16,0},{24,8},{1,17},{9,25},{17,1},{25,9},{2,18},{10... | collective-permute-start | bytes 2359304 | tf_op jit(solution)/shard_map/ppermute | solution.py:843
  198.0 53.3 %copy-start.22 = (bf16[256,1536]{1,0:T(8,128)(2,1)}, bf16[256,1536]{1,0:T(8,128)(2,1)S(1)}, u32[]{:S(2)}) copy-start(bf16[256,1536]{1,0:T(8,128)(2,1)S(1)} %collective-permute-done.11.refs_3_) | copy-start | bytes 2359300
  198.0 53.3 %collective-permute-start.14 = (bf16[256,1536]{1,0:T(8,128)(2,1)}, bf16[256,1536]{1,0:T(8,128)(2,1)S(1)}, u32[]{:S(2)}, u32[]{:S(2)}) collective-permute-start(bf16[256,1536]{1,0:T(8,128)(2,1)} %get-tuple-element.94), channel_id=1, source_target_pairs={{0,8},{8,0},{16,24},{24,16},{1,9},{9,1},{17,25},{25,17},{2,10},{10... | collective-permute-start | bytes 2359304 | tf_op jit(solution)/shard_map/ppermute | solution.py:843
  236.5 14.8 %copy-start.21 = (bf16[256,1536]{1,0:T(8,128)(2,1)}, bf16[256,1536]{1,0:T(8,128)(2,1)S(1)}, u32[]{:S(2)}) copy-start(bf16[256,1536]{1,0:T(8,128)(2,1)S(1)} %collective-permute-done.13.refs_6_.refs_1_) | copy-start | bytes 2359300
  247.9 3.4 copy-start.24
  286.3 294.3 %reduce-scatter.7.cloned.1.call-start = ((), (), s32[]{:S(2)}) async-start(), calls=%async_computation.12 | async-start | bytes 2621440 | tf_op jit(solution)/shard_map/reduce_scatter | solution.py:931
  297.2 4.6 collective-permute-start.17
  344.6 26.3 %collective-permute-start.35 = (bf16[1024,512]{1,0:T(8,128)(2,1)}, bf16[1024,512]{1,0:T(8,128)(2,1)}, u32[]{:S(2)}, u32[]{:S(2)}) collective-permute-start(bf16[1024,512]{1,0:T(8,128)(2,1)} %get-tuple-element.133), channel_id=1, source_target_pairs={{0,16},{8,24},{16,0},{24,8},{1,17},{9,25},{17,1},{25,9},{2,18},{10... | collective-permute-start | bytes 3145736 | tf_op jit(solution)/shard_map/ppermute | solution.py:843
  346.1 28.5 %collective-permute-start.33 = (bf16[1024,512]{1,0:T(8,128)(2,1)}, bf16[1024,512]{1,0:T(8,128)(2,1)S(1)}, u32[]{:S(2)}, u32[]{:S(2)}) collective-permute-start(bf16[1024,512]{1,0:T(8,128)(2,1)} %get-tuple-element.130), channel_id=1, source_target_pairs={{0,8},{8,0},{16,24},{24,16},{1,9},{9,1},{17,25},{25,17},{2,10},{10... | collective-permute-start | bytes 3145736 | tf_op jit(solution)/shard_map/ppermute | solution.py:843
  356.9 36.4 %collective-permute-start.31 = (bf16[1024,512]{1,0:T(8,128)(2,1)}, bf16[1024,512]{1,0:T(8,128)(2,1)S(1)}, u32[]{:S(2)}, u32[]{:S(2)}) collective-permute-start(bf16[1024,512]{1,0:T(8,128)(2,1)} %get-tuple-element.127), channel_id=1, source_target_pairs={{0,16},{8,24},{16,0},{24,8},{1,17},{9,25},{17,1},{25,9},{2,18},{10... | collective-permute-start | bytes 3145736 | tf_op jit(solution)/shard_map/ppermute | solution.py:843
  357.4 44.4 %collective-permute-start.29 = (bf16[1024,512]{1,0:T(8,128)(2,1)}, bf16[1024,512]{1,0:T(8,128)(2,1)S(1)}, u32[]{:S(2)}, u32[]{:S(2)}) collective-permute-start(bf16[1024,512]{1,0:T(8,128)(2,1)} %get-tuple-element.124), channel_id=1, source_target_pairs={{0,8},{8,0},{16,24},{24,16},{1,9},{9,1},{17,25},{25,17},{2,10},{10... | collective-permute-start | bytes 3145736 | tf_op jit(solution)/shard_map/ppermute | solution.py:843
  358.0 35.3 %copy-start.9 = (bf16[512,512]{1,0:T(8,128)(2,1)S(1)}, bf16[512,512]{1,0:T(8,128)(2,1)}, u32[]{:S(2)}) copy-start(bf16[512,512]{1,0:T(8,128)(2,1)} %get-tuple-element.128) | copy-start | bytes 1572868
  373.1 33.1 %collective-permute-start.36 = (bf16[512,512]{1,0:T(8,128)(2,1)}, bf16[512,512]{1,0:T(8,128)(2,1)}, u32[]{:S(2)}, u32[]{:S(2)}) collective-permute-start(bf16[512,512]{1,0:T(8,128)(2,1)} %add_convert_fusion.4), channel_id=1, source_target_pairs={{0,8},{8,0},{16,24},{24,16},{1,9},{9,1},{17,25},{25,17},{2,10},{10... | collective-permute-start | bytes 1572872 | tf_op jit(solution)/shard_map/ppermute | solution.py:843
  376.5 63.6 %collective-permute-start.34 = (bf16[512,512]{1,0:T(8,128)(2,1)}, bf16[512,512]{1,0:T(8,128)(2,1)}, u32[]{:S(2)}, u32[]{:S(2)}) collective-permute-start(bf16[512,512]{1,0:T(8,128)(2,1)} %add_convert_fusion.6), channel_id=1, source_target_pairs={{0,16},{8,24},{16,0},{24,8},{1,17},{9,25},{17,1},{25,9},{2,18},{10... | collective-permute-start | bytes 1572872 | tf_op jit(solution)/shard_map/ppermute | solution.py:843
  393.3 5.6 copy-start.4
  398.9 29.7 %copy-start.3 = (bf16[512,2048]{1,0:T(8,128)(2,1)S(1)}, bf16[512,2048]{1,0:T(8,128)(2,1)}, u32[]{:S(2)}) copy-start(bf16[512,2048]{1,0:T(8,128)(2,1)} %weight_ref.1) | copy-start | bytes 6291460
  398.9 29.7 %copy-start.8 = (bf16[128,2048]{1,0:T(8,128)(2,1)S(1)}, bf16[128,2048]{1,0:T(8,128)(2,1)}, u32[]{:S(2)}) copy-start(bf16[128,2048]{1,0:T(8,128)(2,1)} %get-tuple-element.105.refs_0_) | copy-start | bytes 1572868
  398.9 18.4 %collective-permute-start.20 = (bf16[128,2048]{1,0:T(8,128)(2,1)}, bf16[128,2048]{1,0:T(8,128)(2,1)S(1)}, u32[]{:S(2)}, u32[]{:S(2)}) collective-permute-start(bf16[128,2048]{1,0:T(8,128)(2,1)} %get-tuple-element.105.refs_0_), channel_id=1, source_target_pairs={{0,24},{8,16},{16,8},{24,0},{1,25},{9,17},{17,9},{25,1},{2,26},{10... | collective-permute-start | bytes 1572872 | tf_op jit(solution)/shard_map/ppermute | solution.py:843
  401.3 25.7 %collective-permute-start.19 = (bf16[128,2048]{1,0:T(8,128)(2,1)}, bf16[128,2048]{1,0:T(8,128)(2,1)S(1)}, u32[]{:S(2)}, u32[]{:S(2)}) collective-permute-start(bf16[128,2048]{1,0:T(8,128)(2,1)} %get-tuple-element.105.refs_0_), channel_id=1, source_target_pairs={{0,16},{8,24},{16,0},{24,8},{1,17},{9,25},{17,1},{25,9},{2,18},{10... | collective-permute-start | bytes 1572872 | tf_op jit(solution)/shard_map/ppermute | solution.py:843
  401.9 26.7 %collective-permute-start.18 = (bf16[128,2048]{1,0:T(8,128)(2,1)}, bf16[128,2048]{1,0:T(8,128)(2,1)S(1)}, u32[]{:S(2)}, u32[]{:S(2)}) collective-permute-start(bf16[128,2048]{1,0:T(8,128)(2,1)} %get-tuple-element.105.refs_0_), channel_id=1, source_target_pairs={{0,8},{8,0},{16,24},{24,16},{1,9},{9,1},{17,25},{25,17},{2,10},{10... | collective-permute-start | bytes 1572872 | tf_op jit(solution)/shard_map/ppermute | solution.py:843
  406.1 35.5 %collective-permute-start.32 = (bf16[512,512]{1,0:T(8,128)(2,1)}, bf16[512,512]{1,0:T(8,128)(2,1)}, u32[]{:S(2)}, u32[]{:S(2)}) collective-permute-start(bf16[512,512]{1,0:T(8,128)(2,1)} %add_convert_fusion.8), channel_id=1, source_target_pairs={{0,8},{8,0},{16,24},{24,16},{1,9},{9,1},{17,25},{25,17},{2,10},{10... | collective-permute-start | bytes 1572872 | tf_op jit(solution)/shard_map/ppermute | solution.py:843
  417.3 12.5 %copy-start.10 = (bf16[128,2048]{1,0:T(8,128)(2,1)}, bf16[128,2048]{1,0:T(8,128)(2,1)S(1)}, u32[]{:S(2)}) copy-start(bf16[128,2048]{1,0:T(8,128)(2,1)S(1)} %collective-permute-done.20.refs_3_) | copy-start | bytes 1572868
  417.3 25.7 %collective-permute-start.30 = (bf16[512,512]{1,0:T(8,128)(2,1)}, bf16[512,512]{1,0:T(8,128)(2,1)}, u32[]{:S(2)}, u32[]{:S(2)}) collective-permute-start(bf16[512,512]{1,0:T(8,128)(2,1)} %add_convert_fusion.10), channel_id=1, source_target_pairs={{0,16},{8,24},{16,0},{24,8},{1,17},{9,25},{17,1},{25,9},{2,18},{10... | collective-permute-start | bytes 1572872 | tf_op jit(solution)/shard_map/ppermute | solution.py:843
  431.0 18.8 %all-to-all-start.1 = ((bf16[32,64,128]{2,1,0:T(8,128)(2,1)}), bf16[32,64,128]{2,1,0:T(8,128)(2,1)S(1)}, u32[]{:S(2)}, u32[]{:S(2)}) async-start(bf16[32,64,128]{2,1,0:T(8,128)(2,1)} %bitcast.14), calls=%async_computation.3 | async-start | bytes 1048576 | tf_op jit(solution)/shard_map/all_to_all | solution.py:938
  433.6 150.1 %reduce-scatter.11.cloned.1.call-start = ((), (), s32[]{:S(2)}) async-start(), calls=%async_computation.14 | async-start | bytes 2359296 | tf_op jit(solution)/shard_map/reduce_scatter | solution.py:925
  440.1 2.9 copy-start.14
  450.6 116.0 %all-to-all-start.3 = ((bf16[8,64,2048]{2,1,0:T(8,128)(2,1)}), bf16[8,64,2048]{2,1,0:T(8,128)(2,1)S(1)}, u32[]{:S(2)}, u32[]{:S(2)}) async-start(bf16[8,64,2048]{2,1,0:T(8,128)(2,1)} %bitcast.32), calls=%async_computation.6 | async-start | bytes 4194304 | tf_op jit(solution)/shard_map/all_to_all | solution.py:938
  454.3 167.7 %reduce-scatter.9.cloned.1.call-start = ((), (), s32[]{:S(2)}) async-start(), calls=%async_computation.13 | async-start | bytes 2621440 | tf_op jit(solution)/shard_map/reduce_scatter | solution.py:931
  476.2 53.3 %collective-permute-start.21 = (bf16[512,2048]{1,0:T(8,128)(2,1)}, bf16[512,2048]{1,0:T(8,128)(2,1)}, u32[]{:S(2)}, u32[]{:S(2)}) collective-permute-start(bf16[512,2048]{1,0:T(8,128)(2,1)} %get-tuple-element.111), channel_id=1, source_target_pairs={{0,1},{1,0},{2,3},{3,2},{4,5},{5,4},{6,7},{7,6},{8,9},{9,8},{10,11... | collective-permute-start | bytes 6291464 | tf_op jit(solution)/shard_map/ppermute | solution.py:929
  485.8 25.7 %collective-permute-start.24 = (bf16[1024,512]{1,0:T(8,128)(2,1)}, bf16[1024,512]{1,0:T(8,128)(2,1)S(1)}, u32[]{:S(2)}, u32[]{:S(2)}) collective-permute-start(bf16[1024,512]{1,0:T(8,128)(2,1)} %get-tuple-element.117), channel_id=1, source_target_pairs={{0,16},{8,24},{16,0},{24,8},{1,17},{9,25},{17,1},{25,9},{2,18},{10... | collective-permute-start | bytes 3145736 | tf_op jit(solution)/shard_map/ppermute | solution.py:843
  486.6 27.7 %collective-permute-start.22 = (bf16[1024,512]{1,0:T(8,128)(2,1)}, bf16[1024,512]{1,0:T(8,128)(2,1)S(1)}, u32[]{:S(2)}, u32[]{:S(2)}) collective-permute-start(bf16[1024,512]{1,0:T(8,128)(2,1)} %get-tuple-element.114), channel_id=1, source_target_pairs={{0,8},{8,0},{16,24},{24,16},{1,9},{9,1},{17,25},{25,17},{2,10},{10... | collective-permute-start | bytes 3145736 | tf_op jit(solution)/shard_map/ppermute | solution.py:843
  513.8 20.8 %collective-permute-start.25 = (bf16[512,512]{1,0:T(8,128)(2,1)}, bf16[512,512]{1,0:T(8,128)(2,1)}, u32[]{:S(2)}, u32[]{:S(2)}) collective-permute-start(bf16[512,512]{1,0:T(8,128)(2,1)} %add_convert_fusion.12), channel_id=1, source_target_pairs={{0,8},{8,0},{16,24},{24,16},{1,9},{9,1},{17,25},{25,17},{2,10},{10... | collective-permute-start | bytes 1572872 | tf_op jit(solution)/shard_map/ppermute | solution.py:843
  516.2 29.3 %collective-permute-start.23 = (bf16[512,512]{1,0:T(8,128)(2,1)}, bf16[512,512]{1,0:T(8,128)(2,1)}, u32[]{:S(2)}, u32[]{:S(2)}) collective-permute-start(bf16[512,512]{1,0:T(8,128)(2,1)} %add_convert_fusion.14), channel_id=1, source_target_pairs={{0,16},{8,24},{16,0},{24,8},{1,17},{9,25},{17,1},{25,9},{2,18},{10... | collective-permute-start | bytes 1572872 | tf_op jit(solution)/shard_map/ppermute | solution.py:843
  526.6 36.6 %collective-permute-start.28 = (bf16[512,768]{1,0:T(8,128)(2,1)}, bf16[512,768]{1,0:T(8,128)(2,1)}, u32[]{:S(2)}, u32[]{:S(2)}) collective-permute-start(bf16[512,768]{1,0:T(8,128)(2,1)} %get-tuple-element.122), channel_id=1, source_target_pairs={{0,16},{8,24},{16,0},{24,8},{1,17},{9,25},{17,1},{25,9},{2,18},{10... | collective-permute-start | bytes 2359304 | tf_op jit(solution)/shard_map/ppermute | solution.py:843
  528.0 35.2 %collective-permute-start.27 = (bf16[512,768]{1,0:T(8,128)(2,1)}, bf16[512,768]{1,0:T(8,128)(2,1)}, u32[]{:S(2)}, u32[]{:S(2)}) collective-permute-start(bf16[512,768]{1,0:T(8,128)(2,1)} %get-tuple-element.121), channel_id=1, source_target_pairs={{0,24},{8,16},{16,8},{24,0},{1,25},{9,17},{17,9},{25,1},{2,26},{10... | collective-permute-start | bytes 2359304 | tf_op jit(solution)/shard_map/ppermute | solution.py:843
  529.5 33.7 %collective-permute-start.26 = (bf16[512,768]{1,0:T(8,128)(2,1)}, bf16[512,768]{1,0:T(8,128)(2,1)}, u32[]{:S(2)}, u32[]{:S(2)}) collective-permute-start(bf16[512,768]{1,0:T(8,128)(2,1)} %get-tuple-element.120), channel_id=1, source_target_pairs={{0,8},{8,0},{16,24},{24,16},{1,9},{9,1},{17,25},{25,17},{2,10},{10... | collective-permute-start | bytes 2359304 | tf_op jit(solution)/shard_map/ppermute | solution.py:843
  534.6 10.9 %copy-start.16 = (bf16[512,512]{1,0:T(8,128)(2,1)S(1)}, bf16[512,512]{1,0:T(8,128)(2,1)}, u32[]{:S(2)}) copy-start(bf16[512,512]{1,0:T(8,128)(2,1)} %get-tuple-element.113) | copy-start | bytes 1572868
  534.6 28.7 %copy-start.7 = (bf16[512,768]{1,0:T(8,128)(2,1)S(1)}, bf16[512,768]{1,0:T(8,128)(2,1)}, u32[]{:S(2)}) copy-start(bf16[512,768]{1,0:T(8,128)(2,1)} %get-tuple-element.119) | copy-start | bytes 2359300
  566.7 7.6 %copy-start = (bf16[8,64,2048]{2,1,0:T(8,128)(2,1)}, bf16[8,64,2048]{2,1,0:T(8,128)(2,1)S(1)}, u32[]{:S(2)}) copy-start(bf16[8,64,2048]{2,1,0:T(8,128)(2,1)S(1)} %all-to-all-done.3.refs_0_) | copy-start | bytes 6291460
  566.7 51.1 %all-to-all-start.2 = ((bf16[8,64,1792]{2,1,0:T(8,128)(2,1)}), bf16[8,64,1792]{2,1,0:T(8,128)(2,1)}, u32[]{:S(2)}, u32[]{:S(2)}) async-start(bf16[8,64,1792]{2,1,0:T(8,128)(2,1)} %bitcast.33), calls=%async_computation.5 | async-start | bytes 3670016 | tf_op jit(solution)/shard_map/all_to_all | solution.py:938
  (10 other events, 16.0 us)
Sparse Core Ops, SparseCore 0:
  11.1 49.5 all-gather.3
  76.8 53.6 all-gather.7
  140.6 48.5 all-gather.5
  286.4 48.7 reduce-scatter.4
  337.3 42.0 reduce-scatter.6
  440.2 52.3 reduce-scatter.10
  534.7 45.9 reduce-scatter.8
